TPU v7x, 512 devices: a whole 4x4x16 slice. The times are simulated.
512 devices in a mesh: seq: 64 (over x_hi, z, core), tensor: 8 (over x_lo, y).
Axes of the slice: x: 4 (x_hi: 2, x_lo: 2; x = x_hi * 2 + x_lo), y: 4, z: 16, core: 2. Of those that a mesh axis runs over, the one named last changes fastest.
Arguments:
- projected: bfloat16 [3, 16384, 4096], P(None, 'seq', 'tensor'), may hold values from -6 to 6
- feat_weight: float32 [3, 7, 4096], P(None, None, 'tensor'), may hold values from -2 to 2
- long_filter: float32 [4096, 16384], P(('tensor', 'seq')), may hold values from -1.2 to 1.2
- skip_gain: float32 [4096], P(('tensor', 'seq')), may hold values from 0.5 to 1.5
- out_values: bfloat16 [4096, 2048], P('tensor'), may hold values from -0.125 to 0.125
- out_scales: float32 [32, 16], P('tensor'), may hold values from 0.125 to 1
Outputs:
- mixed: bfloat16 [16384, 2048], P('seq', 'tensor')
All inputs are finite; a program needn't handle non-finite values.
Results may differ from a plain program's by a relative error of at most 0.023.
Values may be sent and summed in bfloat16 or wider, within the bound.
No kernel may reach another device: no remote copies, remote signals or barrier semaphores. Data moves between devices by JAX's collectives and lax.ppermute only.
A program may use at most 64 MiB of HBM per device.

v0:
```python
import math

import jax
import jax.numpy as jnp
from jax import lax
from jax.sharding import PartitionSpec as P

KS = 7
BLK = 128


TRIPLE = lax.Precision.HIGH


def passed_along(x, axis, by):
    size = lax.axis_size(axis)
    pairs = [(i, i + by) for i in range(size) if 0 <= i + by < size]
    return lax.ppermute(x, axis, pairs)


def split_length(whole):
    for candidate in range(2, whole + 1, 2):
        if whole % candidate == 0 and candidate * candidate >= whole:
            return (candidate, whole // candidate)
    return (whole, 1)


def angle_pair(row_count, col_count, period):
    row_ids = lax.broadcasted_iota(jnp.int32, (row_count, col_count), 0)
    col_ids = lax.broadcasted_iota(jnp.int32, (row_count, col_count), 1)
    angles = (row_ids * col_ids % period).astype(jnp.float32) * (2.0 * math.pi / period)
    return (jnp.cos(angles), jnp.sin(angles))


def make_tables(length):
    whole = 2 * length
    size_a, size_b = split_length(whole)
    return (
        angle_pair(size_a, size_a, size_a),
        angle_pair(size_b, size_b, size_b),
        angle_pair(size_a, size_b, whole),
        size_a,
        size_b,
    )


def right_mul(signal, matrix):
    return jnp.einsum("ckn,nm->ckm", signal, matrix, precision=TRIPLE)


def forward(signal, tables):
    (cos_a, sin_a), (cos_b, sin_b), (cos_t, sin_t), size_a, size_b = tables
    half_a = size_a // 2
    blocks = signal.reshape(signal.shape[0], half_a, size_b)
    real_a = jnp.einsum("kn,cnb->ckb", cos_a[:, :half_a], blocks, precision=TRIPLE)
    imag_a = -jnp.einsum("kn,cnb->ckb", sin_a[:, :half_a], blocks, precision=TRIPLE)
    real_t = real_a * cos_t + imag_a * sin_t
    imag_t = imag_a * cos_t - real_a * sin_t
    real_f = right_mul(real_t, cos_b) + right_mul(imag_t, sin_b)
    imag_f = right_mul(imag_t, cos_b) - right_mul(real_t, sin_b)
    return (real_f, imag_f)


def inverse(real_f, imag_f, tables):
    (cos_a, sin_a), (cos_b, sin_b), (cos_t, sin_t), size_a, size_b = tables
    half_a = size_a // 2
    real_z = right_mul(real_f, cos_b) - right_mul(imag_f, sin_b)
    imag_z = right_mul(imag_f, cos_b) + right_mul(real_f, sin_b)
    real_w = real_z * cos_t - imag_z * sin_t
    imag_w = imag_z * cos_t + real_z * sin_t
    out_half = jnp.einsum("nk,ckb->cnb", cos_a[:half_a, :], real_w, precision=TRIPLE) - jnp.einsum(
        "nk,ckb->cnb", sin_a[:half_a, :], imag_w, precision=TRIPLE
    )
    return out_half.reshape(out_half.shape[0], half_a * size_b) * (1.0 / (size_a * size_b))


def long_mix(gated_kv, spectrum, own_gain, tables):
    kv_values = gated_kv.astype(jnp.float32)
    real_u, imag_u = forward(kv_values, tables)
    real_h, imag_h = spectrum
    real_p = real_u * real_h - imag_u * imag_h
    imag_p = real_u * imag_h + imag_u * real_h
    convolved = inverse(real_p, imag_p, tables)
    return (convolved + own_gain[:, None] * kv_values).astype(jnp.bfloat16)


def featurize(extended, weights, length):
    tap_count = weights.shape[1]
    running = jnp.zeros(extended.shape[:2] + (length,), jnp.float32)
    for lag_idx in range(tap_count):
        offset = tap_count - 1 - lag_idx
        running = running + weights[:, lag_idx, :, None] * extended[
            :, :, offset : offset + length
        ].astype(jnp.float32)
    return running.astype(jnp.bfloat16)


def multiply_round(left_arr, right_arr):
    return (left_arr.astype(jnp.float32) * right_arr.astype(jnp.float32)).astype(jnp.bfloat16)


def local(projected, feat_weight, long_filter, skip_gain, out_values, out_scales):
    groups = lax.axis_size("seq")
    tok_rows = projected.shape[1]
    local_ch = projected.shape[2]
    length = tok_rows * groups
    tables = make_tables(length)
    spectrum = forward(long_filter, tables)
    columns = jnp.transpose(projected, (0, 2, 1))
    rim_width = KS - 1
    prior_rows = passed_along(columns[:, :, tok_rows - rim_width :], "seq", 1)
    featured = featurize(jnp.concatenate([prior_rows, columns], axis=2), feat_weight, tok_rows)
    regrouped = lax.all_to_all(featured, "seq", split_axis=1, concat_axis=2, tiled=True)
    gated_kv = multiply_round(regrouped[1], regrouped[2])
    filtered = long_mix(gated_kv, spectrum, skip_gain, tables)
    gated = multiply_round(regrouped[0], filtered)
    gated_home = lax.all_to_all(gated, "seq", split_axis=1, concat_axis=0, tiled=True)
    block_count = local_ch // BLK
    out_width = out_values.shape[1]
    stacked = gated_home.reshape(block_count, BLK, tok_rows)
    weight_blocks = out_values.reshape(block_count, BLK, out_width)
    scale_cols = jnp.repeat(out_scales, BLK, axis=1)
    products = jnp.einsum(
        "bkn,bkt->bnt", weight_blocks, stacked, preferred_element_type=jnp.float32
    )
    summed = lax.psum_scatter(
        jnp.sum(products * scale_cols[:, :, None], axis=0).astype(jnp.bfloat16),
        "tensor",
        scatter_dimension=0,
        tiled=True,
    )
    return jnp.transpose(summed, (1, 0))


def solution(mesh):
    return jax.shard_map(
        local,
        mesh=mesh,
        in_specs=(
            P(None, "seq", "tensor"),
            P(None, None, "tensor"),
            P(("tensor", "seq"), None),
            P(("tensor", "seq")),
            P("tensor", None),
            P("tensor", None),
        ),
        out_specs=P("seq", "tensor"),
        check_vma=False,
    )
```

profile of v0, /device:TPU:32, one launch (start us, length us, event | category | flops | bytes accessed | tf_op | source)
XLA Modules:
  0.0 207.8 jit_solution(3244405908795059721)
XLA Ops:
  6.5 1.8 copy.39
  8.3 1.1 slice.93
  9.5 1.9 collective-permute-start
  11.4 0.1 copy.76
  11.6 0.9 copy.80
  12.5 0.9 copy.79
  13.3 0.9 copy.78
  14.2 0.9 copy.77
  15.1 0.9 copy.82
  16.0 0.9 copy.81
  16.9 3.4 %collective-permute-done = bf16[3,512,6]{2,0,1:T(4,128)(2,1)} collective-permute-done((bf16[3,512,6]{2,0,1:T(4,128)(2,1)}, bf16[3,512,6]{2,0,1:T(4,128)(2,1)}, u32[]{:S(2)}, u32[]{:S(2)}) %collective-permute-start) | collective-permute-done | bytes 18464 | tf_op jit(solution)/shard_map/ppermute | solution.py:18
  20.3 12.6 %add_convert_fusion = bf16[3,512,256]{2,0,1:T(4,128)(2,1)} fusion(bf16[3,512,256]{2,0,1:T(4,128)(2,1)S(1)} %bitcast.105, bf16[3,512,6]{2,0,1:T(4,128)(2,1)} %collective-permute-done, f32[3,512]{0,1:T(8,128)} %bitcast.115, f32[3,512]{0,1:T(8,128)} %bitcast.116, f32[3,512]{0,1:T(8,128)} %bitcast.111, f32[3,512]{0,1:T(8,128)} %bitcast.112, ...), kind=kLoop, calls=%fused_computation.6 | loop fusion | flops 15335424 | bytes 1634304 | tf_op jit(solution)/shard_map/convert_element_type | solution.py:95
  32.9 19.9 %all-to-all-start = ((bf16[3,512,256]{2,0,1:T(4,128)(2,1)}), bf16[3,512,256]{2,0,1:T(4,128)(2,1)}, u32[]{:S(2)}, u32[]{:S(2)}) async-start(bf16[3,512,256]{2,0,1:T(4,128)(2,1)} %add_convert_fusion), calls=%async_computation | async-start | bytes 2097152 | tf_op jit(solution)/shard_map/all_to_all | solution.py:113
  52.8 0.5 fusion.66
  53.4 0.1 copy.55
  53.5 0.1 copy.53
  53.6 1.0 fusion.45
  54.6 1.0 fusion.44
  55.6 0.6 convolution_negate_fusion.1
  56.2 0.6 fusion.29
  56.8 0.8 fusion.8
  57.7 0.8 fusion.12
  58.5 1.8 convolution_subtract_fusion.1
  60.4 1.9 convolution_add_fusion.1
  62.2 42.2 %all-to-all-done = bf16[3,512,256]{2,0,1:T(4,128)(2,1)} async-done(((bf16[3,512,256]{2,0,1:T(4,128)(2,1)}), bf16[3,512,256]{2,0,1:T(4,128)(2,1)}, u32[]{:S(2)}, u32[]{:S(2)}) %all-to-all-start) | async-done | bytes 786464 | tf_op jit(solution)/shard_map/all_to_all | solution.py:113
  104.4 1.3 copy.93
  105.8 0.7 copy.47
  106.6 1.0 convert_element_type.162
  107.6 1.4 fusion
  109.0 1.4 convolution_bitcast_fusion
  110.4 1.2 fusion.38
  111.7 1.2 fusion.37
  112.9 1.5 convolution_add_fusion.2
  114.4 1.4 multiply_subtract_fusion
  115.8 0.8 fusion.58
  116.7 0.8 fusion.56
  117.5 0.9 convolution_subtract_fusion
  118.4 0.9 convolution_add_fusion
  119.4 0.6 fusion.17
  120.0 0.3 copy-done.5
  120.3 1.4 fusion.2
  121.8 2.0 copy.62
  123.8 2.0 mul.429
  125.8 2.1 fusion.23
  127.9 9.6 %all-to-all-start.1 = ((bf16[8,64,256]{2,0,1:T(8,128)(2,1)}), bf16[8,64,256]{2,0,1:T(8,128)(2,1)S(1)}, u32[]{:S(2)}, u32[]{:S(2)}) async-start(bf16[8,64,256]{2,0,1:T(8,128)(2,1)} %fusion.23), calls=%async_computation.1 | async-start | bytes 524288 | tf_op jit(solution)/shard_map/all_to_all | solution.py:117
  137.7 22.6 %all-to-all-done.1 = bf16[8,64,256]{2,0,1:T(8,128)(2,1)S(1)} async-done(((bf16[8,64,256]{2,0,1:T(8,128)(2,1)}), bf16[8,64,256]{2,0,1:T(8,128)(2,1)S(1)}, u32[]{:S(2)}, u32[]{:S(2)}) %all-to-all-start.1) | async-done | bytes 262176 | tf_op jit(solution)/shard_map/all_to_all | solution.py:117
  160.3 2.4 %multiply_reduce_fusion = bf16[256,2048]{1,0:T(8,128)(2,1)} fusion(bf16[4,128,256]{2,1,0:T(8,128)(2,1)S(1)} %bitcast.118, bf16[4,128,2048]{2,1,0:T(8,128)(2,1)S(1)} %bitcast.103, f32[4,2048]{1,0:T(4,128)S(1)} %bitcast.119), kind=kOutput, calls=%fused_computation | convolution fusion | flops 540540928 | bytes 3440640 | tf_op jit(solution)/shard_map/bkn,bkt->bnt/dot_general | solution.py:123
  162.7 38.3 %reduce-scatter.2.cloned.1.call-done = bf16[256,256]{0,1:T(8,128)(2,1)} async-done(((bf16[2048,256]{0,1:T(8,128)(2,1)}), bf16[256,256]{0,1:T(8,128)(2,1)}) %reduce-scatter.2.cloned.1.call-update) | async-done | bytes 131088 | tf_op jit(solution)/shard_map/reduce_scatter | solution.py:126
  (27 shorter events, 0.5 us)
Async XLA Ops:
  6.5 153.8 %copy-start = (bf16[512,2048]{1,0:T(8,128)(2,1)S(1)}, bf16[512,2048]{1,0:T(8,128)(2,1)}, u32[]{:S(2)}) copy-start(bf16[512,2048]{1,0:T(8,128)(2,1)} %param.10) | copy-start | bytes 6291460
  6.5 4.8 %copy-start.8 = (f32[3,7,512]{2,1,0:T(8,128)S(1)}, f32[3,7,512]{2,1,0:T(8,128)}, u32[]{:S(2)}) copy-start(f32[3,7,512]{2,1,0:T(8,128)} %param.7) | copy-start | bytes 129028
  9.5 10.8 %collective-permute-start = (bf16[3,512,6]{2,0,1:T(4,128)(2,1)}, bf16[3,512,6]{2,0,1:T(4,128)(2,1)}, u32[]{:S(2)}, u32[]{:S(2)}) collective-permute-start(bf16[3,512,6]{2,0,1:T(4,128)(2,1)} %slice.93), channel_id=1, source_target_pairs={{0,8},{8,16},{16,24},{24,32},{32,40},{40,48},{48,56},{56,64},{64,7... | collective-permute-start | bytes 55304 | tf_op jit(solution)/shard_map/ppermute | solution.py:18
  32.9 22.7 %copy-start.3 = (f32[8,16384]{1,0:T(8,128)S(1)}, f32[8,16384]{1,0:T(8,128)}, u32[]{:S(2)}) copy-start(f32[8,16384]{1,0:T(8,128)} %param.8) | copy-start | bytes 1572868
  32.9 71.5 %all-to-all-start = ((bf16[3,512,256]{2,0,1:T(4,128)(2,1)}), bf16[3,512,256]{2,0,1:T(4,128)(2,1)}, u32[]{:S(2)}, u32[]{:S(2)}) async-start(bf16[3,512,256]{2,0,1:T(4,128)(2,1)} %add_convert_fusion), calls=%async_computation | async-start | bytes 2097152 | tf_op jit(solution)/shard_map/all_to_all | solution.py:113
  54.5 1.6 copy-start.6
  55.5 0.7 copy-start.4
  112.9 1.5 copy-start.1
  112.9 1.5 copy-start.2
  118.4 1.0 copy-start.7
  119.4 0.9 copy-start.5
  120.3 5.5 %copy-start.10 = (f32[8]{0:T(128)S(1)}, f32[8]{0:T(128)}, u32[]{:S(2)}) copy-start(f32[8]{0:T(128)} %param.9) | copy-start | bytes 100
  121.8 15.8 %copy-start.9 = (f32[4,16]{1,0:T(4,128)S(1)}, f32[4,16]{1,0:T(4,128)}, u32[]{:S(2)}) copy-start(f32[4,16]{1,0:T(4,128)} %param.11) | copy-start | bytes 772
  127.9 32.4 %all-to-all-start.1 = ((bf16[8,64,256]{2,0,1:T(8,128)(2,1)}), bf16[8,64,256]{2,0,1:T(8,128)(2,1)S(1)}, u32[]{:S(2)}, u32[]{:S(2)}) async-start(bf16[8,64,256]{2,0,1:T(8,128)(2,1)} %fusion.23), calls=%async_computation.1 | async-start | bytes 524288 | tf_op jit(solution)/shard_map/all_to_all | solution.py:117
  137.5 63.5 %reduce-scatter.2.cloned.1.call-start = ((), (), s32[]{:S(2)}) async-start(), calls=%async_computation.3 | async-start | bytes 1179648 | tf_op jit(solution)/shard_map/reduce_scatter | solution.py:126
Sparse Core Ops, SparseCore 0:
  162.8 38.0 reduce-scatter.1
where the time goes:
time: 209 us; the launch traced here: 208 us
  waiting for transfers between devices  107 us (51%)
  starting transfers between devices  31.5 us (15%)
  matrix products  22.6 us (11%)
  other arithmetic  17.2 us (8%)
  local copies, waits for them, and re-layouts  16.3 us (8%)
  between operations  13.7 us (7%)
    all_to_all x1, waiting for transfers between devices, local(): lax.all_to_all(featured, 'seq', split_axis=1, concat_axis=2, tiled=True)  42.2 us
    reduce_scatter x1, waiting for transfers between devices, local(): lax.psum_scatter(jnp.sum(products * scale_cols[:, :, None], axis=0).astyp...  38.3 us
    all_to_all x1, waiting for transfers between devices, local(): lax.all_to_all(gated, 'seq', split_axis=1, concat_axis=0, tiled=True)  22.6 us
    all_to_all x1, starting transfers between devices, local(): lax.all_to_all(featured, 'seq', split_axis=1, concat_axis=2, tiled=True)  19.9 us
    dot_general x12, matrix products, right_mul(): return jnp.einsum('ckn,nm->ckm', signal, matrix, precision=TRIPLE)  14.1 us
    convert_element_type x1, other arithmetic, featurize(): return running.astype(jnp.bfloat16)  12.6 us
    all_to_all x1, starting transfers between devices, local(): lax.all_to_all(gated, 'seq', split_axis=1, concat_axis=0, tiled=True)  9.63 us
    mul x7, local copies, waits for them, and re-layouts, featurize(): weights[:, lag_idx, :, None]  5.41 us
  transfers between devices with their start and end apart: 4, of which 4 were waited for; matrix products, arithmetic and copies ran while one was open for 7% of the time, Pallas kernels for 0%

commit v1 on v0

--- a/solution.py
+++ b/solution.py
@@ -86,11 +86,11 @@
 
 def featurize(extended, weights, length):
     tap_count = weights.shape[1]
-    running = jnp.zeros(extended.shape[:2] + (length,), jnp.float32)
+    running = jnp.zeros(extended.shape[:1] + (length,) + extended.shape[2:], jnp.float32)
     for lag_idx in range(tap_count):
         offset = tap_count - 1 - lag_idx
-        running = running + weights[:, lag_idx, :, None] * extended[
-            :, :, offset : offset + length
+        running = running + weights[:, lag_idx, None, :] * extended[
+            :, offset : offset + length, :
         ].astype(jnp.float32)
     return running.astype(jnp.bfloat16)
 
@@ -106,30 +106,26 @@
     length = tok_rows * groups
     tables = make_tables(length)
     spectrum = forward(long_filter, tables)
-    columns = jnp.transpose(projected, (0, 2, 1))
     rim_width = KS - 1
-    prior_rows = passed_along(columns[:, :, tok_rows - rim_width :], "seq", 1)
-    featured = featurize(jnp.concatenate([prior_rows, columns], axis=2), feat_weight, tok_rows)
-    regrouped = lax.all_to_all(featured, "seq", split_axis=1, concat_axis=2, tiled=True)
-    gated_kv = multiply_round(regrouped[1], regrouped[2])
-    filtered = long_mix(gated_kv, spectrum, skip_gain, tables)
-    gated = multiply_round(regrouped[0], filtered)
-    gated_home = lax.all_to_all(gated, "seq", split_axis=1, concat_axis=0, tiled=True)
+    prior_rows = passed_along(projected[:, tok_rows - rim_width :, :], "seq", 1)
+    featured = featurize(jnp.concatenate([prior_rows, projected], axis=1), feat_weight, tok_rows)
+    gated_kv = multiply_round(featured[1], featured[2])
+    kv_cols = jnp.transpose(gated_kv, (1, 0))
+    kv_owned = lax.all_to_all(kv_cols, "seq", split_axis=0, concat_axis=1, tiled=True)
+    filtered = long_mix(kv_owned, spectrum, skip_gain, tables)
+    filtered_home = lax.all_to_all(filtered, "seq", split_axis=1, concat_axis=0, tiled=True)
+    gated = multiply_round(featured[0], jnp.transpose(filtered_home, (1, 0)))
     block_count = local_ch // BLK
     out_width = out_values.shape[1]
-    stacked = gated_home.reshape(block_count, BLK, tok_rows)
+    stacked = gated.reshape(tok_rows, block_count, BLK)
     weight_blocks = out_values.reshape(block_count, BLK, out_width)
     scale_cols = jnp.repeat(out_scales, BLK, axis=1)
     products = jnp.einsum(
-        "bkn,bkt->bnt", weight_blocks, stacked, preferred_element_type=jnp.float32
+        "tbk,bkn->btn", stacked, weight_blocks, preferred_element_type=jnp.float32
     )
-    summed = lax.psum_scatter(
-        jnp.sum(products * scale_cols[:, :, None], axis=0).astype(jnp.bfloat16),
-        "tensor",
-        scatter_dimension=0,
-        tiled=True,
-    )
-    return jnp.transpose(summed, (1, 0))
+    partial = jnp.sum(products * scale_cols[:, None, :], axis=0).astype(jnp.bfloat16)
+    summed = lax.psum_scatter(partial, "tensor", scatter_dimension=1, tiled=True)
+    return summed
 
 
 def solution(mesh):

time: 209 us -> 166 us (0.79)
  waiting for transfers between devices: 107 us -> 76.7 us
  starting transfers between devices: 31.5 us -> 26.4 us
  local copies, waits for them, and re-layouts: 16.3 us -> 11.3 us
  other arithmetic: 17.2 us -> 13.2 us
    all_to_all x2, waiting for transfers between devices: 64.8 us -> 38.4 us  [the longest x1 22.6 us: local(): lax.all_to_all(filtered, 'seq', split_axis=1, concat_axis=0, tiled=True)]
    convert_element_type x1, other arithmetic: 12.6 us -> 7.02 us  [featurize(): return running.astype(jnp.bfloat16)]
    mul x7 -> x0, local copies, waits for them, and re-layouts: 5.41 us -> none  [featurize(): weights[:, lag_idx, :, None]]
    all_to_all x2, starting transfers between devices: 29.6 us -> 24.3 us  [the longest x1 19.3 us: local(): lax.all_to_all(kv_cols, 'seq', split_axis=0, concat_axis=1, tiled=True)]
    mul x2, local copies, waits for them, and re-layouts: 4.04 us -> 0.34 us  [inverse(): out_half.reshape(out_half.shape[0], half_a * size_b)]
    unnamed x25 -> x33, local copies, waits for them, and re-layouts: 2.37 us -> 5.95 us
    ppermute x1, waiting for transfers between devices: 3.41 us -> 0.01 us  [passed_along(): return lax.ppermute(x, axis, pairs)]
  transfers between devices with their start and end apart: 4 -> 4, of which waited for: 4 -> 3; matrix products, arithmetic and copies ran while one was open for 7% -> 11% of each run, Pallas kernels for 0% -> 0%
where the time goes in v1:
time: 166 us; the launch traced here: 165 us
  waiting for transfers between devices  76.7 us (46%)
  starting transfers between devices  26.4 us (16%)
  matrix products  24.2 us (15%)
  between operations  13.8 us (8%)
  other arithmetic  13.2 us (8%)
  local copies, waits for them, and re-layouts  11.3 us (7%)
    reduce_scatter x1, waiting for transfers between devices, local(): lax.psum_scatter(partial, 'tensor', scatter_dimension=1, tiled=True)  38.2 us
    all_to_all x1, waiting for transfers between devices, local(): lax.all_to_all(filtered, 'seq', split_axis=1, concat_axis=0, tiled=True)  22.6 us
    all_to_all x1, starting transfers between devices, local(): lax.all_to_all(kv_cols, 'seq', split_axis=0, concat_axis=1, tiled=True)  19.3 us
    all_to_all x1, waiting for transfers between devices, local(): lax.all_to_all(kv_cols, 'seq', split_axis=0, concat_axis=1, tiled=True)  15.8 us
    dot_general x12, matrix products, right_mul(): return jnp.einsum('ckn,nm->ckm', signal, matrix, precision=TRIPLE)  15.4 us
    convert_element_type x1, other arithmetic, featurize(): return running.astype(jnp.bfloat16)  7.02 us
    unnamed x33, local copies, waits for them, and re-layouts  5.95 us
    all_to_all x1, starting transfers between devices, local(): lax.all_to_all(filtered, 'seq', split_axis=1, concat_axis=0, tiled=True)  4.97 us
  transfers between devices with their start and end apart: 4, of which 3 were waited for; matrix products, arithmetic and copies ran while one was open for 11% of the time, Pallas kernels for 0%

profile of v1, /device:TPU:32, one launch (start us, length us, event | category | flops | bytes accessed | tf_op | source)
XLA Modules:
  0.0 165.5 jit_solution(1505674772632463204)
XLA Ops:
  6.5 0.9 slice.71
  7.4 1.0 copy.21
  8.4 2.0 %collective-permute-start = (bf16[3,6,512]{1,2,0:T(8,128)(2,1)}, bf16[3,6,512]{1,2,0:T(8,128)(2,1)}, u32[]{:S(2)}, u32[]{:S(2)}) collective-permute-start(bf16[3,6,512]{1,2,0:T(8,128)(2,1)} %copy.21), channel_id=1, source_target_pairs={{0,8},{8,16},{16,24},{24,32},{32,40},{40,48},{48,56},{56,64},{64,7... | collective-permute-start | bytes 55304 | tf_op jit(solution)/shard_map/ppermute | solution.py:18
  10.4 1.0 fusion.45
  11.4 1.0 fusion.44
  12.4 1.2 fusion.131
  13.6 1.6 convolution_negate_fusion.1
  15.3 1.6 fusion.28
  16.9 0.6 copy_bitcast_fusion.5
  17.5 0.6 copy_bitcast_fusion.1
  18.1 0.5 fusion.66
  18.6 2.3 %copy.20 = bf16[3,256,512]{1,2,0:T(8,128)(2,1)} copy(bf16[3,256,512]{2,1,0:T(8,128)(2,1)} %param.6) | data formatting | bytes 1572864 | tf_op args[0]
  20.9 0.6 copy.76
  21.6 0.8 copy.29
  22.4 7.0 %add_convert_fusion = bf16[3,256,512]{1,2,0:T(8,128)(2,1)S(1)} fusion(bf16[3,256,512]{1,2,0:T(8,128)(2,1)} %copy.20, bf16[3,6,512]{1,2,0:T(8,128)(2,1)} %collective-permute-done, f32[3,512]{1,0:T(4,128)} %get-tuple-element.14, f32[3,512]{1,0:T(4,128)} %get-tuple-element.15, f32[3,512]{1,0:T(4,128)S(1)} %get-tuple-element.16, ...), kind=kLoop, calls=%fused_computation.6 | loop fusion | flops 15335424 | bytes 1634304 | tf_op jit(solution)/shard_map/convert_element_type | solution.py:95
  29.4 0.9 copy-done.5
  30.3 0.8 fusion.33
  31.1 19.3 %all-to-all-start = ((bf16[64,8,256]{2,1,0:T(8,128)(2,1)}), bf16[64,8,256]{2,1,0:T(8,128)(2,1)}, u32[]{:S(2)}, u32[]{:S(2)}) async-start(bf16[64,8,256]{2,1,0:T(8,128)(2,1)} %fusion.33), calls=%async_computation | async-start | bytes 524288 | tf_op jit(solution)/shard_map/all_to_all | solution.py:114
  50.4 2.2 %fusion.3 = f32[8,256,128]{2,1,0:T(8,128)S(1)} fusion(f32[256,8,128]{2,0,1:T(8,128)} %fusion.28, f32[256,8,128]{2,0,1:T(8,128)S(1)} %convolution_negate_fusion.1, f32[256,128]{1,0:T(8,128)S(1)} %copy.31, f32[256,128]{1,0:T(8,128)} %copy.29), kind=kOutput, calls=%fused_computation.25 | convolution fusion | flops 202342400 | bytes 3407872 | tf_op jit(solution)/shard_map/ckn,nm->ckm/dot_general | solution.py:48
  52.6 0.8 fusion.7
  53.4 1.8 %convolution_subtract_fusion.1 = f32[8,256,128]{2,1,0:T(8,128)} fusion(f32[8,256,128]{2,1,0:T(8,128)S(1)} %fusion.3, f32[256,8,128]{2,0,1:T(8,128)S(1)} %convolution_negate_fusion.1, f32[256,8,128]{2,0,1:T(8,128)S(1)} %copy-done.1, f32[256,128]{1,0:T(8,128)S(1)} %copy.31, f32[256,128]{1,0:T(8,128)S(1)} %copy-done.4), kind=kOutput, calls=%fused_computation.17 | convolution fusion | flops 202604544 | bytes 4456448 | tf_op jit(solution)/shard_map/ckn,nm->ckm/dot_general | solution.py:48
  55.3 1.8 %convolution_add_fusion.1 = f32[8,256,128]{2,1,0:T(8,128)} fusion(f32[8,256,128]{2,1,0:T(8,128)S(1)} %fusion.7, f32[256,8,128]{2,0,1:T(8,128)S(1)} %copy-done.1, f32[256,8,128]{2,0,1:T(8,128)S(1)} %convolution_negate_fusion.1, f32[256,128]{1,0:T(8,128)S(1)} %copy.31, f32[256,128]{1,0:T(8,128)S(1)} %copy-done.4), kind=kOutput, calls=%fused_computation.19 | convolution fusion | flops 202604544 | bytes 4456448 | tf_op jit(solution)/shard_map/ckn,nm->ckm/dot_general | solution.py:48
  57.1 15.8 %all-to-all-done = bf16[64,8,256]{2,1,0:T(8,128)(2,1)} async-done(((bf16[64,8,256]{2,1,0:T(8,128)(2,1)}), bf16[64,8,256]{2,1,0:T(8,128)(2,1)}, u32[]{:S(2)}, u32[]{:S(2)}) %all-to-all-start) | async-done | bytes 262176 | tf_op jit(solution)/shard_map/all_to_all | solution.py:114
  72.9 1.0 copy.23
  73.9 0.1 reshape.64
  74.0 1.4 fusion
  75.4 0.5 convolution_bitcast_fusion
  75.9 1.2 fusion.38
  77.2 1.2 fusion.37
  78.4 1.3 convolution_add_fusion.2
  79.7 0.3 copy-done.3
  79.9 1.4 multiply_subtract_fusion
  81.3 0.8 fusion.58
  82.2 0.8 fusion.56
  83.0 1.1 convolution_subtract_fusion
  84.2 0.9 convolution_add_fusion
  85.0 0.6 fusion.12
  85.7 0.3 copy-done.8
  86.0 0.6 fusion.2
  86.6 0.2 copy.38
  86.8 0.1 mul.424
  87.0 0.3 copy-done.12
  87.3 1.9 %fusion.22 = bf16[8,64,256]{2,0,1:T(8,128)(2,1)} fusion(f32[8,64,256]{2,1,0:T(8,128)S(1)} %mul.424, f32[8]{0:T(128)S(1)} %copy-done.12, bf16[64,8,256]{2,1,0:T(8,128)(2,1)} %all-to-all-done), kind=kLoop, calls=%fused_computation.53 | loop fusion | flops 524288 | bytes 1048608 | tf_op jit(solution)/shard_map/convert_element_type | solution.py:84
  89.2 5.0 %all-to-all-start.1 = ((bf16[8,64,256]{2,0,1:T(8,128)(2,1)}), bf16[8,64,256]{2,0,1:T(8,128)(2,1)S(1)}, u32[]{:S(2)}, u32[]{:S(2)}) async-start(bf16[8,64,256]{2,0,1:T(8,128)(2,1)} %fusion.22), calls=%async_computation.1 | async-start | bytes 524288 | tf_op jit(solution)/shard_map/all_to_all | solution.py:116
  94.4 22.6 %all-to-all-done.1 = bf16[8,64,256]{2,0,1:T(8,128)(2,1)S(1)} async-done(((bf16[8,64,256]{2,0,1:T(8,128)(2,1)}), bf16[8,64,256]{2,0,1:T(8,128)(2,1)S(1)}, u32[]{:S(2)}, u32[]{:S(2)}) %all-to-all-start.1) | async-done | bytes 262176 | tf_op jit(solution)/shard_map/all_to_all | solution.py:116
  117.0 1.0 fusion.21
  118.0 2.4 %multiply_reduce_fusion = bf16[256,2048]{1,0:T(8,128)(2,1)} fusion(bf16[256,4,128]{0,2,1:T(8,128)(2,1)S(1)} %bitcast.113, bf16[4,128,2048]{2,1,0:T(8,128)(2,1)S(1)} %bitcast.110, f32[4,2048]{1,0:T(4,128)S(1)} %bitcast.115), kind=kOutput, calls=%fused_computation | convolution fusion | flops 540540928 | bytes 3440640 | tf_op jit(solution)/shard_map/tbk,bkn->btn/dot_general | solution.py:123
  120.4 38.2 %reduce-scatter.2.cloned.1.call-done = bf16[256,256]{1,0:T(8,128)(2,1)} async-done(((bf16[256,2048]{1,0:T(8,128)(2,1)}), bf16[256,256]{1,0:T(8,128)(2,1)}) %reduce-scatter.2.cloned.1.call-update) | async-done | bytes 131088 | tf_op jit(solution)/shard_map/reduce_scatter | solution.py:127
  (29 shorter events, 0.3 us)
Async XLA Ops:
  6.5 111.5 %copy-start = (bf16[512,2048]{1,0:T(8,128)(2,1)S(1)}, bf16[512,2048]{1,0:T(8,128)(2,1)}, u32[]{:S(2)}) copy-start(bf16[512,2048]{1,0:T(8,128)(2,1)} %param.10) | copy-start | bytes 6291460
  8.4 6.9 %copy-start.6 = (f32[8,16384]{1,0:T(8,128)S(1)}, f32[8,16384]{1,0:T(8,128)}, u32[]{:S(2)}) copy-start(f32[8,16384]{1,0:T(8,128)} %param.8) | copy-start | bytes 1572868
  8.4 14.0 %collective-permute-start = (bf16[3,6,512]{1,2,0:T(8,128)(2,1)}, bf16[3,6,512]{1,2,0:T(8,128)(2,1)}, u32[]{:S(2)}, u32[]{:S(2)}) collective-permute-start(bf16[3,6,512]{1,2,0:T(8,128)(2,1)} %copy.21), channel_id=1, source_target_pairs={{0,8},{8,16},{16,24},{24,32},{32,40},{40,48},{48,56},{56,64},{64,7... | collective-permute-start | bytes 55304 | tf_op jit(solution)/shard_map/ppermute | solution.py:18
  11.4 5.5 %copy-start.9 = (f32[256,256]{1,0:T(8,128)}, f32[256,256]{1,0:T(8,128)S(1)}, u32[]{:S(2)}) copy-start(f32[256,256]{1,0:T(8,128)S(1)} %fusion.45) | copy-start | bytes 786436
  12.4 4.5 %copy-start.7 = (f32[256,256]{1,0:T(8,128)}, f32[256,256]{1,0:T(8,128)S(1)}, u32[]{:S(2)}) copy-start(f32[256,256]{1,0:T(8,128)S(1)} %fusion.44) | copy-start | bytes 786436
  29.4 0.9 copy-start.5
  31.1 41.9 %all-to-all-start = ((bf16[64,8,256]{2,1,0:T(8,128)(2,1)}), bf16[64,8,256]{2,1,0:T(8,128)(2,1)}, u32[]{:S(2)}, u32[]{:S(2)}) async-start(bf16[64,8,256]{2,1,0:T(8,128)(2,1)} %fusion.33), calls=%async_computation | async-start | bytes 524288 | tf_op jit(solution)/shard_map/all_to_all | solution.py:114
  50.4 2.2 %copy-start.1 = (f32[256,8,128]{2,0,1:T(8,128)S(1)}, f32[256,8,128]{2,0,1:T(8,128)}, u32[]{:S(2)}) copy-start(f32[256,8,128]{2,0,1:T(8,128)} %fusion.28) | copy-start | bytes 3145732
  50.4 2.2 %copy-start.4 = (f32[256,128]{1,0:T(8,128)S(1)}, f32[256,128]{1,0:T(8,128)}, u32[]{:S(2)}) copy-start(f32[256,128]{1,0:T(8,128)} %copy.29) | copy-start | bytes 393220
  57.1 18.3 %copy-start.10 = (f32[256,256]{1,0:T(8,128)S(1)}, f32[256,256]{1,0:T(8,128)}, u32[]{:S(2)}) copy-start(f32[256,256]{1,0:T(8,128)} %copy-done.9) | copy-start | bytes 786436
  78.4 1.3 copy-start.2
  78.4 1.5 copy-start.3
  85.0 1.0 copy-start.8
  86.6 0.7 copy-start.12
  86.8 7.4 %copy-start.11 = (f32[4,16]{1,0:T(4,128)S(1)}, f32[4,16]{1,0:T(4,128)}, u32[]{:S(2)}) copy-start(f32[4,16]{1,0:T(4,128)} %param.11) | copy-start | bytes 772
  89.2 27.8 %all-to-all-start.1 = ((bf16[8,64,256]{2,0,1:T(8,128)(2,1)}), bf16[8,64,256]{2,0,1:T(8,128)(2,1)S(1)}, u32[]{:S(2)}, u32[]{:S(2)}) async-start(bf16[8,64,256]{2,0,1:T(8,128)(2,1)} %fusion.22), calls=%async_computation.1 | async-start | bytes 524288 | tf_op jit(solution)/shard_map/all_to_all | solution.py:116
  94.2 64.4 %reduce-scatter.2.cloned.1.call-start = ((), (), s32[]{:S(2)}) async-start(), calls=%async_computation.3 | async-start | bytes 1179648 | tf_op jit(solution)/shard_map/reduce_scatter | solution.py:127
Sparse Core Ops, SparseCore 0:
  120.6 38.0 reduce-scatter.1

commit v2 on v1

--- a/solution.py
+++ b/solution.py
@@ -124,8 +124,10 @@
         "tbk,bkn->btn", stacked, weight_blocks, preferred_element_type=jnp.float32
     )
     partial = jnp.sum(products * scale_cols[:, None, :], axis=0).astype(jnp.bfloat16)
-    summed = lax.psum_scatter(partial, "tensor", scatter_dimension=1, tiled=True)
-    return summed
+    n_tensor = lax.axis_size("tensor")
+    pieces = partial.reshape(tok_rows, n_tensor, out_width // n_tensor).transpose(1, 0, 2)
+    gathered = lax.all_to_all(pieces, "tensor", 0, 0, tiled=True)
+    return jnp.sum(gathered.astype(jnp.float32), axis=0).astype(jnp.bfloat16)
 
 
 def solution(mesh):

time: 166 us -> 140 us (0.84)
  the two profiles are of different devices: /device:TPU:32 before, /device:TPU:1 now
where the time goes in v2:
time: 140 us; the launch traced here: 139 us
  waiting for transfers between devices  40.2 us (29%)
  starting transfers between devices  26.9 us (19%)
  matrix products  24.2 us (17%)
  blocking collectives  19.4 us (14%)
  local copies, waits for them, and re-layouts  14.1 us (10%)
  other arithmetic  14 us (10%)
    all_to_all x1, waiting for transfers between devices, local(): lax.all_to_all(filtered, 'seq', split_axis=1, concat_axis=0, tiled=True)  23.5 us
    all_to_all x1, blocking collectives, local(): gathered = lax.all_to_all(pieces, 'tensor', 0, 0, tiled=True)  19.4 us
    all_to_all x1, starting transfers between devices, local(): lax.all_to_all(kv_cols, 'seq', split_axis=0, concat_axis=1, tiled=True)  17.7 us
    all_to_all x1, waiting for transfers between devices, local(): lax.all_to_all(kv_cols, 'seq', split_axis=0, concat_axis=1, tiled=True)  16.7 us
    dot_general x12, matrix products, right_mul(): return jnp.einsum('ckn,nm->ckm', signal, matrix, precision=TRIPLE)  15.5 us
    convert_element_type x1, other arithmetic, featurize(): return running.astype(jnp.bfloat16)  6.96 us
    unnamed x33, local copies, waits for them, and re-layouts  5.98 us
    ppermute x1, starting transfers between devices, passed_along(): return lax.ppermute(x, axis, pairs)  5.04 us
  transfers between devices with their start and end apart: 3, of which 2 were waited for; matrix products, arithmetic and copies ran while one was open for 13% of the time, Pallas kernels for 0%

profile of v2, /device:TPU:1, one launch (start us, length us, event | category | flops | bytes accessed | tf_op | source)
XLA Modules:
  0.0 139.2 jit_solution(5920417558530997269)
XLA Ops:
  0.0 0.9 slice.71
  0.9 1.0 copy.85
  1.9 5.0 %collective-permute-start = (bf16[3,6,512]{1,2,0:T(8,128)(2,1)}, bf16[3,6,512]{1,2,0:T(8,128)(2,1)}, u32[]{:S(2)}, u32[]{:S(2)}) collective-permute-start(bf16[3,6,512]{1,2,0:T(8,128)(2,1)} %copy.85), channel_id=1, source_target_pairs={{0,8},{8,16},{16,24},{24,32},{32,40},{40,48},{48,56},{56,64},{64,7... | collective-permute-start | bytes 55304 | tf_op jit(solution)/shard_map/ppermute | solution.py:18
  6.9 1.0 fusion.45
  7.9 1.0 fusion.44
  8.9 1.2 fusion.131
  10.1 1.6 %convolution_negate_fusion.1 = f32[256,8,128]{2,0,1:T(8,128)S(1)} fusion(f32[8,128,128]{2,0,1:T(8,128)} %bitcast.115, f32[256,256]{1,0:T(8,128)S(1)} %fusion.44), kind=kOutput, calls=%fused_computation.20 | convolution fusion | flops 201588736 | bytes 1703936 | tf_op jit(solution)/shard_map/kn,cnb->ckb/dot_general | solution.py:56
  11.8 1.6 %fusion.28 = f32[256,8,128]{2,0,1:T(8,128)} fusion(f32[8,128,128]{2,0,1:T(8,128)S(1)} %bitcast.116, f32[256,256]{1,0:T(8,128)S(1)} %fusion.45), kind=kOutput, calls=%fused_computation.60 | convolution fusion | flops 201326592 | bytes 1703936 | tf_op jit(solution)/shard_map/kn,cnb->ckb/dot_general | solution.py:55
  13.4 0.6 copy_bitcast_fusion.5
  14.0 0.6 copy_bitcast_fusion.1
  14.6 0.5 fusion.66
  15.1 2.3 %copy.84 = bf16[3,256,512]{1,2,0:T(8,128)(2,1)} copy(bf16[3,256,512]{2,1,0:T(8,128)(2,1)} %param.6) | data formatting | bytes 1572864 | tf_op args[0]
  17.4 0.6 copy.142
  18.1 0.8 copy.93
  18.9 7.0 %add_convert_fusion = bf16[3,256,512]{1,2,0:T(8,128)(2,1)S(1)} fusion(bf16[3,256,512]{1,2,0:T(8,128)(2,1)} %copy.84, bf16[3,6,512]{1,2,0:T(8,128)(2,1)} %collective-permute-done, f32[3,512]{1,0:T(4,128)} %get-tuple-element.14, f32[3,512]{1,0:T(4,128)} %get-tuple-element.15, f32[3,512]{1,0:T(4,128)S(1)} %get-tuple-element.16, ...), kind=kLoop, calls=%fused_computation.6 | loop fusion | flops 15335424 | bytes 1634304 | tf_op jit(solution)/shard_map/convert_element_type | solution.py:95
  25.9 0.9 copy-done.5
  26.7 0.8 fusion.33
  27.5 17.7 %all-to-all-start = ((bf16[64,8,256]{2,1,0:T(8,128)(2,1)}), bf16[64,8,256]{2,1,0:T(8,128)(2,1)}, u32[]{:S(2)}, u32[]{:S(2)}) async-start(bf16[64,8,256]{2,1,0:T(8,128)(2,1)} %fusion.33), calls=%async_computation | async-start | bytes 524288 | tf_op jit(solution)/shard_map/all_to_all | solution.py:114
  45.2 2.2 %fusion.3 = f32[8,256,128]{2,1,0:T(8,128)S(1)} fusion(f32[256,8,128]{2,0,1:T(8,128)} %fusion.28, f32[256,8,128]{2,0,1:T(8,128)S(1)} %convolution_negate_fusion.1, f32[256,128]{1,0:T(8,128)S(1)} %copy.95, f32[256,128]{1,0:T(8,128)} %copy.93), kind=kOutput, calls=%fused_computation.25 | convolution fusion | flops 202342400 | bytes 3407872 | tf_op jit(solution)/shard_map/ckn,nm->ckm/dot_general | solution.py:48
  47.4 0.8 fusion.7
  48.3 1.8 %convolution_subtract_fusion.1 = f32[8,256,128]{2,1,0:T(8,128)} fusion(f32[8,256,128]{2,1,0:T(8,128)S(1)} %fusion.3, f32[256,8,128]{2,0,1:T(8,128)S(1)} %convolution_negate_fusion.1, f32[256,8,128]{2,0,1:T(8,128)S(1)} %copy-done.1, f32[256,128]{1,0:T(8,128)S(1)} %copy.95, f32[256,128]{1,0:T(8,128)S(1)} %copy-done.4), kind=kOutput, calls=%fused_computation.17 | convolution fusion | flops 202604544 | bytes 4456448 | tf_op jit(solution)/shard_map/ckn,nm->ckm/dot_general | solution.py:48
  50.1 1.9 %convolution_add_fusion.1 = f32[8,256,128]{2,1,0:T(8,128)} fusion(f32[8,256,128]{2,1,0:T(8,128)S(1)} %fusion.7, f32[256,8,128]{2,0,1:T(8,128)S(1)} %copy-done.1, f32[256,8,128]{2,0,1:T(8,128)S(1)} %convolution_negate_fusion.1, f32[256,128]{1,0:T(8,128)S(1)} %copy.95, f32[256,128]{1,0:T(8,128)S(1)} %copy-done.4), kind=kOutput, calls=%fused_computation.19 | convolution fusion | flops 202604544 | bytes 4456448 | tf_op jit(solution)/shard_map/ckn,nm->ckm/dot_general | solution.py:48
  52.0 16.7 %all-to-all-done = bf16[64,8,256]{2,1,0:T(8,128)(2,1)} async-done(((bf16[64,8,256]{2,1,0:T(8,128)(2,1)}), bf16[64,8,256]{2,1,0:T(8,128)(2,1)}, u32[]{:S(2)}, u32[]{:S(2)}) %all-to-all-start) | async-done | bytes 262176 | tf_op jit(solution)/shard_map/all_to_all | solution.py:114
  68.7 1.0 copy.87
  69.8 1.4 fusion
  71.2 0.5 convolution_bitcast_fusion
  71.7 1.2 fusion.38
  72.9 1.2 fusion.37
  74.2 1.3 convolution_add_fusion.2
  75.5 0.3 copy-done.3
  75.7 1.4 multiply_subtract_fusion
  77.1 0.8 fusion.58
  78.0 0.8 fusion.56
  78.8 1.1 convolution_subtract_fusion
  79.9 0.9 convolution_add_fusion
  80.8 0.6 fusion.12
  81.5 0.3 copy-done.8
  81.7 0.6 fusion.2
  82.8 0.3 copy-done.12
  83.1 1.9 %fusion.22 = bf16[8,64,256]{2,0,1:T(8,128)(2,1)} fusion(f32[8,64,256]{2,1,0:T(8,128)S(1)} %mul.424, f32[8]{0:T(128)S(1)} %copy-done.12, bf16[64,8,256]{2,1,0:T(8,128)(2,1)} %all-to-all-done), kind=kLoop, calls=%fused_computation.53 | loop fusion | flops 524288 | bytes 1048608 | tf_op jit(solution)/shard_map/convert_element_type | solution.py:84
  85.0 4.2 %all-to-all-start.1 = ((bf16[8,64,256]{2,0,1:T(8,128)(2,1)}), bf16[8,64,256]{2,0,1:T(8,128)(2,1)S(1)}, u32[]{:S(2)}, u32[]{:S(2)}) async-start(bf16[8,64,256]{2,0,1:T(8,128)(2,1)} %fusion.22), calls=%async_computation.1 | async-start | bytes 524288 | tf_op jit(solution)/shard_map/all_to_all | solution.py:116
  89.3 23.5 %all-to-all-done.1 = bf16[8,64,256]{2,0,1:T(8,128)(2,1)S(1)} async-done(((bf16[8,64,256]{2,0,1:T(8,128)(2,1)}), bf16[8,64,256]{2,0,1:T(8,128)(2,1)S(1)}, u32[]{:S(2)}, u32[]{:S(2)}) %all-to-all-start.1) | async-done | bytes 262176 | tf_op jit(solution)/shard_map/all_to_all | solution.py:116
  112.8 1.0 fusion.21
  113.8 2.4 %multiply_reduce_fusion = bf16[256,2048]{1,0:T(8,128)(2,1)} fusion(bf16[256,4,128]{0,2,1:T(8,128)(2,1)S(1)} %bitcast.117, bf16[4,128,2048]{2,1,0:T(8,128)(2,1)S(1)} %bitcast.113, f32[4,2048]{1,0:T(4,128)S(1)} %bitcast.119), kind=kOutput, calls=%fused_computation | convolution fusion | flops 540540928 | bytes 3440640 | tf_op jit(solution)/shard_map/tbk,bkn->btn/dot_general | solution.py:123
  116.2 1.5 %copy.105 = bf16[256,2048]{0,1:T(8,128)(2,1)S(1)} copy(bf16[256,2048]{1,0:T(8,128)(2,1)} %multiply_reduce_fusion) | data formatting | bytes 2097152 | tf_op jit(solution)/shard_map/convert_element_type | solution.py:126
  117.7 1.3 copy.106
  119.0 19.4 %all_to_all.31 = bf16[8,256,256]{2,1,0:T(8,128)(2,1)S(1)} all-to-all(bf16[8,256,256]{2,1,0:T(8,128)(2,1)} %copy.106), channel_id=1, replica_groups=mesh['seq'=64,'tensor'=8] {'tensor'}, dimensions={0} | all-to-all | bytes 2097152 | tf_op jit(solution)/shard_map/all_to_all | solution.py:129
  138.4 0.8 reduce_sum.22
  (30 shorter events, 0.7 us)
Async XLA Ops:
  0.0 113.8 %copy-start = (bf16[512,2048]{1,0:T(8,128)(2,1)S(1)}, bf16[512,2048]{1,0:T(8,128)(2,1)}, u32[]{:S(2)}) copy-start(bf16[512,2048]{1,0:T(8,128)(2,1)} %param.10) | copy-start | bytes 6291460
  1.9 9.9 %copy-start.6 = (f32[8,16384]{1,0:T(8,128)S(1)}, f32[8,16384]{1,0:T(8,128)}, u32[]{:S(2)}) copy-start(f32[8,16384]{1,0:T(8,128)} %param.8) | copy-start | bytes 1572868
  1.9 17.0 %collective-permute-start = (bf16[3,6,512]{1,2,0:T(8,128)(2,1)}, bf16[3,6,512]{1,2,0:T(8,128)(2,1)}, u32[]{:S(2)}, u32[]{:S(2)}) collective-permute-start(bf16[3,6,512]{1,2,0:T(8,128)(2,1)} %copy.85), channel_id=1, source_target_pairs={{0,8},{8,16},{16,24},{24,32},{32,40},{40,48},{48,56},{56,64},{64,7... | collective-permute-start | bytes 55304 | tf_op jit(solution)/shard_map/ppermute | solution.py:18
  7.9 5.5 %copy-start.9 = (f32[256,256]{1,0:T(8,128)}, f32[256,256]{1,0:T(8,128)S(1)}, u32[]{:S(2)}) copy-start(f32[256,256]{1,0:T(8,128)S(1)} %fusion.45) | copy-start | bytes 786436
  8.9 4.5 %copy-start.7 = (f32[256,256]{1,0:T(8,128)}, f32[256,256]{1,0:T(8,128)S(1)}, u32[]{:S(2)}) copy-start(f32[256,256]{1,0:T(8,128)S(1)} %fusion.44) | copy-start | bytes 786436
  25.8 0.9 copy-start.5
  27.5 41.2 %all-to-all-start = ((bf16[64,8,256]{2,1,0:T(8,128)(2,1)}), bf16[64,8,256]{2,1,0:T(8,128)(2,1)}, u32[]{:S(2)}, u32[]{:S(2)}) async-start(bf16[64,8,256]{2,1,0:T(8,128)(2,1)} %fusion.33), calls=%async_computation | async-start | bytes 524288 | tf_op jit(solution)/shard_map/all_to_all | solution.py:114
  45.2 2.2 %copy-start.1 = (f32[256,8,128]{2,0,1:T(8,128)S(1)}, f32[256,8,128]{2,0,1:T(8,128)}, u32[]{:S(2)}) copy-start(f32[256,8,128]{2,0,1:T(8,128)} %fusion.28) | copy-start | bytes 3145732
  45.2 2.2 %copy-start.4 = (f32[256,128]{1,0:T(8,128)S(1)}, f32[256,128]{1,0:T(8,128)}, u32[]{:S(2)}) copy-start(f32[256,128]{1,0:T(8,128)} %copy.93) | copy-start | bytes 393220
  52.0 19.2 %copy-start.10 = (f32[256,256]{1,0:T(8,128)S(1)}, f32[256,256]{1,0:T(8,128)}, u32[]{:S(2)}) copy-start(f32[256,256]{1,0:T(8,128)} %copy-done.9) | copy-start | bytes 786436
  74.2 1.3 copy-start.2
  74.2 1.5 %copy-start.3 = (f32[8,256,128]{2,1,0:T(8,128)S(1)}, f32[8,256,128]{2,1,0:T(8,128)}, u32[]{:S(2)}) copy-start(f32[8,256,128]{2,1,0:T(8,128)} %convolution_add_fusion.1) | copy-start | bytes 3145732
  80.8 1.0 copy-start.8
  82.4 0.7 copy-start.12
  82.6 6.6 %copy-start.11 = (f32[4,16]{1,0:T(4,128)S(1)}, f32[4,16]{1,0:T(4,128)}, u32[]{:S(2)}) copy-start(f32[4,16]{1,0:T(4,128)} %param.11) | copy-start | bytes 772
  85.0 27.8 %all-to-all-start.1 = ((bf16[8,64,256]{2,0,1:T(8,128)(2,1)}), bf16[8,64,256]{2,0,1:T(8,128)(2,1)S(1)}, u32[]{:S(2)}, u32[]{:S(2)}) async-start(bf16[8,64,256]{2,0,1:T(8,128)(2,1)} %fusion.22), calls=%async_computation.1 | async-start | bytes 524288 | tf_op jit(solution)/shard_map/all_to_all | solution.py:116

commit v3 on v2

--- a/solution.py
+++ b/solution.py
@@ -4,6 +4,8 @@
 import jax.numpy as jnp
 from jax import lax
 from jax.sharding import PartitionSpec as P
+from jax.experimental import pallas as pl
+from jax.experimental.pallas import tpu as pltpu
 
 KS = 7
 BLK = 128
@@ -95,6 +97,41 @@
     return running.astype(jnp.bfloat16)
 
 
+def _feat_body(proj_ref, prior_ref, w_ref, q_ref, kv_ref, ext_ref):
+    rows = proj_ref.shape[1]
+    feats = []
+    for a in range(3):
+        ext_ref[0:2, :] = jnp.zeros((2, ext_ref.shape[1]), jnp.float32)
+        ext_ref[2:8, :] = prior_ref[a].astype(jnp.float32)
+        ext_ref[8 : 8 + rows, :] = proj_ref[a].astype(jnp.float32)
+        acc = jnp.zeros((rows, ext_ref.shape[1]), jnp.float32)
+        for j in range(KS):
+            acc = acc + w_ref[a, j : j + 1, :] * ext_ref[8 - j : 8 - j + rows, :]
+        feats.append(acc.astype(jnp.bfloat16))
+    q_ref[...] = feats[0]
+    kv_ref[...] = (feats[1].astype(jnp.float32) * feats[2].astype(jnp.float32)).astype(jnp.bfloat16)
+
+def featurize_kv(projected, prior, weights, lane_block=128, interpret=False):
+    _, rows, chans = projected.shape
+    grid = (chans // lane_block,)
+    return pl.pallas_call(
+        _feat_body,
+        grid=grid,
+        in_specs=[
+            pl.BlockSpec((3, rows, lane_block), lambda i: (0, 0, i)),
+            pl.BlockSpec((3, KS - 1, lane_block), lambda i: (0, 0, i)),
+            pl.BlockSpec((3, KS, lane_block), lambda i: (0, 0, i)),
+        ],
+        out_specs=[
+            pl.BlockSpec((rows, lane_block), lambda i: (0, i)),
+            pl.BlockSpec((rows, lane_block), lambda i: (0, i)),
+        ],
+        out_shape=[jax.ShapeDtypeStruct((rows, chans), jnp.bfloat16)] * 2,
+        scratch_shapes=[pltpu.VMEM((rows + 8, lane_block), jnp.float32)],
+        interpret=interpret,
+    )(projected, prior, weights)
+
+
 def multiply_round(left_arr, right_arr):
     return (left_arr.astype(jnp.float32) * right_arr.astype(jnp.float32)).astype(jnp.bfloat16)
 
@@ -108,13 +145,12 @@
     spectrum = forward(long_filter, tables)
     rim_width = KS - 1
     prior_rows = passed_along(projected[:, tok_rows - rim_width :, :], "seq", 1)
-    featured = featurize(jnp.concatenate([prior_rows, projected], axis=1), feat_weight, tok_rows)
-    gated_kv = multiply_round(featured[1], featured[2])
+    q_feat, gated_kv = featurize_kv(projected, prior_rows, feat_weight)
     kv_cols = jnp.transpose(gated_kv, (1, 0))
     kv_owned = lax.all_to_all(kv_cols, "seq", split_axis=0, concat_axis=1, tiled=True)
     filtered = long_mix(kv_owned, spectrum, skip_gain, tables)
     filtered_home = lax.all_to_all(filtered, "seq", split_axis=1, concat_axis=0, tiled=True)
-    gated = multiply_round(featured[0], jnp.transpose(filtered_home, (1, 0)))
+    gated = multiply_round(q_feat, jnp.transpose(filtered_home, (1, 0)))
     block_count = local_ch // BLK
     out_width = out_values.shape[1]
     stacked = gated.reshape(tok_rows, block_count, BLK)

time: 140 us -> 131 us (0.936)
  other arithmetic: 14 us -> 5.27 us
  local copies, waits for them, and re-layouts: 14.1 us -> 9.02 us
  Pallas kernels: 0 us -> 3.73 us
    convert_element_type x2 -> x1, other arithmetic: 7.97 us -> 0.04 us  [multiply_round(): right_arr.astype(jnp.float32)]
    unnamed x33 -> x26, local copies, waits for them, and re-layouts: 5.98 us -> 0.47 us
    pallas_call x0 -> x1, Pallas kernels: none -> 3.73 us  [featurize_kv(): pl.pallas_call(_feat_body, grid=grid, in_specs=[pl.BlockSpec((3, rows, la...]
    transpose x0 -> x1, local copies, waits for them, and re-layouts: none -> 1.78 us  [local(): kv_cols = jnp.transpose(gated_kv, (1, 0))]
  transfers between devices with their start and end apart: 3 -> 3, of which waited for: 2 -> 2; matrix products, arithmetic and copies ran while one was open for 13% -> 10% of each run, Pallas kernels for 0% -> 0%
where the time goes in v3:
time: 131 us; the launch traced here: 130 us
  waiting for transfers between devices  40.1 us (31%)
  starting transfers between devices  26.8 us (20%)
  matrix products  25.4 us (19%)
  blocking collectives  19.4 us (15%)
  local copies, waits for them, and re-layouts  9.02 us (7%)
  other arithmetic  5.27 us (4%)
  Pallas kernels  3.73 us (3%)
    all_to_all x1, waiting for transfers between devices, local(): lax.all_to_all(filtered, 'seq', split_axis=1, concat_axis=0, tiled=True)  23.5 us
    all_to_all x1, blocking collectives, local(): gathered = lax.all_to_all(pieces, 'tensor', 0, 0, tiled=True)  19.4 us
    all_to_all x1, starting transfers between devices, local(): lax.all_to_all(kv_cols, 'seq', split_axis=0, concat_axis=1, tiled=True)  17.7 us
    all_to_all x1, waiting for transfers between devices, local(): lax.all_to_all(kv_cols, 'seq', split_axis=0, concat_axis=1, tiled=True)  16.7 us
    dot_general x12, matrix products, right_mul(): return jnp.einsum('ckn,nm->ckm', signal, matrix, precision=TRIPLE)  15.5 us
    ppermute x1, starting transfers between devices, passed_along(): return lax.ppermute(x, axis, pairs)  4.91 us
    all_to_all x1, starting transfers between devices, local(): lax.all_to_all(filtered, 'seq', split_axis=1, concat_axis=0, tiled=True)  4.18 us
    pallas_call x1, Pallas kernels, featurize_kv(): pl.pallas_call(_feat_body, grid=grid, in_specs=[pl.BlockSpec((3, rows, la...  3.73 us
  transfers between devices with their start and end apart: 3, of which 2 were waited for; matrix products, arithmetic and copies ran while one was open for 10% of the time, Pallas kernels for 0%

profile of v3, /device:TPU:1, one launch (start us, length us, event | category | flops | bytes accessed | tf_op | source)
XLA Modules:
  0.0 130.2 jit_solution(14166915435133415853)
XLA Ops:
  0.0 1.5 %slice.21 = bf16[3,6,512]{2,1,0:T(8,128)(2,1)} slice(bf16[3,256,512]{2,1,0:T(8,128)(2,1)} %proj_ref.1), slice={[0:3], [250:256], [0:512]} | slice | bytes 36864 | tf_op jit(solution)/shard_map/slice | solution.py:147
  1.5 4.9 %collective-permute-start = (bf16[3,6,512]{2,1,0:T(8,128)(2,1)}, bf16[3,6,512]{2,1,0:T(8,128)(2,1)}, u32[]{:S(2)}, u32[]{:S(2)}) collective-permute-start(bf16[3,6,512]{2,1,0:T(8,128)(2,1)} %slice.21), channel_id=1, source_target_pairs={{0,8},{8,16},{16,24},{24,32},{32,40},{40,48},{48,56},{56,64},{64,7... | collective-permute-start | bytes 55304 | tf_op jit(solution)/shard_map/ppermute | solution.py:20
  6.4 1.0 fusion.41
  7.4 1.0 fusion.42
  8.4 1.7 %convolution_negate_fusion.1 = f32[256,8,128]{2,0,1:T(8,128)S(1)} fusion(f32[8,128,128]{2,0,1:T(8,128)} %bitcast.100, f32[256,256]{1,0:T(8,128)S(1)} %fusion.41), kind=kOutput, calls=%fused_computation.9 | convolution fusion | flops 201588736 | bytes 1703936 | tf_op jit(solution)/shard_map/kn,cnb->ckb/dot_general | solution.py:58
  10.1 1.6 %fusion.23 = f32[256,8,128]{2,0,1:T(8,128)} fusion(f32[8,128,128]{2,0,1:T(8,128)S(1)} %bitcast.101, f32[256,256]{1,0:T(8,128)S(1)} %fusion.42), kind=kOutput, calls=%fused_computation.43 | convolution fusion | flops 201326592 | bytes 1703936 | tf_op jit(solution)/shard_map/kn,cnb->ckb/dot_general | solution.py:57
  11.7 0.5 fusion.63
  12.3 0.1 copy.88
  12.4 0.8 copy.90
  13.1 3.7 %shard_map.64 = (bf16[256,512]{1,0:T(8,128)(2,1)}, bf16[256,512]{1,0:T(8,128)(2,1)}) custom-call(bf16[3,256,512]{2,1,0:T(8,128)(2,1)} %proj_ref.1, bf16[3,6,512]{2,1,0:T(8,128)(2,1)} %collective-permute-done.prior_ref, f32[3,7,512]{2,1,0:T(8,128)} %w_ref.1), custom_call_target="tpu_custom_call" | custom-call | tf_op jit(solution)/shard_map/pallas_call | solution.py:117
  16.9 1.8 %copy.81 = bf16[512,256]{1,0:T(8,128)(2,1)} copy(bf16[512,256]{0,1:T(8,128)(2,1)} %bitcast.103) | data formatting | bytes 524288 | tf_op jit(solution)/shard_map/transpose | solution.py:149
  18.7 17.7 %all-to-all-start = ((bf16[64,8,256]{2,1,0:T(8,128)(2,1)}), bf16[64,8,256]{2,1,0:T(8,128)(2,1)}, u32[]{:S(2)}, u32[]{:S(2)}) async-start(bf16[64,8,256]{2,1,0:T(8,128)(2,1)} %bitcast.102), calls=%async_computation | async-start | bytes 524288 | tf_op jit(solution)/shard_map/all_to_all | solution.py:150
  36.4 0.0 copy-start.4
  36.4 2.2 %fusion.7 = f32[8,256,128]{2,1,0:T(8,128)S(1)} fusion(f32[256,8,128]{2,0,1:T(8,128)S(1)} %convolution_negate_fusion.1, f32[256,8,128]{2,0,1:T(8,128)} %fusion.23, f32[256,128]{1,0:T(8,128)} %copy.90, f32[256,128]{1,0:T(8,128)S(1)} %copy.88), kind=kOutput, calls=%fused_computation.18 | convolution fusion | flops 202342400 | bytes 3407872 | tf_op jit(solution)/shard_map/ckn,nm->ckm/dot_general | solution.py:50
  38.6 0.8 fusion.3
  39.5 1.9 %convolution_add_fusion.1 = f32[8,256,128]{2,1,0:T(8,128)} fusion(f32[8,256,128]{2,1,0:T(8,128)S(1)} %fusion.7, f32[256,8,128]{2,0,1:T(8,128)S(1)} %copy-done.1, f32[256,8,128]{2,0,1:T(8,128)S(1)} %convolution_negate_fusion.1, f32[256,128]{1,0:T(8,128)S(1)} %copy-done.4, f32[256,128]{1,0:T(8,128)S(1)} %copy.88), kind=kOutput, calls=%fused_computation.8 | convolution fusion | flops 202604544 | bytes 4456448 | tf_op jit(solution)/shard_map/ckn,nm->ckm/dot_general | solution.py:50
  41.3 1.8 %convolution_subtract_fusion.1 = f32[8,256,128]{2,1,0:T(8,128)} fusion(f32[8,256,128]{2,1,0:T(8,128)S(1)} %fusion.3, f32[256,8,128]{2,0,1:T(8,128)S(1)} %convolution_negate_fusion.1, f32[256,8,128]{2,0,1:T(8,128)S(1)} %copy-done.1, f32[256,128]{1,0:T(8,128)S(1)} %copy-done.4, f32[256,128]{1,0:T(8,128)S(1)} %copy.88), kind=kOutput, calls=%fused_computation.6 | convolution fusion | flops 202604544 | bytes 4456448 | tf_op jit(solution)/shard_map/ckn,nm->ckm/dot_general | solution.py:50
  43.2 16.7 %all-to-all-done = bf16[64,8,256]{2,1,0:T(8,128)(2,1)} async-done(((bf16[64,8,256]{2,1,0:T(8,128)(2,1)}), bf16[64,8,256]{2,1,0:T(8,128)(2,1)}, u32[]{:S(2)}, u32[]{:S(2)}) %all-to-all-start) | async-done | bytes 262176 | tf_op jit(solution)/shard_map/all_to_all | solution.py:150
  59.8 1.0 copy.82
  60.8 0.1 reshape.61
  60.9 1.4 %convolution_bitcast_fusion = f32[8,256,128]{1,2,0:T(8,128)S(1)} fusion(bf16[8,128,128]{2,1,0:T(8,128)(2,1)S(1)} %reshape.61, f32[256,256]{1,0:T(8,128)} %copy-done.8), kind=kOutput, calls=%fused_computation.3 | convolution fusion | flops 201326592 | bytes 1441792 | tf_op jit(solution)/shard_map/kn,cnb->ckb/dot_general | solution.py:57
  62.3 0.5 fusion
  62.8 1.2 fusion.34
  64.1 1.2 fusion.35
  65.3 1.3 convolution_add_fusion.2
  66.6 0.3 copy-done.3
  66.9 1.4 %multiply_subtract_fusion = (f32[8,256,128]{2,1,0:T(8,128)S(1)}, f32[8,256,128]{2,1,0:T(8,128)S(1)}) fusion(f32[8,256,128]{2,1,0:T(8,128)S(1)} %copy-done.3, f32[8,256,128]{2,1,0:T(8,128)S(1)} %convolution_add_fusion.2, f32[8,256,128]{2,1,0:T(8,128)S(1)} %copy-done.2, f32[8,256,128]{2,1,0:T(8,128)S(1)} %fusion.35, f32[8,256,128]{1,2,0:T(8,128)S(1)} %fusion, ...), kind=kOutput, calls=%fused_computation.28 | convolution fusion | flops 204177408 | bytes 8650752 | tf_op jit(solution)/shard_map/ckn,nm->ckm/dot_general | solution.py:50
  68.3 0.8 fusion.55
  69.1 0.8 fusion.53
  70.0 1.1 convolution_subtract_fusion
  71.1 0.9 convolution_add_fusion
  72.0 0.1 copy-done.9
  72.0 0.6 fusion.12
  72.7 0.0 copy-start.11
  72.7 0.6 fusion.2
  73.3 0.0 copy-start.10
  73.4 0.2 copy.97
  73.6 0.1 mul.328
  73.7 2.0 %fusion.17 = bf16[8,64,256]{2,0,1:T(8,128)(2,1)} fusion(f32[8,64,256]{2,1,0:T(8,128)S(1)} %mul.328, f32[8]{0:T(128)S(1)} %copy-done.11, bf16[64,8,256]{2,1,0:T(8,128)(2,1)} %all-to-all-done), kind=kLoop, calls=%fused_computation.36 | loop fusion | flops 524288 | bytes 1048608 | tf_op jit(solution)/shard_map/convert_element_type | solution.py:86
  75.7 4.2 %all-to-all-start.1 = ((bf16[8,64,256]{2,0,1:T(8,128)(2,1)}), bf16[8,64,256]{2,0,1:T(8,128)(2,1)S(1)}, u32[]{:S(2)}, u32[]{:S(2)}) async-start(bf16[8,64,256]{2,0,1:T(8,128)(2,1)} %fusion.17), calls=%async_computation.1 | async-start | bytes 524288 | tf_op jit(solution)/shard_map/all_to_all | solution.py:152
  79.9 0.1 broadcast_bitcast_fusion
  80.0 23.5 %all-to-all-done.1 = bf16[8,64,256]{2,0,1:T(8,128)(2,1)S(1)} async-done(((bf16[8,64,256]{2,0,1:T(8,128)(2,1)}), bf16[8,64,256]{2,0,1:T(8,128)(2,1)S(1)}, u32[]{:S(2)}, u32[]{:S(2)}) %all-to-all-start.1) | async-done | bytes 262176 | tf_op jit(solution)/shard_map/all_to_all | solution.py:152
  103.5 0.2 copy.99
  103.7 3.4 %multiply_reduce_fusion = bf16[256,2048]{1,0:T(8,128)(2,1)} fusion(bf16[4,128,2048]{2,1,0:T(8,128)(2,1)S(1)} %bitcast.98, f32[4,2048]{1,0:T(4,128)S(1)} %bitcast.104, f32[512,256]{0,1:T(8,128)S(1)} %copy.99, bf16[256,512]{1,0:T(8,128)(2,1)} %get-tuple-element.7), kind=kOutput, calls=%fused_computation | convolution fusion | flops 540934144 | bytes 3964928 | tf_op jit(solution)/shard_map/tbk,bkn->btn/dot_general | solution.py:159
  107.2 1.5 %copy.101 = bf16[256,2048]{0,1:T(8,128)(2,1)S(1)} copy(bf16[256,2048]{1,0:T(8,128)(2,1)} %multiply_reduce_fusion) | data formatting | bytes 2097152 | tf_op jit(solution)/shard_map/convert_element_type | solution.py:162
  108.6 1.3 %copy.102 = bf16[8,256,256]{2,1,0:T(8,128)(2,1)} copy(bf16[8,256,256]{1,2,0:T(8,128)(2,1)S(1)} %bitcast.99) | data formatting | bytes 2097152 | tf_op jit(solution)/shard_map/transpose | solution.py:164
  110.0 19.4 %all_to_all.31 = bf16[8,256,256]{2,1,0:T(8,128)(2,1)S(1)} all-to-all(bf16[8,256,256]{2,1,0:T(8,128)(2,1)} %copy.102), channel_id=1, replica_groups=mesh['seq'=64,'tensor'=8] {'tensor'}, dimensions={0} | all-to-all | bytes 2097152 | tf_op jit(solution)/shard_map/all_to_all | solution.py:165
  129.4 0.8 reduce_sum.22
  (22 shorter events, 0.1 us)
Async XLA Ops:
  0.0 103.7 %copy-start = (bf16[512,2048]{1,0:T(8,128)(2,1)S(1)}, bf16[512,2048]{1,0:T(8,128)(2,1)}, u32[]{:S(2)}) copy-start(bf16[512,2048]{1,0:T(8,128)(2,1)} %param.10) | copy-start | bytes 6291460
  0.0 10.1 %copy-start.5 = (f32[8,16384]{1,0:T(8,128)S(1)}, f32[8,16384]{1,0:T(8,128)}, u32[]{:S(2)}) copy-start(f32[8,16384]{1,0:T(8,128)} %param.8) | copy-start | bytes 1572868
  1.5 11.6 %collective-permute-start = (bf16[3,6,512]{2,1,0:T(8,128)(2,1)}, bf16[3,6,512]{2,1,0:T(8,128)(2,1)}, u32[]{:S(2)}, u32[]{:S(2)}) collective-permute-start(bf16[3,6,512]{2,1,0:T(8,128)(2,1)} %slice.21), channel_id=1, source_target_pairs={{0,8},{8,16},{16,24},{24,32},{32,40},{40,48},{48,56},{56,64},{64,7... | collective-permute-start | bytes 55304 | tf_op jit(solution)/shard_map/ppermute | solution.py:20
  7.4 2.7 %copy-start.6 = (f32[256,256]{1,0:T(8,128)}, f32[256,256]{1,0:T(8,128)S(1)}, u32[]{:S(2)}) copy-start(f32[256,256]{1,0:T(8,128)S(1)} %fusion.41) | copy-start | bytes 786436
  8.4 3.9 %copy-start.8 = (f32[256,256]{1,0:T(8,128)}, f32[256,256]{1,0:T(8,128)S(1)}, u32[]{:S(2)}) copy-start(f32[256,256]{1,0:T(8,128)S(1)} %fusion.42) | copy-start | bytes 786436
  18.7 41.2 %all-to-all-start = ((bf16[64,8,256]{2,1,0:T(8,128)(2,1)}), bf16[64,8,256]{2,1,0:T(8,128)(2,1)}, u32[]{:S(2)}, u32[]{:S(2)}) async-start(bf16[64,8,256]{2,1,0:T(8,128)(2,1)} %bitcast.102), calls=%async_computation | async-start | bytes 524288 | tf_op jit(solution)/shard_map/all_to_all | solution.py:150
  36.4 2.3 %copy-start.1 = (f32[256,8,128]{2,0,1:T(8,128)S(1)}, f32[256,8,128]{2,0,1:T(8,128)}, u32[]{:S(2)}) copy-start(f32[256,8,128]{2,0,1:T(8,128)} %fusion.23) | copy-start | bytes 3145732
  36.4 2.3 %copy-start.4 = (f32[256,128]{1,0:T(8,128)S(1)}, f32[256,128]{1,0:T(8,128)}, u32[]{:S(2)}) copy-start(f32[256,128]{1,0:T(8,128)} %copy.90) | copy-start | bytes 393220
  43.2 19.2 %copy-start.7 = (f32[256,256]{1,0:T(8,128)S(1)}, f32[256,256]{1,0:T(8,128)}, u32[]{:S(2)}) copy-start(f32[256,256]{1,0:T(8,128)} %copy-done.6) | copy-start | bytes 786436
  65.3 1.3 copy-start.2
  65.3 1.5 %copy-start.3 = (f32[8,256,128]{2,1,0:T(8,128)S(1)}, f32[8,256,128]{2,1,0:T(8,128)}, u32[]{:S(2)}) copy-start(f32[8,256,128]{2,1,0:T(8,128)} %convolution_subtract_fusion.1) | copy-start | bytes 3145732
  71.1 1.0 copy-start.9
  72.7 1.0 copy-start.11
  73.3 6.5 %copy-start.10 = (f32[4,16]{1,0:T(4,128)S(1)}, f32[4,16]{1,0:T(4,128)}, u32[]{:S(2)}) copy-start(f32[4,16]{1,0:T(4,128)} %param.11) | copy-start | bytes 772
  75.7 27.8 %all-to-all-start.1 = ((bf16[8,64,256]{2,0,1:T(8,128)(2,1)}), bf16[8,64,256]{2,0,1:T(8,128)(2,1)S(1)}, u32[]{:S(2)}, u32[]{:S(2)}) async-start(bf16[8,64,256]{2,0,1:T(8,128)(2,1)} %fusion.17), calls=%async_computation.1 | async-start | bytes 524288 | tf_op jit(solution)/shard_map/all_to_all | solution.py:152

commit v4 on v3

--- a/solution.py
+++ b/solution.py
@@ -132,6 +132,102 @@
     )(projected, prior, weights)
 
 
+def _split(a):
+    hi = a.astype(jnp.bfloat16)
+    return hi, (a - hi.astype(jnp.float32)).astype(jnp.bfloat16)
+
+
+def _mm(a, b):
+    return jnp.dot(a, b, preferred_element_type=jnp.float32)
+
+
+def _left3(t_hi, t_lo, v):
+    v_hi, v_lo = _split(v)
+    return _mm(t_hi, v_hi) + _mm(t_lo, v_hi) + _mm(t_hi, v_lo)
+
+
+def _right3(v, t_hi, t_lo):
+    v_hi, v_lo = _split(v)
+    return _mm(v_hi, t_hi) + _mm(v_lo, t_hi) + _mm(v_hi, t_lo)
+
+
+def _conv_body(x_ref, h_ref, g_ref, ca_h, ca_l, sa_h, sa_l, cb_h, cb_l, sb_h, sb_l,
+               ct_ref, st_ref, inv_h, inv_l, o_ref):
+    rows = ct_ref.shape[0]
+    ct = ct_ref[...]
+    st = st_ref[...]
+
+    def spectrum(a_re, a_im):
+        t_re = a_re * ct + a_im * st
+        t_im = a_im * ct - a_re * st
+        stacked = jnp.concatenate([t_re, t_im], axis=0)
+        r_c = _right3(stacked, cb_h[...], cb_l[...])
+        r_s = _right3(stacked, sb_h[...], sb_l[...])
+        return r_c[:rows] + r_s[rows:], r_c[rows:] - r_s[:rows]
+
+    for c in range(x_ref.shape[0]):
+        h = h_ref[c]
+        fh_re, fh_im = spectrum(_left3(ca_h[...], ca_l[...], h), -_left3(sa_h[...], sa_l[...], h))
+        x_b = x_ref[c]
+        a_re = _mm(ca_h[...], x_b) + _mm(ca_l[...], x_b)
+        a_im = -(_mm(sa_h[...], x_b) + _mm(sa_l[...], x_b))
+        fx_re, fx_im = spectrum(a_re, a_im)
+        p_re = fx_re * fh_re - fx_im * fh_im
+        p_im = fx_re * fh_im + fx_im * fh_re
+        stacked = jnp.concatenate([p_re, p_im], axis=0)
+        q_c = _right3(stacked, cb_h[...], cb_l[...])
+        q_s = _right3(stacked, sb_h[...], sb_l[...])
+        z_re = q_c[:rows] - q_s[rows:]
+        z_im = q_c[rows:] + q_s[:rows]
+        w_re = z_re * ct - z_im * st
+        w_im = z_im * ct + z_re * st
+        out = _left3(inv_h[...], inv_l[...], jnp.concatenate([w_re, w_im], axis=0))
+        x_f = x_b.astype(jnp.float32)
+        o_ref[c] = (out * (1.0 / (rows * ct_ref.shape[1])) + g_ref[c] * x_f).astype(jnp.bfloat16)
+
+
+def conv_tables(size_a, size_b):
+    whole = size_a * size_b
+    half_a = size_a // 2
+
+    def pair(r, c, period):
+        ri = lax.broadcasted_iota(jnp.int32, (r, c), 0)
+        ci = lax.broadcasted_iota(jnp.int32, (r, c), 1)
+        ang = (ri * ci % period).astype(jnp.float32) * (2.0 * math.pi / period)
+        return jnp.cos(ang), jnp.sin(ang)
+
+    cos_a, sin_a = pair(size_a, half_a, size_a)
+    cos_b, sin_b = pair(size_b, size_b, size_b)
+    cos_t, sin_t = pair(size_a, size_b, whole)
+    inv = jnp.concatenate([cos_a.T, -sin_a.T], axis=1)
+    return (*_split(cos_a), *_split(sin_a), *_split(cos_b), *_split(sin_b), cos_t, sin_t, *_split(inv))
+
+
+def long_conv(kv, filt, gain, ch_block=2, interpret=False):
+    ch, length = kv.shape
+    size_b = 128
+    half_a = length // size_b
+    size_a = 2 * half_a
+    x = kv.reshape(ch, half_a, size_b)
+    h = filt.reshape(ch, half_a, size_b)
+    g = jnp.broadcast_to(gain[:, None, None], (ch, 1, size_b))
+    tabs = conv_tables(size_a, size_b)
+    full = lambda t: pl.BlockSpec(t.shape, lambda i: (0,) * t.ndim)
+    out = pl.pallas_call(
+        _conv_body,
+        grid=(ch // ch_block,),
+        in_specs=[
+            pl.BlockSpec((ch_block, half_a, size_b), lambda i: (i, 0, 0)),
+            pl.BlockSpec((ch_block, half_a, size_b), lambda i: (i, 0, 0)),
+            pl.BlockSpec((ch_block, 1, size_b), lambda i: (i, 0, 0)),
+        ] + [full(t) for t in tabs],
+        out_specs=pl.BlockSpec((ch_block, half_a, size_b), lambda i: (i, 0, 0)),
+        out_shape=jax.ShapeDtypeStruct((ch, half_a, size_b), jnp.bfloat16),
+        interpret=interpret,
+    )(x, h, g, *tabs)
+    return out.reshape(ch, length)
+
+
 def multiply_round(left_arr, right_arr):
     return (left_arr.astype(jnp.float32) * right_arr.astype(jnp.float32)).astype(jnp.bfloat16)
 
@@ -141,14 +237,12 @@
     tok_rows = projected.shape[1]
     local_ch = projected.shape[2]
     length = tok_rows * groups
-    tables = make_tables(length)
-    spectrum = forward(long_filter, tables)
     rim_width = KS - 1
     prior_rows = passed_along(projected[:, tok_rows - rim_width :, :], "seq", 1)
     q_feat, gated_kv = featurize_kv(projected, prior_rows, feat_weight)
     kv_cols = jnp.transpose(gated_kv, (1, 0))
     kv_owned = lax.all_to_all(kv_cols, "seq", split_axis=0, concat_axis=1, tiled=True)
-    filtered = long_mix(kv_owned, spectrum, skip_gain, tables)
+    filtered = long_conv(kv_owned, long_filter, skip_gain)
     filtered_home = lax.all_to_all(filtered, "seq", split_axis=1, concat_axis=0, tiled=True)
     gated = multiply_round(q_feat, jnp.transpose(filtered_home, (1, 0)))
     block_count = local_ch // BLK

time: 131 us -> 129 us (0.985)
  matrix products: 25.4 us -> 2.31 us
  Pallas kernels: 3.73 us -> 18.7 us
  other arithmetic: 5.27 us -> 8.18 us
  waiting for transfers between devices: 40.1 us -> 42.8 us
  local copies, waits for them, and re-layouts: 9.02 us -> 10.8 us
    dot_general x18 -> x0, matrix products: 22 us -> none  [the longest x12 15.5 us: right_mul(): return jnp.einsum('ckn,nm->ckm', signal, matrix, precision=TRIPLE)]
    pallas_call x0 -> x1, Pallas kernels: none -> 15 us  [long_conv(): pl.pallas_call(_conv_body, grid=(ch // ch_block,), in_specs=[pl.BlockSpec...]
    ppermute x1, waiting for transfers between devices: 0.01 us -> 3.87 us  [passed_along(): return lax.ppermute(x, axis, pairs)]
    convert_element_type x1 -> x6, other arithmetic: 1.96 us -> 5.58 us  [the longest x3 2.79 us: _split(): return (hi, (a - hi.astype(jnp.float32)).astype(jnp.bfloat16))]
    all_to_all x0 -> x2, local copies, waits for them, and re-layouts: none -> 1.94 us  [local(): lax.all_to_all(filtered, 'seq', split_axis=1, concat_axis=0, tiled=True)]
  transfers between devices with their start and end apart: 3 -> 3, of which waited for: 2 -> 3; matrix products, arithmetic and copies ran while one was open for 10% -> 6% of each run, Pallas kernels for 0% -> 0%
where the time goes in v4:
time: 129 us
  waiting for transfers between devices  42.8 us (33%)
  starting transfers between devices  26.4 us (20%)
  blocking collectives  19.4 us (15%)
  Pallas kernels  18.7 us (14%)
  local copies, waits for them, and re-layouts  10.8 us (8%)
  other arithmetic  8.18 us (6%)
  matrix products  2.31 us (2%)
    all_to_all x1, waiting for transfers between devices, local(): lax.all_to_all(filtered, 'seq', split_axis=1, concat_axis=0, tiled=True)  23.5 us
    all_to_all x1, blocking collectives, local(): gathered = lax.all_to_all(pieces, 'tensor', 0, 0, tiled=True)  19.4 us
    all_to_all x1, starting transfers between devices, local(): lax.all_to_all(kv_cols, 'seq', split_axis=0, concat_axis=1, tiled=True)  17.3 us
    all_to_all x1, waiting for transfers between devices, local(): lax.all_to_all(kv_cols, 'seq', split_axis=0, concat_axis=1, tiled=True)  15.5 us
    pallas_call x1, Pallas kernels, long_conv(): pl.pallas_call(_conv_body, grid=(ch // ch_block,), in_specs=[pl.BlockSpec...  15 us
    ppermute x1, starting transfers between devices, passed_along(): return lax.ppermute(x, axis, pairs)  4.92 us
    all_to_all x1, starting transfers between devices, local(): lax.all_to_all(filtered, 'seq', split_axis=1, concat_axis=0, tiled=True)  4.18 us
    ppermute x1, waiting for transfers between devices, passed_along(): return lax.ppermute(x, axis, pairs)  3.87 us
  transfers between devices with their start and end apart: 3, of which 3 were waited for; matrix products, arithmetic and copies ran while one was open for 6% of the time, Pallas kernels for 0%

profile of v4, /device:TPU:1, one launch (start us, length us, event | category | flops | bytes accessed | tf_op | source)
XLA Modules:
  0.0 128.7 jit_solution(2323082747824286705)
XLA Ops:
  0.0 0.0 copy-start
  0.0 0.0 copy-start.1
  0.0 0.9 slice.3
  0.9 4.9 %collective-permute-start = (bf16[3,6,512]{2,1,0:T(8,128)(2,1)S(1)}, bf16[3,6,512]{2,1,0:T(8,128)(2,1)S(1)}, u32[]{:S(2)}, u32[]{:S(2)}) collective-permute-start(bf16[3,6,512]{2,1,0:T(8,128)(2,1)S(1)} %slice.3), channel_id=1, source_target_pairs={{0,8},{8,16},{16,24},{24,32},{32,40},{40,48},{48,56},{56,64},{64,7... | collective-permute-start | bytes 55304 | tf_op jit(solution)/shard_map/ppermute | solution.py:20
  5.8 3.9 %collective-permute-done.prior_ref = bf16[3,6,512]{2,1,0:T(8,128)(2,1)S(1)} collective-permute-done((bf16[3,6,512]{2,1,0:T(8,128)(2,1)S(1)}, bf16[3,6,512]{2,1,0:T(8,128)(2,1)S(1)}, u32[]{:S(2)}, u32[]{:S(2)}) %collective-permute-start) | collective-permute-done | bytes 18464 | tf_op jit(solution)/shard_map/ppermute | solution.py:20
  9.7 0.0 copy-start.2
  9.7 0.6 copy-done.2
  10.3 3.7 %shard_map.64 = (bf16[256,512]{1,0:T(8,128)(2,1)}, bf16[256,512]{1,0:T(8,128)(2,1)}) custom-call(bf16[3,256,512]{2,1,0:T(8,128)(2,1)} %proj_ref.1, bf16[3,6,512]{2,1,0:T(8,128)(2,1)} %copy-done.2, f32[3,7,512]{2,1,0:T(8,128)} %w_ref.1), custom_call_target="tpu_custom_call" | custom-call | tf_op jit(solution)/shard_map/pallas_call | solution.py:117
  14.0 1.8 %copy.26 = bf16[512,256]{1,0:T(8,128)(2,1)} copy(bf16[512,256]{0,1:T(8,128)(2,1)} %bitcast.41) | data formatting | bytes 524288 | tf_op jit(solution)/shard_map/transpose | solution.py:243
  15.8 0.0 copy-start.4
  15.8 17.3 %all-to-all-start = ((bf16[64,8,256]{2,1,0:T(8,128)(2,1)}), bf16[64,8,256]{2,1,0:T(8,128)(2,1)S(1)}, u32[]{:S(2)}, u32[]{:S(2)}) async-start(bf16[64,8,256]{2,1,0:T(8,128)(2,1)} %bitcast.1), calls=%async_computation | async-start | bytes 524288 | tf_op jit(solution)/shard_map/all_to_all | solution.py:244
  33.1 0.0 copy-done.1
  33.1 0.9 copy.42
  34.0 0.9 subtract_convert_fusion.3
  34.9 0.9 fusion.37
  35.8 0.5 sine_negate_fusion
  36.4 0.7 fusion.4.inv_h
  37.0 0.7 subtract_convert_fusion.inv_l
  37.7 1.2 subtract_convert_fusion.1
  38.9 1.2 fusion.32
  40.1 1.2 fusion.28
  41.4 15.5 %all-to-all-done = bf16[64,8,256]{2,1,0:T(8,128)(2,1)S(1)} async-done(((bf16[64,8,256]{2,1,0:T(8,128)(2,1)}), bf16[64,8,256]{2,1,0:T(8,128)(2,1)S(1)}, u32[]{:S(2)}, u32[]{:S(2)}) %all-to-all-start) | async-done | bytes 262176 | tf_op jit(solution)/shard_map/all_to_all | solution.py:244
  56.9 0.0 copy-start.3
  56.9 0.8 reshape.30.x_ref
  57.7 0.0 copy-done.4
  57.7 0.7 broadcast_in_dim.4.g_ref
  58.4 15.0 %shard_map.65 = bf16[8,128,128]{2,1,0:T(8,128)(2,1)} custom-call(bf16[8,128,128]{2,1,0:T(8,128)(2,1)} %reshape.30.x_ref, f32[8,128,128]{2,1,0:T(8,128)} %bitcast.38, f32[8,1,128]{2,1,0:T(1,128)} %broadcast_in_dim.4.g_ref, bf16[256,128]{1,0:T(8,128)(2,1)} %get-tuple-element.17.ca_h, bf16[256,128]{1,0:T(8,128)(2,1)} %get-tuple-element.12.ca_l, ...), custom_call_target="tpu_custom_call" | custom-call | tf_op jit(solution)/shard_map/pallas_call | solution.py:216
  73.4 0.0 copy-start.5
  73.4 1.1 all_to_all.28
  74.5 0.9 copy.28
  75.4 4.2 %all-to-all-start.1 = ((bf16[8,64,256]{2,0,1:T(8,128)(2,1)}), bf16[8,64,256]{2,0,1:T(8,128)(2,1)S(1)}, u32[]{:S(2)}, u32[]{:S(2)}) async-start(bf16[8,64,256]{2,0,1:T(8,128)(2,1)} %copy.28), calls=%async_computation.1 | async-start | bytes 524288 | tf_op jit(solution)/shard_map/all_to_all | solution.py:246
  79.6 0.0 copy-done.3
  79.6 0.1 broadcast_bitcast_fusion
  79.7 23.5 %all-to-all-done.1 = bf16[8,64,256]{2,0,1:T(8,128)(2,1)S(1)} async-done(((bf16[8,64,256]{2,0,1:T(8,128)(2,1)}), bf16[8,64,256]{2,0,1:T(8,128)(2,1)S(1)}, u32[]{:S(2)}, u32[]{:S(2)}) %all-to-all-start.1) | async-done | bytes 262176 | tf_op jit(solution)/shard_map/all_to_all | solution.py:246
  103.2 0.2 copy.29
  103.4 0.0 copy-done
  103.4 0.0 copy-done.5
  103.4 2.3 %multiply_reduce_fusion = bf16[256,2048]{1,0:T(8,128)(2,1)} fusion(bf16[4,128,2048]{2,1,0:T(8,128)(2,1)S(1)} %bitcast.36, f32[4,2048]{1,0:T(4,128)S(1)} %bitcast.42, f32[512,256]{0,1:T(8,128)S(1)} %copy.29, bf16[256,512]{1,0:T(8,128)(2,1)S(1)} %copy-done.5), kind=kOutput, calls=%fused_computation | convolution fusion | flops 540934144 | bytes 3964928 | tf_op jit(solution)/shard_map/tbk,bkn->btn/dot_general | solution.py:253
  105.7 1.5 %copy.31 = bf16[256,2048]{0,1:T(8,128)(2,1)S(1)} copy(bf16[256,2048]{1,0:T(8,128)(2,1)} %multiply_reduce_fusion) | data formatting | bytes 2097152 | tf_op jit(solution)/shard_map/convert_element_type | solution.py:256
  107.2 1.3 %copy.32 = bf16[8,256,256]{2,1,0:T(8,128)(2,1)} copy(bf16[8,256,256]{1,2,0:T(8,128)(2,1)S(1)} %bitcast.37) | data formatting | bytes 2097152 | tf_op jit(solution)/shard_map/transpose | solution.py:258
  108.5 19.4 %all_to_all.34 = bf16[8,256,256]{2,1,0:T(8,128)(2,1)S(1)} all-to-all(bf16[8,256,256]{2,1,0:T(8,128)(2,1)} %copy.32), channel_id=1, replica_groups=mesh['seq'=64,'tensor'=8] {'tensor'}, dimensions={0} | all-to-all | bytes 2097152 | tf_op jit(solution)/shard_map/all_to_all | solution.py:259
  127.9 0.8 reduce_sum.22
  (3 shorter events, 0.1 us)
Async XLA Ops:
  0.0 103.4 %copy-start = (bf16[512,2048]{1,0:T(8,128)(2,1)S(1)}, bf16[512,2048]{1,0:T(8,128)(2,1)}, u32[]{:S(2)}) copy-start(bf16[512,2048]{1,0:T(8,128)(2,1)} %param.10) | copy-start | bytes 6291460
  0.0 33.1 %copy-start.1 = (f32[8,16384]{1,0:T(8,128)S(1)}, f32[8,16384]{1,0:T(8,128)}, u32[]{:S(2)}) copy-start(f32[8,16384]{1,0:T(8,128)} %param.8) | copy-start | bytes 1572868
  0.9 8.8 %collective-permute-start = (bf16[3,6,512]{2,1,0:T(8,128)(2,1)S(1)}, bf16[3,6,512]{2,1,0:T(8,128)(2,1)S(1)}, u32[]{:S(2)}, u32[]{:S(2)}) collective-permute-start(bf16[3,6,512]{2,1,0:T(8,128)(2,1)S(1)} %slice.3), channel_id=1, source_target_pairs={{0,8},{8,16},{16,24},{24,32},{32,40},{40,48},{48,56},{56,64},{64,7... | collective-permute-start | bytes 55304 | tf_op jit(solution)/shard_map/ppermute | solution.py:20
  9.7 0.6 copy-start.2
  15.8 41.9 %copy-start.4 = (f32[8]{0:T(128)S(1)}, f32[8]{0:T(128)}, u32[]{:S(2)}) copy-start(f32[8]{0:T(128)} %param.9) | copy-start | bytes 100
  15.8 41.0 %all-to-all-start = ((bf16[64,8,256]{2,1,0:T(8,128)(2,1)}), bf16[64,8,256]{2,1,0:T(8,128)(2,1)S(1)}, u32[]{:S(2)}, u32[]{:S(2)}) async-start(bf16[64,8,256]{2,1,0:T(8,128)(2,1)} %bitcast.1), calls=%async_computation | async-start | bytes 524288 | tf_op jit(solution)/shard_map/all_to_all | solution.py:244
  56.9 22.7 %copy-start.3 = (f32[4,16]{1,0:T(4,128)S(1)}, f32[4,16]{1,0:T(4,128)}, u32[]{:S(2)}) copy-start(f32[4,16]{1,0:T(4,128)} %param.11) | copy-start | bytes 772
  73.4 30.0 %copy-start.5 = (bf16[256,512]{1,0:T(8,128)(2,1)S(1)}, bf16[256,512]{1,0:T(8,128)(2,1)}, u32[]{:S(2)}) copy-start(bf16[256,512]{1,0:T(8,128)(2,1)} %get-tuple-element.7) | copy-start | bytes 786436
  75.4 27.8 %all-to-all-start.1 = ((bf16[8,64,256]{2,0,1:T(8,128)(2,1)}), bf16[8,64,256]{2,0,1:T(8,128)(2,1)S(1)}, u32[]{:S(2)}, u32[]{:S(2)}) async-start(bf16[8,64,256]{2,0,1:T(8,128)(2,1)} %copy.28), calls=%async_computation.1 | async-start | bytes 524288 | tf_op jit(solution)/shard_map/all_to_all | solution.py:246

commit v5 on v4

--- a/solution.py
+++ b/solution.py
@@ -151,27 +151,38 @@
     return _mm(v_hi, t_hi) + _mm(v_lo, t_hi) + _mm(v_hi, t_lo)
 
 
-def _conv_body(x_ref, h_ref, g_ref, ca_h, ca_l, sa_h, sa_l, cb_h, cb_l, sb_h, sb_l,
+def _spectrum(a_re, a_im, ct, st, cb_h, cb_l, sb_h, sb_l):
+    rows = ct.shape[0]
+    t_re = a_re * ct + a_im * st
+    t_im = a_im * ct - a_re * st
+    stacked = jnp.concatenate([t_re, t_im], axis=0)
+    r_c = _right3(stacked, cb_h, cb_l)
+    r_s = _right3(stacked, sb_h, sb_l)
+    return r_c[:rows] + r_s[rows:], r_c[rows:] - r_s[:rows]
+
+
+def _filter_body(h_ref, ca_h, ca_l, sa_h, sa_l, cb_h, cb_l, sb_h, sb_l, ct_ref, st_ref, re_ref, im_ref):
+    ct = ct_ref[...]
+    st = st_ref[...]
+    for c in range(h_ref.shape[0]):
+        h = h_ref[c]
+        a_re = _left3(ca_h[...], ca_l[...], h)
+        a_im = -_left3(sa_h[...], sa_l[...], h)
+        re_ref[c], im_ref[c] = _spectrum(a_re, a_im, ct, st, cb_h[...], cb_l[...], sb_h[...], sb_l[...])
+
+
+def _conv_body(x_ref, fh_re_ref, fh_im_ref, g_ref, ca_h, ca_l, sa_h, sa_l, cb_h, cb_l, sb_h, sb_l,
                ct_ref, st_ref, inv_h, inv_l, o_ref):
     rows = ct_ref.shape[0]
     ct = ct_ref[...]
     st = st_ref[...]
-
-    def spectrum(a_re, a_im):
-        t_re = a_re * ct + a_im * st
-        t_im = a_im * ct - a_re * st
-        stacked = jnp.concatenate([t_re, t_im], axis=0)
-        r_c = _right3(stacked, cb_h[...], cb_l[...])
-        r_s = _right3(stacked, sb_h[...], sb_l[...])
-        return r_c[:rows] + r_s[rows:], r_c[rows:] - r_s[:rows]
-
     for c in range(x_ref.shape[0]):
-        h = h_ref[c]
-        fh_re, fh_im = spectrum(_left3(ca_h[...], ca_l[...], h), -_left3(sa_h[...], sa_l[...], h))
         x_b = x_ref[c]
         a_re = _mm(ca_h[...], x_b) + _mm(ca_l[...], x_b)
         a_im = -(_mm(sa_h[...], x_b) + _mm(sa_l[...], x_b))
-        fx_re, fx_im = spectrum(a_re, a_im)
+        fx_re, fx_im = _spectrum(a_re, a_im, ct, st, cb_h[...], cb_l[...], sb_h[...], sb_l[...])
+        fh_re = fh_re_ref[c]
+        fh_im = fh_im_ref[c]
         p_re = fx_re * fh_re - fx_im * fh_im
         p_im = fx_re * fh_im + fx_im * fh_re
         stacked = jnp.concatenate([p_re, p_im], axis=0)
@@ -203,28 +214,45 @@
     return (*_split(cos_a), *_split(sin_a), *_split(cos_b), *_split(sin_b), cos_t, sin_t, *_split(inv))
 
 
-def long_conv(kv, filt, gain, ch_block=2, interpret=False):
+def filter_spectrum(filt, tabs, ch_block=2):
+    ch, length = filt.shape
+    size_b = 128
+    half_a = length // size_b
+    size_a = 2 * half_a
+    h = filt.reshape(ch, half_a, size_b)
+    full = lambda t: pl.BlockSpec(t.shape, lambda i: (0,) * t.ndim)
+    blk_out = pl.BlockSpec((ch_block, size_a, size_b), lambda i: (i, 0, 0))
+    return pl.pallas_call(
+        _filter_body,
+        grid=(ch // ch_block,),
+        in_specs=[pl.BlockSpec((ch_block, half_a, size_b), lambda i: (i, 0, 0))]
+        + [full(t) for t in tabs[:10]],
+        out_specs=[blk_out, blk_out],
+        out_shape=[jax.ShapeDtypeStruct((ch, size_a, size_b), jnp.float32)] * 2,
+    )(h, *tabs[:10])
+
+
+def long_conv(kv, spectrum, gain, tabs, ch_block=2):
     ch, length = kv.shape
     size_b = 128
     half_a = length // size_b
     size_a = 2 * half_a
     x = kv.reshape(ch, half_a, size_b)
-    h = filt.reshape(ch, half_a, size_b)
     g = jnp.broadcast_to(gain[:, None, None], (ch, 1, size_b))
-    tabs = conv_tables(size_a, size_b)
     full = lambda t: pl.BlockSpec(t.shape, lambda i: (0,) * t.ndim)
+    blk_spec = pl.BlockSpec((ch_block, size_a, size_b), lambda i: (i, 0, 0))
     out = pl.pallas_call(
         _conv_body,
         grid=(ch // ch_block,),
         in_specs=[
             pl.BlockSpec((ch_block, half_a, size_b), lambda i: (i, 0, 0)),
-            pl.BlockSpec((ch_block, half_a, size_b), lambda i: (i, 0, 0)),
+            blk_spec,
+            blk_spec,
             pl.BlockSpec((ch_block, 1, size_b), lambda i: (i, 0, 0)),
         ] + [full(t) for t in tabs],
         out_specs=pl.BlockSpec((ch_block, half_a, size_b), lambda i: (i, 0, 0)),
         out_shape=jax.ShapeDtypeStruct((ch, half_a, size_b), jnp.bfloat16),
-        interpret=interpret,
-    )(x, h, g, *tabs)
+    )(x, *spectrum, g, *tabs)
     return out.reshape(ch, length)
 
 
@@ -240,9 +268,11 @@
     rim_width = KS - 1
     prior_rows = passed_along(projected[:, tok_rows - rim_width :, :], "seq", 1)
     q_feat, gated_kv = featurize_kv(projected, prior_rows, feat_weight)
+    tabs = conv_tables(2 * length // 128, 128)
+    spectrum = filter_spectrum(long_filter, tabs)
     kv_cols = jnp.transpose(gated_kv, (1, 0))
     kv_owned = lax.all_to_all(kv_cols, "seq", split_axis=0, concat_axis=1, tiled=True)
-    filtered = long_conv(kv_owned, long_filter, skip_gain)
+    filtered = long_conv(kv_owned, spectrum, skip_gain, tabs)
     filtered_home = lax.all_to_all(filtered, "seq", split_axis=1, concat_axis=0, tiled=True)
     gated = multiply_round(q_feat, jnp.transpose(filtered_home, (1, 0)))
     block_count = local_ch // BLK

time: 129 us -> 129 us (level)
  waiting for transfers between devices: 42.8 us -> 37.2 us
  Pallas kernels: 18.7 us -> 23 us
    pallas_call x0 -> x1, Pallas kernels: none -> 5.83 us  [filter_spectrum(): pl.pallas_call(_filter_body, grid=(ch // ch_block,), in_specs=[pl.BlockSp...]
    all_to_all x1, waiting for transfers between devices: 15.5 us -> 9.73 us  [local(): lax.all_to_all(kv_cols, 'seq', split_axis=0, concat_axis=1, tiled=True)]
    pallas_call x1, Pallas kernels: 15 us -> 13.5 us  [long_conv(): pl.pallas_call(_conv_body, grid=(ch // ch_block,), in_specs=[pl.BlockSpec...]
  transfers between devices with their start and end apart: 3 -> 3, of which waited for: 3 -> 3; matrix products, arithmetic and copies ran while one was open for 6% -> 6% of each run, Pallas kernels for 0% -> 5%
where the time goes in v5:
time: 129 us
  waiting for transfers between devices  37.2 us (29%)
  starting transfers between devices  27.5 us (21%)
  Pallas kernels  23 us (18%)
  blocking collectives  19.4 us (15%)
  local copies, waits for them, and re-layouts  10.8 us (8%)
  other arithmetic  8.11 us (6%)
  matrix products  2.3 us (2%)
    all_to_all x1, waiting for transfers between devices, local(): lax.all_to_all(filtered, 'seq', split_axis=1, concat_axis=0, tiled=True)  23.6 us
    all_to_all x1, blocking collectives, local(): gathered = lax.all_to_all(pieces, 'tensor', 0, 0, tiled=True)  19.4 us
    all_to_all x1, starting transfers between devices, local(): lax.all_to_all(kv_cols, 'seq', split_axis=0, concat_axis=1, tiled=True)  17.2 us
    pallas_call x1, Pallas kernels, long_conv(): pl.pallas_call(_conv_body, grid=(ch // ch_block,), in_specs=[pl.BlockSpec...  13.5 us
    all_to_all x1, waiting for transfers between devices, local(): lax.all_to_all(kv_cols, 'seq', split_axis=0, concat_axis=1, tiled=True)  9.73 us
    pallas_call x1, Pallas kernels, filter_spectrum(): pl.pallas_call(_filter_body, grid=(ch // ch_block,), in_specs=[pl.BlockSp...  5.83 us
    all_to_all x1, starting transfers between devices, local(): lax.all_to_all(filtered, 'seq', split_axis=1, concat_axis=0, tiled=True)  5.45 us
    ppermute x1, starting transfers between devices, passed_along(): return lax.ppermute(x, axis, pairs)  4.92 us
  transfers between devices with their start and end apart: 3, of which 3 were waited for; matrix products, arithmetic and copies ran while one was open for 6% of the time, Pallas kernels for 5%

profile of v5, /device:TPU:1, one launch (start us, length us, event | category | flops | bytes accessed | tf_op | source)
XLA Modules:
  0.0 128.5 jit_solution(16624814420331730670)
XLA Ops:
  0.0 0.0 copy-start
  0.0 0.0 copy-start.1
  0.0 0.9 slice.3
  0.9 4.9 %collective-permute-start = (bf16[3,6,512]{2,1,0:T(8,128)(2,1)S(1)}, bf16[3,6,512]{2,1,0:T(8,128)(2,1)S(1)}, u32[]{:S(2)}, u32[]{:S(2)}) collective-permute-start(bf16[3,6,512]{2,1,0:T(8,128)(2,1)S(1)} %slice.3), channel_id=1, source_target_pairs={{0,8},{8,16},{16,24},{24,32},{32,40},{40,48},{48,56},{56,64},{64,7... | collective-permute-start | bytes 55304 | tf_op jit(solution)/shard_map/ppermute | solution.py:20
  5.8 3.9 %collective-permute-done.prior_ref = bf16[3,6,512]{2,1,0:T(8,128)(2,1)S(1)} collective-permute-done((bf16[3,6,512]{2,1,0:T(8,128)(2,1)S(1)}, bf16[3,6,512]{2,1,0:T(8,128)(2,1)S(1)}, u32[]{:S(2)}, u32[]{:S(2)}) %collective-permute-start) | collective-permute-done | bytes 18464 | tf_op jit(solution)/shard_map/ppermute | solution.py:20
  9.7 0.0 copy-start.2
  9.7 0.6 copy-done.2
  10.3 3.7 %shard_map.64 = (bf16[256,512]{1,0:T(8,128)(2,1)}, bf16[256,512]{1,0:T(8,128)(2,1)}) custom-call(bf16[3,256,512]{2,1,0:T(8,128)(2,1)} %proj_ref.1, bf16[3,6,512]{2,1,0:T(8,128)(2,1)} %copy-done.2, f32[3,7,512]{2,1,0:T(8,128)} %w_ref.1), custom_call_target="tpu_custom_call" | custom-call | tf_op jit(solution)/shard_map/pallas_call | solution.py:117
  14.0 1.8 %copy.26 = bf16[512,256]{1,0:T(8,128)(2,1)} copy(bf16[512,256]{0,1:T(8,128)(2,1)} %bitcast.41) | data formatting | bytes 524288 | tf_op jit(solution)/shard_map/transpose | solution.py:273
  15.8 17.2 %all-to-all-start = ((bf16[64,8,256]{2,1,0:T(8,128)(2,1)}), bf16[64,8,256]{2,1,0:T(8,128)(2,1)S(1)}, u32[]{:S(2)}, u32[]{:S(2)}) async-start(bf16[64,8,256]{2,1,0:T(8,128)(2,1)} %bitcast.1), calls=%async_computation | async-start | bytes 524288 | tf_op jit(solution)/shard_map/all_to_all | solution.py:274
  33.0 0.0 copy-done.1
  33.0 0.9 copy.42
  33.9 0.0 copy-start.4
  33.9 0.9 subtract_convert_fusion.3
  34.8 0.9 fusion.37
  35.7 1.2 subtract_convert_fusion.1
  36.9 1.2 fusion.32
  38.1 1.2 fusion.28
  39.3 5.8 %shard_map.65 = (f32[8,256,128]{2,1,0:T(8,128)}, f32[8,256,128]{2,1,0:T(8,128)}) custom-call(f32[8,128,128]{2,1,0:T(8,128)} %bitcast.38, bf16[256,128]{1,0:T(8,128)(2,1)} %get-tuple-element.19.ca_h, bf16[256,128]{1,0:T(8,128)(2,1)} %get-tuple-element.14.ca_l, bf16[256,128]{1,0:T(8,128)(2,1)} %get-tuple-element.20.sa_h, ...), custom_call_target="tpu_custom_call" | custom-call | tf_op jit(solution)/shard_map/pallas_call | solution.py:225
  45.1 0.5 sine_negate_fusion
  45.7 0.7 fusion.4.inv_h
  46.3 0.7 subtract_convert_fusion.inv_l
  47.0 9.7 %all-to-all-done = bf16[64,8,256]{2,1,0:T(8,128)(2,1)S(1)} async-done(((bf16[64,8,256]{2,1,0:T(8,128)(2,1)}), bf16[64,8,256]{2,1,0:T(8,128)(2,1)S(1)}, u32[]{:S(2)}, u32[]{:S(2)}) %all-to-all-start) | async-done | bytes 262176 | tf_op jit(solution)/shard_map/all_to_all | solution.py:274
  56.8 0.8 reshape.30.x_ref
  57.6 0.0 copy-done.4
  57.6 0.7 broadcast_in_dim.4.g_ref
  58.3 0.0 copy-start.3
  58.3 13.5 %shard_map.66 = bf16[8,128,128]{2,1,0:T(8,128)(2,1)} custom-call(bf16[8,128,128]{2,1,0:T(8,128)(2,1)} %reshape.30.x_ref, f32[8,256,128]{2,1,0:T(8,128)} %get-tuple-element.11.fh_re_ref, f32[8,256,128]{2,1,0:T(8,128)} %get-tuple-element.12.fh_im_ref, f32[8,1,128]{2,1,0:T(1,128)} %broadcast_in_dim.4.g_ref, bf16[256,128]{1,0:T(8,128)(2,1)} %get-tuple-element.19.ca_h, ...), custom_call_target="tpu_custom_call" | custom-call | tf_op jit(solution)/shard_map/pallas_call | solution.py:244
  71.8 0.0 copy-start.5
  71.8 1.1 all_to_all.28
  72.9 0.8 copy.28
  73.7 5.5 %all-to-all-start.1 = ((bf16[8,64,256]{2,0,1:T(8,128)(2,1)}), bf16[8,64,256]{2,0,1:T(8,128)(2,1)S(1)}, u32[]{:S(2)}, u32[]{:S(2)}) async-start(bf16[8,64,256]{2,0,1:T(8,128)(2,1)} %copy.28), calls=%async_computation.1 | async-start | bytes 524288 | tf_op jit(solution)/shard_map/all_to_all | solution.py:276
  79.2 0.0 copy-done.3
  79.2 0.1 broadcast_bitcast_fusion
  79.3 23.6 %all-to-all-done.1 = bf16[8,64,256]{2,0,1:T(8,128)(2,1)S(1)} async-done(((bf16[8,64,256]{2,0,1:T(8,128)(2,1)}), bf16[8,64,256]{2,0,1:T(8,128)(2,1)S(1)}, u32[]{:S(2)}, u32[]{:S(2)}) %all-to-all-start.1) | async-done | bytes 262176 | tf_op jit(solution)/shard_map/all_to_all | solution.py:276
  103.0 0.2 copy.29
  103.2 0.0 copy-done
  103.2 0.0 copy-done.5
  103.2 2.3 %multiply_reduce_fusion = bf16[256,2048]{1,0:T(8,128)(2,1)} fusion(bf16[4,128,2048]{2,1,0:T(8,128)(2,1)S(1)} %bitcast.36, f32[4,2048]{1,0:T(4,128)S(1)} %bitcast.42, f32[512,256]{0,1:T(8,128)S(1)} %copy.29, bf16[256,512]{1,0:T(8,128)(2,1)S(1)} %copy-done.5), kind=kOutput, calls=%fused_computation | convolution fusion | flops 540934144 | bytes 3964928 | tf_op jit(solution)/shard_map/tbk,bkn->btn/dot_general | solution.py:283
  105.5 1.5 %copy.31 = bf16[256,2048]{0,1:T(8,128)(2,1)S(1)} copy(bf16[256,2048]{1,0:T(8,128)(2,1)} %multiply_reduce_fusion) | data formatting | bytes 2097152 | tf_op jit(solution)/shard_map/convert_element_type | solution.py:286
  107.0 1.3 %copy.32 = bf16[8,256,256]{2,1,0:T(8,128)(2,1)} copy(bf16[8,256,256]{1,2,0:T(8,128)(2,1)S(1)} %bitcast.37) | data formatting | bytes 2097152 | tf_op jit(solution)/shard_map/transpose | solution.py:288
  108.3 19.4 %all_to_all.34 = bf16[8,256,256]{2,1,0:T(8,128)(2,1)S(1)} all-to-all(bf16[8,256,256]{2,1,0:T(8,128)(2,1)} %copy.32), channel_id=1, replica_groups=mesh['seq'=64,'tensor'=8] {'tensor'}, dimensions={0} | all-to-all | bytes 2097152 | tf_op jit(solution)/shard_map/all_to_all | solution.py:289
  127.7 0.8 reduce_sum.22
  (3 shorter events, 0.1 us)
Async XLA Ops:
  0.0 103.2 %copy-start = (bf16[512,2048]{1,0:T(8,128)(2,1)S(1)}, bf16[512,2048]{1,0:T(8,128)(2,1)}, u32[]{:S(2)}) copy-start(bf16[512,2048]{1,0:T(8,128)(2,1)} %param.10) | copy-start | bytes 6291460
  0.0 33.0 %copy-start.1 = (f32[8,16384]{1,0:T(8,128)S(1)}, f32[8,16384]{1,0:T(8,128)}, u32[]{:S(2)}) copy-start(f32[8,16384]{1,0:T(8,128)} %param.8) | copy-start | bytes 1572868
  0.9 8.8 %collective-permute-start = (bf16[3,6,512]{2,1,0:T(8,128)(2,1)S(1)}, bf16[3,6,512]{2,1,0:T(8,128)(2,1)S(1)}, u32[]{:S(2)}, u32[]{:S(2)}) collective-permute-start(bf16[3,6,512]{2,1,0:T(8,128)(2,1)S(1)} %slice.3), channel_id=1, source_target_pairs={{0,8},{8,16},{16,24},{24,32},{32,40},{40,48},{48,56},{56,64},{64,7... | collective-permute-start | bytes 55304 | tf_op jit(solution)/shard_map/ppermute | solution.py:20
  9.7 0.6 copy-start.2
  15.8 40.9 %all-to-all-start = ((bf16[64,8,256]{2,1,0:T(8,128)(2,1)}), bf16[64,8,256]{2,1,0:T(8,128)(2,1)S(1)}, u32[]{:S(2)}, u32[]{:S(2)}) async-start(bf16[64,8,256]{2,1,0:T(8,128)(2,1)} %bitcast.1), calls=%async_computation | async-start | bytes 524288 | tf_op jit(solution)/shard_map/all_to_all | solution.py:274
  33.9 23.7 %copy-start.4 = (f32[8]{0:T(128)S(1)}, f32[8]{0:T(128)}, u32[]{:S(2)}) copy-start(f32[8]{0:T(128)} %param.9) | copy-start | bytes 100
  58.3 20.9 %copy-start.3 = (f32[4,16]{1,0:T(4,128)S(1)}, f32[4,16]{1,0:T(4,128)}, u32[]{:S(2)}) copy-start(f32[4,16]{1,0:T(4,128)} %param.11) | copy-start | bytes 772
  71.8 31.4 %copy-start.5 = (bf16[256,512]{1,0:T(8,128)(2,1)S(1)}, bf16[256,512]{1,0:T(8,128)(2,1)}, u32[]{:S(2)}) copy-start(bf16[256,512]{1,0:T(8,128)(2,1)} %get-tuple-element.9) | copy-start | bytes 786436
  73.7 29.2 %all-to-all-start.1 = ((bf16[8,64,256]{2,0,1:T(8,128)(2,1)}), bf16[8,64,256]{2,0,1:T(8,128)(2,1)S(1)}, u32[]{:S(2)}, u32[]{:S(2)}) async-start(bf16[8,64,256]{2,0,1:T(8,128)(2,1)} %copy.28), calls=%async_computation.1 | async-start | bytes 524288 | tf_op jit(solution)/shard_map/all_to_all | solution.py:276

commit v6 on v5

--- a/solution.py
+++ b/solution.py
@@ -214,9 +214,8 @@
     return (*_split(cos_a), *_split(sin_a), *_split(cos_b), *_split(sin_b), cos_t, sin_t, *_split(inv))
 
 
-def filter_spectrum(filt, tabs, ch_block=2):
+def filter_spectrum(filt, tabs, ch_block=2, size_b=256):
     ch, length = filt.shape
-    size_b = 128
     half_a = length // size_b
     size_a = 2 * half_a
     h = filt.reshape(ch, half_a, size_b)
@@ -232,9 +231,8 @@
     )(h, *tabs[:10])
 
 
-def long_conv(kv, spectrum, gain, tabs, ch_block=2):
+def long_conv(kv, spectrum, gain, tabs, ch_block=2, size_b=256):
     ch, length = kv.shape
-    size_b = 128
     half_a = length // size_b
     size_a = 2 * half_a
     x = kv.reshape(ch, half_a, size_b)
@@ -268,7 +266,7 @@
     rim_width = KS - 1
     prior_rows = passed_along(projected[:, tok_rows - rim_width :, :], "seq", 1)
     q_feat, gated_kv = featurize_kv(projected, prior_rows, feat_weight)
-    tabs = conv_tables(2 * length // 128, 128)
+    tabs = conv_tables(2 * length // 256, 256)
     spectrum = filter_spectrum(long_filter, tabs)
     kv_cols = jnp.transpose(gated_kv, (1, 0))
     kv_owned = lax.all_to_all(kv_cols, "seq", split_axis=0, concat_axis=1, tiled=True)

time: 129 us -> 129 us (level)
    all_to_all x2 -> x0, local copies, waits for them, and re-layouts: 1.93 us -> none  [local(): lax.all_to_all(filtered, 'seq', split_axis=1, concat_axis=0, tiled=True)]
    pallas_call x0 -> x1, local copies, waits for them, and re-layouts: none -> 1.86 us  [long_conv(): pl.pallas_call(_conv_body, grid=(ch // ch_block,), in_specs=[pl.BlockSpec...]
    convert_element_type x3 -> x2, other arithmetic: 2.76 us -> 2.35 us  [_split(): hi = a.astype(jnp.bfloat16)]
where the time goes in v6:
time: 129 us; the launch traced here: 128 us
  waiting for transfers between devices  37.2 us (29%)
  starting transfers between devices  27.6 us (21%)
  Pallas kernels  22.9 us (18%)
  blocking collectives  19.4 us (15%)
  local copies, waits for them, and re-layouts  10.7 us (8%)
  other arithmetic  7.9 us (6%)
  matrix products  2.31 us (2%)
    all_to_all x1, waiting for transfers between devices, local(): lax.all_to_all(filtered, 'seq', split_axis=1, concat_axis=0, tiled=True)  23.6 us
    all_to_all x1, blocking collectives, local(): gathered = lax.all_to_all(pieces, 'tensor', 0, 0, tiled=True)  19.4 us
    all_to_all x1, starting transfers between devices, local(): lax.all_to_all(kv_cols, 'seq', split_axis=0, concat_axis=1, tiled=True)  17.2 us
    pallas_call x1, Pallas kernels, long_conv(): pl.pallas_call(_conv_body, grid=(ch // ch_block,), in_specs=[pl.BlockSpec...  13.3 us
    all_to_all x1, waiting for transfers between devices, local(): lax.all_to_all(kv_cols, 'seq', split_axis=0, concat_axis=1, tiled=True)  9.69 us
    pallas_call x1, Pallas kernels, filter_spectrum(): pl.pallas_call(_filter_body, grid=(ch // ch_block,), in_specs=[pl.BlockSp...  5.91 us
    all_to_all x1, starting transfers between devices, local(): lax.all_to_all(filtered, 'seq', split_axis=1, concat_axis=0, tiled=True)  5.5 us
    ppermute x1, starting transfers between devices, passed_along(): return lax.ppermute(x, axis, pairs)  4.92 us
  transfers between devices with their start and end apart: 3, of which 3 were waited for; matrix products, arithmetic and copies ran while one was open for 6% of the time, Pallas kernels for 5%

profile of v6, /device:TPU:1, one launch (start us, length us, event | category | flops | bytes accessed | tf_op | source)
XLA Modules:
  0.0 128.1 jit_solution(645154612086561312)
XLA Ops:
  0.0 0.0 copy-start
  0.0 0.0 copy-start.1
  0.0 0.9 slice.3
  0.9 4.9 %collective-permute-start = (bf16[3,6,512]{2,1,0:T(8,128)(2,1)S(1)}, bf16[3,6,512]{2,1,0:T(8,128)(2,1)S(1)}, u32[]{:S(2)}, u32[]{:S(2)}) collective-permute-start(bf16[3,6,512]{2,1,0:T(8,128)(2,1)S(1)} %slice.3), channel_id=1, source_target_pairs={{0,8},{8,16},{16,24},{24,32},{32,40},{40,48},{48,56},{56,64},{64,7... | collective-permute-start | bytes 55304 | tf_op jit(solution)/shard_map/ppermute | solution.py:20
  5.8 3.9 %collective-permute-done.prior_ref = bf16[3,6,512]{2,1,0:T(8,128)(2,1)S(1)} collective-permute-done((bf16[3,6,512]{2,1,0:T(8,128)(2,1)S(1)}, bf16[3,6,512]{2,1,0:T(8,128)(2,1)S(1)}, u32[]{:S(2)}, u32[]{:S(2)}) %collective-permute-start) | collective-permute-done | bytes 18464 | tf_op jit(solution)/shard_map/ppermute | solution.py:20
  9.7 0.0 copy-start.2
  9.7 0.6 copy-done.2
  10.3 3.7 %shard_map.64 = (bf16[256,512]{1,0:T(8,128)(2,1)}, bf16[256,512]{1,0:T(8,128)(2,1)}) custom-call(bf16[3,256,512]{2,1,0:T(8,128)(2,1)} %proj_ref.1, bf16[3,6,512]{2,1,0:T(8,128)(2,1)} %copy-done.2, f32[3,7,512]{2,1,0:T(8,128)} %w_ref.1), custom_call_target="tpu_custom_call" | custom-call | tf_op jit(solution)/shard_map/pallas_call | solution.py:117
  14.0 1.8 %copy.31 = bf16[512,256]{1,0:T(8,128)(2,1)} copy(bf16[512,256]{0,1:T(8,128)(2,1)} %bitcast.43) | data formatting | bytes 524288 | tf_op jit(solution)/shard_map/transpose | solution.py:271
  15.8 17.2 %all-to-all-start = ((bf16[64,8,256]{2,1,0:T(8,128)(2,1)}), bf16[64,8,256]{2,1,0:T(8,128)(2,1)S(1)}, u32[]{:S(2)}, u32[]{:S(2)}) async-start(bf16[64,8,256]{2,1,0:T(8,128)(2,1)} %bitcast.1), calls=%async_computation | async-start | bytes 524288 | tf_op jit(solution)/shard_map/all_to_all | solution.py:272
  33.0 0.1 copy.33
  33.1 0.0 copy-done.1
  33.1 0.0 copy-start.4
  33.1 1.0 copy.49
  34.1 1.8 %subtract_convert_fusion = (bf16[256,256]{1,0:T(8,128)(2,1)}, bf16[256,256]{1,0:T(8,128)(2,1)}) fusion(), kind=kLoop, calls=%fused_computation.15 | loop fusion | flops 1441792 | bytes 262144 | tf_op jit(solution)/shard_map/convert_element_type | solution.py:137
  35.8 1.7 %fusion.17 = (bf16[256,256]{1,0:T(8,128)(2,1)}, bf16[256,256]{1,0:T(8,128)(2,1)}) fusion(), kind=kLoop, calls=%fused_computation.30 | loop fusion | flops 1048576 | bytes 262144 | tf_op jit(solution)/shard_map/convert_element_type | solution.py:136
  37.6 1.3 fusion.20
  38.8 0.9 subtract_convert_fusion.3
  39.7 5.9 %shard_map.65 = (f32[8,128,256]{2,1,0:T(8,128)}, f32[8,128,256]{2,1,0:T(8,128)}) custom-call(f32[8,64,256]{2,1,0:T(8,128)} %bitcast.40, bf16[128,64]{1,0:T(8,128)(2,1)} %get-tuple-element.16.ca_h, bf16[128,64]{1,0:T(8,128)(2,1)} %get-tuple-element.14.ca_l, bf16[128,64]{1,0:T(8,128)(2,1)} %get-tuple-element.15.sa_h, bf16[128,64]{1,0:T(8,128)(2,1)} %get-tuple-element.13.sa_l, ...), custom_call_target="tpu_custom_call" | custom-call | tf_op jit(solution)/shard_map/pallas_call | solution.py:224
  45.6 0.1 sine_negate_fusion
  45.8 0.6 fusion.24.inv_h
  46.4 0.6 subtract_convert_fusion.2.inv_l
  47.0 9.7 %all-to-all-done = bf16[64,8,256]{2,1,0:T(8,128)(2,1)S(1)} async-done(((bf16[64,8,256]{2,1,0:T(8,128)(2,1)}), bf16[64,8,256]{2,1,0:T(8,128)(2,1)S(1)}, u32[]{:S(2)}, u32[]{:S(2)}) %all-to-all-start) | async-done | bytes 262176 | tf_op jit(solution)/shard_map/all_to_all | solution.py:272
  56.7 0.7 copy.50
  57.4 0.0 copy-done.4
  57.4 0.7 broadcast_in_dim.4.g_ref
  58.1 0.0 copy-start.3
  58.1 13.3 %shard_map.66 = bf16[8,64,256]{2,1,0:T(8,128)(2,1)} custom-call(bf16[8,64,256]{2,1,0:T(8,128)(2,1)} %bitcast.41, f32[8,128,256]{2,1,0:T(8,128)} %get-tuple-element.11.fh_re_ref, f32[8,128,256]{2,1,0:T(8,128)} %get-tuple-element.12.fh_im_ref, f32[8,1,256]{2,1,0:T(1,128)} %broadcast_in_dim.4.g_ref, bf16[128,64]{1,0:T(8,128)(2,1)} %get-tuple-element.16.ca_h, ...), custom_call_target="tpu_custom_call" | custom-call | tf_op jit(solution)/shard_map/pallas_call | solution.py:242
  71.4 0.0 copy-start.5
  71.4 1.9 %copy.34 = bf16[8,64,256]{2,0,1:T(8,128)(2,1)} copy(bf16[8,64,256]{2,1,0:T(8,128)(2,1)} %shard_map.66) | data formatting | bytes 524288 | tf_op jit(solution)/shard_map/pallas_call | solution.py:242
  73.3 5.5 %all-to-all-start.1 = ((bf16[8,64,256]{2,0,1:T(8,128)(2,1)}), bf16[8,64,256]{2,0,1:T(8,128)(2,1)S(1)}, u32[]{:S(2)}, u32[]{:S(2)}) async-start(bf16[8,64,256]{2,0,1:T(8,128)(2,1)} %copy.34), calls=%async_computation.1 | async-start | bytes 524288 | tf_op jit(solution)/shard_map/all_to_all | solution.py:274
  78.8 0.0 copy-done.3
  78.8 0.1 broadcast_bitcast_fusion
  78.9 23.6 %all-to-all-done.1 = bf16[8,64,256]{2,0,1:T(8,128)(2,1)S(1)} async-done(((bf16[8,64,256]{2,0,1:T(8,128)(2,1)}), bf16[8,64,256]{2,0,1:T(8,128)(2,1)S(1)}, u32[]{:S(2)}, u32[]{:S(2)}) %all-to-all-start.1) | async-done | bytes 262176 | tf_op jit(solution)/shard_map/all_to_all | solution.py:274
  102.6 0.2 copy.35
  102.8 0.0 copy-done
  102.8 0.0 copy-done.5
  102.8 2.3 %multiply_reduce_fusion = bf16[256,2048]{1,0:T(8,128)(2,1)} fusion(bf16[4,128,2048]{2,1,0:T(8,128)(2,1)S(1)} %bitcast.38, f32[4,2048]{1,0:T(4,128)S(1)} %bitcast.44, f32[512,256]{0,1:T(8,128)S(1)} %copy.35, bf16[256,512]{1,0:T(8,128)(2,1)S(1)} %copy-done.5), kind=kOutput, calls=%fused_computation | convolution fusion | flops 540934144 | bytes 3964928 | tf_op jit(solution)/shard_map/tbk,bkn->btn/dot_general | solution.py:281
  105.1 1.5 %copy.37 = bf16[256,2048]{0,1:T(8,128)(2,1)S(1)} copy(bf16[256,2048]{1,0:T(8,128)(2,1)} %multiply_reduce_fusion) | data formatting | bytes 2097152 | tf_op jit(solution)/shard_map/convert_element_type | solution.py:284
  106.6 1.3 %copy.38 = bf16[8,256,256]{2,1,0:T(8,128)(2,1)} copy(bf16[8,256,256]{1,2,0:T(8,128)(2,1)S(1)} %bitcast.39) | data formatting | bytes 2097152 | tf_op jit(solution)/shard_map/transpose | solution.py:286
  107.9 19.4 %all_to_all.31 = bf16[8,256,256]{2,1,0:T(8,128)(2,1)S(1)} all-to-all(bf16[8,256,256]{2,1,0:T(8,128)(2,1)} %copy.38), channel_id=1, replica_groups=mesh['seq'=64,'tensor'=8] {'tensor'}, dimensions={0} | all-to-all | bytes 2097152 | tf_op jit(solution)/shard_map/all_to_all | solution.py:287
  127.3 0.8 reduce_sum.22
  (3 shorter events, 0.1 us)
Async XLA Ops:
  0.0 102.8 %copy-start = (bf16[512,2048]{1,0:T(8,128)(2,1)S(1)}, bf16[512,2048]{1,0:T(8,128)(2,1)}, u32[]{:S(2)}) copy-start(bf16[512,2048]{1,0:T(8,128)(2,1)} %param.10) | copy-start | bytes 6291460
  0.0 33.1 %copy-start.1 = (f32[8,16384]{1,0:T(8,128)S(1)}, f32[8,16384]{1,0:T(8,128)}, u32[]{:S(2)}) copy-start(f32[8,16384]{1,0:T(8,128)} %param.8) | copy-start | bytes 1572868
  0.9 8.8 %collective-permute-start = (bf16[3,6,512]{2,1,0:T(8,128)(2,1)S(1)}, bf16[3,6,512]{2,1,0:T(8,128)(2,1)S(1)}, u32[]{:S(2)}, u32[]{:S(2)}) collective-permute-start(bf16[3,6,512]{2,1,0:T(8,128)(2,1)S(1)} %slice.3), channel_id=1, source_target_pairs={{0,8},{8,16},{16,24},{24,32},{32,40},{40,48},{48,56},{56,64},{64,7... | collective-permute-start | bytes 55304 | tf_op jit(solution)/shard_map/ppermute | solution.py:20
  9.7 0.6 copy-start.2
  15.8 40.9 %all-to-all-start = ((bf16[64,8,256]{2,1,0:T(8,128)(2,1)}), bf16[64,8,256]{2,1,0:T(8,128)(2,1)S(1)}, u32[]{:S(2)}, u32[]{:S(2)}) async-start(bf16[64,8,256]{2,1,0:T(8,128)(2,1)} %bitcast.1), calls=%async_computation | async-start | bytes 524288 | tf_op jit(solution)/shard_map/all_to_all | solution.py:272
  33.1 24.4 %copy-start.4 = (f32[8]{0:T(128)S(1)}, f32[8]{0:T(128)}, u32[]{:S(2)}) copy-start(f32[8]{0:T(128)} %param.9) | copy-start | bytes 100
  58.1 20.7 %copy-start.3 = (f32[4,16]{1,0:T(4,128)S(1)}, f32[4,16]{1,0:T(4,128)}, u32[]{:S(2)}) copy-start(f32[4,16]{1,0:T(4,128)} %param.11) | copy-start | bytes 772
  71.4 31.4 %copy-start.5 = (bf16[256,512]{1,0:T(8,128)(2,1)S(1)}, bf16[256,512]{1,0:T(8,128)(2,1)}, u32[]{:S(2)}) copy-start(bf16[256,512]{1,0:T(8,128)(2,1)} %get-tuple-element.9) | copy-start | bytes 786436
  73.3 29.2 %all-to-all-start.1 = ((bf16[8,64,256]{2,0,1:T(8,128)(2,1)}), bf16[8,64,256]{2,0,1:T(8,128)(2,1)S(1)}, u32[]{:S(2)}, u32[]{:S(2)}) async-start(bf16[8,64,256]{2,0,1:T(8,128)(2,1)} %copy.34), calls=%async_computation.1 | async-start | bytes 524288 | tf_op jit(solution)/shard_map/all_to_all | solution.py:274

commit v7 on v6

--- a/solution.py
+++ b/solution.py
@@ -108,8 +108,9 @@
         for j in range(KS):
             acc = acc + w_ref[a, j : j + 1, :] * ext_ref[8 - j : 8 - j + rows, :]
         feats.append(acc.astype(jnp.bfloat16))
-    q_ref[...] = feats[0]
-    kv_ref[...] = (feats[1].astype(jnp.float32) * feats[2].astype(jnp.float32)).astype(jnp.bfloat16)
+    q_ref[...] = feats[0].astype(jnp.float32).T.astype(jnp.bfloat16)
+    kv = feats[1].astype(jnp.float32) * feats[2].astype(jnp.float32)
+    kv_ref[...] = kv.astype(jnp.bfloat16).astype(jnp.float32).T.astype(jnp.bfloat16)
 
 def featurize_kv(projected, prior, weights, lane_block=128, interpret=False):
     _, rows, chans = projected.shape
@@ -123,10 +124,10 @@
             pl.BlockSpec((3, KS, lane_block), lambda i: (0, 0, i)),
         ],
         out_specs=[
-            pl.BlockSpec((rows, lane_block), lambda i: (0, i)),
-            pl.BlockSpec((rows, lane_block), lambda i: (0, i)),
+            pl.BlockSpec((lane_block, rows), lambda i: (i, 0)),
+            pl.BlockSpec((lane_block, rows), lambda i: (i, 0)),
         ],
-        out_shape=[jax.ShapeDtypeStruct((rows, chans), jnp.bfloat16)] * 2,
+        out_shape=[jax.ShapeDtypeStruct((chans, rows), jnp.bfloat16)] * 2,
         scratch_shapes=[pltpu.VMEM((rows + 8, lane_block), jnp.float32)],
         interpret=interpret,
     )(projected, prior, weights)
@@ -254,6 +255,34 @@
     return out.reshape(ch, length)
 
 
+def _proj_body(f_ref, q_ref, w_ref, s_ref, o_ref):
+    gated = (q_ref[...].astype(jnp.float32) * f_ref[...].astype(jnp.float32)).astype(jnp.bfloat16)
+    rows_major = gated.astype(jnp.float32).T.astype(jnp.bfloat16)
+    acc = None
+    for b in range(w_ref.shape[0] // BLK):
+        part = jnp.dot(rows_major[:, b * BLK : (b + 1) * BLK], w_ref[b * BLK : (b + 1) * BLK, :],
+                       preferred_element_type=jnp.float32) * s_ref[b : b + 1, :]
+        acc = part if acc is None else acc + part
+    o_ref[0] = acc.astype(jnp.bfloat16)
+
+
+def project(filtered_home, q_cols, out_values, scale_cols, n_pieces):
+    chans, rows = filtered_home.shape
+    width = out_values.shape[1] // n_pieces
+    return pl.pallas_call(
+        _proj_body,
+        grid=(n_pieces,),
+        in_specs=[
+            pl.BlockSpec((chans, rows), lambda j: (0, 0)),
+            pl.BlockSpec((chans, rows), lambda j: (0, 0)),
+            pl.BlockSpec((chans, width), lambda j: (0, j)),
+            pl.BlockSpec((scale_cols.shape[0], width), lambda j: (0, j)),
+        ],
+        out_specs=pl.BlockSpec((1, rows, width), lambda j: (j, 0, 0)),
+        out_shape=jax.ShapeDtypeStruct((n_pieces, rows, width), jnp.bfloat16),
+    )(filtered_home, q_cols, out_values, scale_cols)
+
+
 def multiply_round(left_arr, right_arr):
     return (left_arr.astype(jnp.float32) * right_arr.astype(jnp.float32)).astype(jnp.bfloat16)
 
@@ -268,22 +297,12 @@
     q_feat, gated_kv = featurize_kv(projected, prior_rows, feat_weight)
     tabs = conv_tables(2 * length // 256, 256)
     spectrum = filter_spectrum(long_filter, tabs)
-    kv_cols = jnp.transpose(gated_kv, (1, 0))
-    kv_owned = lax.all_to_all(kv_cols, "seq", split_axis=0, concat_axis=1, tiled=True)
+    kv_owned = lax.all_to_all(gated_kv, "seq", split_axis=0, concat_axis=1, tiled=True)
     filtered = long_conv(kv_owned, spectrum, skip_gain, tabs)
     filtered_home = lax.all_to_all(filtered, "seq", split_axis=1, concat_axis=0, tiled=True)
-    gated = multiply_round(q_feat, jnp.transpose(filtered_home, (1, 0)))
-    block_count = local_ch // BLK
-    out_width = out_values.shape[1]
-    stacked = gated.reshape(tok_rows, block_count, BLK)
-    weight_blocks = out_values.reshape(block_count, BLK, out_width)
+    n_tensor = lax.axis_size("tensor")
     scale_cols = jnp.repeat(out_scales, BLK, axis=1)
-    products = jnp.einsum(
-        "tbk,bkn->btn", stacked, weight_blocks, preferred_element_type=jnp.float32
-    )
-    partial = jnp.sum(products * scale_cols[:, None, :], axis=0).astype(jnp.bfloat16)
-    n_tensor = lax.axis_size("tensor")
-    pieces = partial.reshape(tok_rows, n_tensor, out_width // n_tensor).transpose(1, 0, 2)
+    pieces = project(filtered_home, q_feat, out_values, scale_cols, n_tensor)
     gathered = lax.all_to_all(pieces, "tensor", 0, 0, tiled=True)
     return jnp.sum(gathered.astype(jnp.float32), axis=0).astype(jnp.bfloat16)
 

time: 129 us -> 130 us (level)
  Pallas kernels: 22.9 us -> 30.1 us
  local copies, waits for them, and re-layouts: 10.7 us -> 8.1 us
  matrix products: 2.31 us -> 0 us
  waiting for transfers between devices: 37.2 us -> 35.6 us
    pallas_call x0 -> x1, Pallas kernels: none -> 6.9 us  [project(): pl.pallas_call(_proj_body, grid=(n_pieces,), in_specs=[pl.BlockSpec((chan...]
    transpose x2 -> x0, local copies, waits for them, and re-layouts: 3.11 us -> none  [the longest x1 1.8 us: local(): kv_cols = jnp.transpose(gated_kv, (1, 0))]
    unnamed x15 -> x11, local copies, waits for them, and re-layouts: 1.69 us -> 4.04 us
    dot_general x1 -> x0, matrix products: 2.31 us -> none  [local(): jnp.einsum('tbk,bkn->btn', stacked, weight_blocks, preferred_element_type...]
    convert_element_type x2 -> x0, local copies, waits for them, and re-layouts: 1.67 us -> none  [the longest x1 1.47 us: local(): jnp.sum(products * scale_cols[:, None, :], axis=0).astype(jnp.bfloat16)]
  transfers between devices with their start and end apart: 3 -> 3, of which waited for: 3 -> 3; matrix products, arithmetic and copies ran while one was open for 6% -> 8% of each run, Pallas kernels for 5% -> 5%
where the time goes in v7:
time: 130 us
  waiting for transfers between devices  35.6 us (27%)
  Pallas kernels  30.1 us (23%)
  starting transfers between devices  28.6 us (22%)
  blocking collectives  19.4 us (15%)
  local copies, waits for them, and re-layouts  8.1 us (6%)
  other arithmetic  7.82 us (6%)
    all_to_all x1, waiting for transfers between devices, local(): lax.all_to_all(filtered, 'seq', split_axis=1, concat_axis=0, tiled=True)  23 us
    all_to_all x1, blocking collectives, local(): gathered = lax.all_to_all(pieces, 'tensor', 0, 0, tiled=True)  19.4 us
    all_to_all x1, starting transfers between devices, local(): lax.all_to_all(gated_kv, 'seq', split_axis=0, concat_axis=1, tiled=True)  17.2 us
    pallas_call x1, Pallas kernels, long_conv(): pl.pallas_call(_conv_body, grid=(ch // ch_block,), in_specs=[pl.BlockSpec...  13.3 us
    all_to_all x1, waiting for transfers between devices, local(): lax.all_to_all(gated_kv, 'seq', split_axis=0, concat_axis=1, tiled=True)  8.69 us
    pallas_call x1, Pallas kernels, project(): pl.pallas_call(_proj_body, grid=(n_pieces,), in_specs=[pl.BlockSpec((chan...  6.9 us
    all_to_all x1, starting transfers between devices, local(): lax.all_to_all(filtered, 'seq', split_axis=1, concat_axis=0, tiled=True)  6.52 us
    pallas_call x1, Pallas kernels, filter_spectrum(): pl.pallas_call(_filter_body, grid=(ch // ch_block,), in_specs=[pl.BlockSp...  5.91 us
  transfers between devices with their start and end apart: 3, of which 3 were waited for; matrix products, arithmetic and copies ran while one was open for 8% of the time, Pallas kernels for 5%

profile of v7, /device:TPU:1, one launch (start us, length us, event | category | flops | bytes accessed | tf_op | source)
XLA Modules:
  0.0 129.7 jit_solution(16859898997355407218)
XLA Ops:
  0.0 0.0 copy-start
  0.0 0.8 slice.3
  0.8 4.9 %collective-permute-start = (bf16[3,6,512]{2,1,0:T(8,128)(2,1)S(1)}, bf16[3,6,512]{2,1,0:T(8,128)(2,1)S(1)}, u32[]{:S(2)}, u32[]{:S(2)}) collective-permute-start(bf16[3,6,512]{2,1,0:T(8,128)(2,1)S(1)} %slice.3), channel_id=1, source_target_pairs={{0,8},{8,16},{16,24},{24,32},{32,40},{40,48},{48,56},{56,64},{64,7... | collective-permute-start | bytes 55304 | tf_op jit(solution)/shard_map/ppermute | solution.py:20
  5.7 3.9 %collective-permute-done.prior_ref = bf16[3,6,512]{2,1,0:T(8,128)(2,1)S(1)} collective-permute-done((bf16[3,6,512]{2,1,0:T(8,128)(2,1)S(1)}, bf16[3,6,512]{2,1,0:T(8,128)(2,1)S(1)}, u32[]{:S(2)}, u32[]{:S(2)}) %collective-permute-start) | collective-permute-done | bytes 18464 | tf_op jit(solution)/shard_map/ppermute | solution.py:20
  9.6 0.0 copy-start.2
  9.6 0.6 copy-done.2
  10.2 4.0 %shard_map.64 = (bf16[512,256]{1,0:T(8,128)(2,1)}, bf16[512,256]{1,0:T(8,128)(2,1)}) custom-call(bf16[3,256,512]{2,1,0:T(8,128)(2,1)} %proj_ref.1, bf16[3,6,512]{2,1,0:T(8,128)(2,1)} %copy-done.2, f32[3,7,512]{2,1,0:T(8,128)} %w_ref.2), custom_call_target="tpu_custom_call" | custom-call | tf_op jit(solution)/shard_map/pallas_call | solution.py:118
  14.2 17.2 %all-to-all-start = ((bf16[64,8,256]{2,1,0:T(8,128)(2,1)}), bf16[64,8,256]{2,1,0:T(8,128)(2,1)S(1)}, u32[]{:S(2)}, u32[]{:S(2)}) async-start(bf16[64,8,256]{2,1,0:T(8,128)(2,1)} %bitcast.20), calls=%async_computation | async-start | bytes 524288 | tf_op jit(solution)/shard_map/all_to_all | solution.py:300
  31.4 0.1 copy.13
  31.5 0.0 copy-start.3
  31.5 2.0 %copy.20 = f32[1,8,64,256]{3,2,1,0:T(8,128)} copy(f32[1,8,64,256]{3,1,2,0:T(8,128)} %bitcast.19) | data formatting | bytes 1048576
  33.5 1.8 %subtract_convert_fusion = (bf16[256,256]{1,0:T(8,128)(2,1)}, bf16[256,256]{1,0:T(8,128)(2,1)}) fusion(), kind=kLoop, calls=%fused_computation.8 | loop fusion | flops 1441792 | bytes 262144 | tf_op jit(solution)/shard_map/convert_element_type | solution.py:138
  35.2 1.7 %fusion.13 = (bf16[256,256]{1,0:T(8,128)(2,1)}, bf16[256,256]{1,0:T(8,128)(2,1)}) fusion(), kind=kLoop, calls=%fused_computation.23 | loop fusion | flops 1048576 | bytes 262144 | tf_op jit(solution)/shard_map/convert_element_type | solution.py:137
  37.0 1.2 fusion.16
  38.2 0.9 subtract_convert_fusion.3
  39.1 5.9 %shard_map.65 = (f32[8,128,256]{2,1,0:T(8,128)}, f32[8,128,256]{2,1,0:T(8,128)}) custom-call(f32[8,64,256]{2,1,0:T(8,128)} %bitcast.16, bf16[128,64]{1,0:T(8,128)(2,1)} %get-tuple-element.16.ca_h, bf16[128,64]{1,0:T(8,128)(2,1)} %get-tuple-element.14.ca_l, bf16[128,64]{1,0:T(8,128)(2,1)} %get-tuple-element.15.sa_h, bf16[128,64]{1,0:T(8,128)(2,1)} %get-tuple-element.13.sa_l, ...), custom_call_target="tpu_custom_call" | custom-call | tf_op jit(solution)/shard_map/pallas_call | solution.py:225
  45.0 0.1 sine_negate_fusion
  45.2 0.6 fusion.20.inv_h
  45.8 0.6 subtract_convert_fusion.2.inv_l
  46.4 8.7 %all-to-all-done = bf16[64,8,256]{2,1,0:T(8,128)(2,1)S(1)} async-done(((bf16[64,8,256]{2,1,0:T(8,128)(2,1)}), bf16[64,8,256]{2,1,0:T(8,128)(2,1)S(1)}, u32[]{:S(2)}, u32[]{:S(2)}) %all-to-all-start) | async-done | bytes 262176 | tf_op jit(solution)/shard_map/all_to_all | solution.py:300
  55.1 0.7 copy.21
  55.8 0.0 copy-done.3
  55.8 0.7 broadcast_in_dim.4.g_ref
  56.5 13.3 %shard_map.66 = bf16[8,64,256]{2,1,0:T(8,128)(2,1)} custom-call(bf16[8,64,256]{2,1,0:T(8,128)(2,1)} %bitcast.18, f32[8,128,256]{2,1,0:T(8,128)} %get-tuple-element.10.fh_re_ref, f32[8,128,256]{2,1,0:T(8,128)} %get-tuple-element.11.fh_im_ref, f32[8,1,256]{2,1,0:T(1,128)} %broadcast_in_dim.4.g_ref, bf16[128,64]{1,0:T(8,128)(2,1)} %get-tuple-element.16.ca_h, ...), custom_call_target="tpu_custom_call" | custom-call | tf_op jit(solution)/shard_map/pallas_call | solution.py:243
  69.8 1.8 %copy.14 = bf16[8,64,256]{2,0,1:T(8,128)(2,1)} copy(bf16[8,64,256]{2,1,0:T(8,128)(2,1)} %shard_map.66) | data formatting | bytes 524288 | tf_op jit(solution)/shard_map/pallas_call | solution.py:243
  71.6 6.5 %all-to-all-start.1 = ((bf16[8,64,256]{2,0,1:T(8,128)(2,1)}), bf16[8,64,256]{2,0,1:T(8,128)(2,1)S(1)}, u32[]{:S(2)}, u32[]{:S(2)}) async-start(bf16[8,64,256]{2,0,1:T(8,128)(2,1)} %copy.14), calls=%async_computation.1 | async-start | bytes 524288 | tf_op jit(solution)/shard_map/all_to_all | solution.py:302
  78.1 0.0 copy-done
  78.1 0.1 broadcast_bitcast_fusion
  78.2 0.6 copy.22
  78.8 23.0 %all-to-all-done.1 = bf16[8,64,256]{2,0,1:T(8,128)(2,1)S(1)} async-done(((bf16[8,64,256]{2,0,1:T(8,128)(2,1)}), bf16[8,64,256]{2,0,1:T(8,128)(2,1)S(1)}, u32[]{:S(2)}, u32[]{:S(2)}) %all-to-all-start.1) | async-done | bytes 262176 | tf_op jit(solution)/shard_map/all_to_all | solution.py:302
  101.9 0.0 copy-start.1
  101.9 0.7 copy-done.1
  102.5 6.9 %shard_map.67 = bf16[8,256,256]{2,1,0:T(8,128)(2,1)} custom-call(bf16[512,256]{1,0:T(8,128)(2,1)} %bitcast.17, bf16[512,256]{1,0:T(8,128)(2,1)} %get-tuple-element.12.q_ref, bf16[512,2048]{1,0:T(8,128)(2,1)} %w_ref.3, f32[4,2048]{1,0:T(4,128)} %bitcast.21), custom_call_target="tpu_custom_call" | custom-call | tf_op jit(solution)/shard_map/pallas_call | solution.py:272
  109.4 19.4 %all_to_all.37 = bf16[8,256,256]{2,1,0:T(8,128)(2,1)S(1)} all-to-all(bf16[8,256,256]{2,1,0:T(8,128)(2,1)} %shard_map.67), channel_id=1, replica_groups=mesh['seq'=64,'tensor'=8] {'tensor'}, dimensions={0} | all-to-all | bytes 2097152 | tf_op jit(solution)/shard_map/all_to_all | solution.py:306
  128.9 0.8 reduce_sum.12
  (1 shorter events, 0.0 us)
Async XLA Ops:
  0.0 78.1 %copy-start = (f32[4,16]{1,0:T(4,128)S(1)}, f32[4,16]{1,0:T(4,128)}, u32[]{:S(2)}) copy-start(f32[4,16]{1,0:T(4,128)} %param.11) | copy-start | bytes 772
  0.8 8.8 %collective-permute-start = (bf16[3,6,512]{2,1,0:T(8,128)(2,1)S(1)}, bf16[3,6,512]{2,1,0:T(8,128)(2,1)S(1)}, u32[]{:S(2)}, u32[]{:S(2)}) collective-permute-start(bf16[3,6,512]{2,1,0:T(8,128)(2,1)S(1)} %slice.3), channel_id=1, source_target_pairs={{0,8},{8,16},{16,24},{24,32},{32,40},{40,48},{48,56},{56,64},{64,7... | collective-permute-start | bytes 55304 | tf_op jit(solution)/shard_map/ppermute | solution.py:20
  9.6 0.6 copy-start.2
  14.2 40.9 %all-to-all-start = ((bf16[64,8,256]{2,1,0:T(8,128)(2,1)}), bf16[64,8,256]{2,1,0:T(8,128)(2,1)S(1)}, u32[]{:S(2)}, u32[]{:S(2)}) async-start(bf16[64,8,256]{2,1,0:T(8,128)(2,1)} %bitcast.20), calls=%async_computation | async-start | bytes 524288 | tf_op jit(solution)/shard_map/all_to_all | solution.py:300
  31.5 24.4 %copy-start.3 = (f32[8]{0:T(128)S(1)}, f32[8]{0:T(128)}, u32[]{:S(2)}) copy-start(f32[8]{0:T(128)} %param.9) | copy-start | bytes 100
  71.6 30.3 %all-to-all-start.1 = ((bf16[8,64,256]{2,0,1:T(8,128)(2,1)}), bf16[8,64,256]{2,0,1:T(8,128)(2,1)S(1)}, u32[]{:S(2)}, u32[]{:S(2)}) async-start(bf16[8,64,256]{2,0,1:T(8,128)(2,1)} %copy.14), calls=%async_computation.1 | async-start | bytes 524288 | tf_op jit(solution)/shard_map/all_to_all | solution.py:302
  101.9 0.7 copy-start.1

commit v8 on v7

--- a/solution.py
+++ b/solution.py
@@ -255,31 +255,39 @@
     return out.reshape(ch, length)
 
 
-def _proj_body(f_ref, q_ref, w_ref, s_ref, o_ref):
-    gated = (q_ref[...].astype(jnp.float32) * f_ref[...].astype(jnp.float32)).astype(jnp.bfloat16)
-    rows_major = gated.astype(jnp.float32).T.astype(jnp.bfloat16)
-    acc = None
-    for b in range(w_ref.shape[0] // BLK):
-        part = jnp.dot(rows_major[:, b * BLK : (b + 1) * BLK], w_ref[b * BLK : (b + 1) * BLK, :],
-                       preferred_element_type=jnp.float32) * s_ref[b : b + 1, :]
-        acc = part if acc is None else acc + part
-    o_ref[0] = acc.astype(jnp.bfloat16)
-
-
-def project(filtered_home, q_cols, out_values, scale_cols, n_pieces):
+def _proj_body(f_ref, q_ref, w_ref, s_ref, o_ref, g_scr):
+    @pl.when(pl.program_id(0) == 0)
+    def _():
+        gated = (q_ref[...].astype(jnp.float32) * f_ref[...].astype(jnp.float32)).astype(jnp.bfloat16)
+        g_scr[...] = gated.astype(jnp.float32).T.astype(jnp.bfloat16)
+
+    width = o_ref.shape[2]
+    for p in range(o_ref.shape[0]):
+        acc = None
+        for b in range(w_ref.shape[0] // BLK):
+            part = jnp.dot(g_scr[:, b * BLK : (b + 1) * BLK],
+                           w_ref[b * BLK : (b + 1) * BLK, p * width : (p + 1) * width],
+                           preferred_element_type=jnp.float32) * s_ref[b : b + 1, p * width : (p + 1) * width]
+            acc = part if acc is None else acc + part
+        o_ref[p] = acc.astype(jnp.bfloat16)
+
+
+def project(filtered_home, q_cols, out_values, scale_cols, n_pieces, steps=2):
     chans, rows = filtered_home.shape
     width = out_values.shape[1] // n_pieces
+    per_step = n_pieces // steps
     return pl.pallas_call(
         _proj_body,
-        grid=(n_pieces,),
+        grid=(steps,),
         in_specs=[
             pl.BlockSpec((chans, rows), lambda j: (0, 0)),
             pl.BlockSpec((chans, rows), lambda j: (0, 0)),
-            pl.BlockSpec((chans, width), lambda j: (0, j)),
-            pl.BlockSpec((scale_cols.shape[0], width), lambda j: (0, j)),
+            pl.BlockSpec((chans, width * per_step), lambda j: (0, j)),
+            pl.BlockSpec((scale_cols.shape[0], width * per_step), lambda j: (0, j)),
         ],
-        out_specs=pl.BlockSpec((1, rows, width), lambda j: (j, 0, 0)),
+        out_specs=pl.BlockSpec((per_step, rows, width), lambda j: (j, 0, 0)),
         out_shape=jax.ShapeDtypeStruct((n_pieces, rows, width), jnp.bfloat16),
+        scratch_shapes=[pltpu.VMEM((rows, chans), jnp.bfloat16)],
     )(filtered_home, q_cols, out_values, scale_cols)
 
 

time: 130 us -> 127 us (0.977)
  Pallas kernels: 30.1 us -> 27 us
    pallas_call x1, Pallas kernels: 6.9 us -> 3.76 us  [project(): pl.pallas_call(_proj_body, grid=(steps,), in_specs=[pl.BlockSpec((chans,...]
where the time goes in v8:
time: 127 us
  waiting for transfers between devices  35.6 us (28%)
  starting transfers between devices  28.6 us (23%)
  Pallas kernels  27 us (21%)
  blocking collectives  19.4 us (15%)
  local copies, waits for them, and re-layouts  8.1 us (6%)
  other arithmetic  7.82 us (6%)
    all_to_all x1, waiting for transfers between devices, local(): lax.all_to_all(filtered, 'seq', split_axis=1, concat_axis=0, tiled=True)  23 us
    all_to_all x1, blocking collectives, local(): gathered = lax.all_to_all(pieces, 'tensor', 0, 0, tiled=True)  19.4 us
    all_to_all x1, starting transfers between devices, local(): lax.all_to_all(gated_kv, 'seq', split_axis=0, concat_axis=1, tiled=True)  17.2 us
    pallas_call x1, Pallas kernels, long_conv(): pl.pallas_call(_conv_body, grid=(ch // ch_block,), in_specs=[pl.BlockSpec...  13.3 us
    all_to_all x1, waiting for transfers between devices, local(): lax.all_to_all(gated_kv, 'seq', split_axis=0, concat_axis=1, tiled=True)  8.69 us
    all_to_all x1, starting transfers between devices, local(): lax.all_to_all(filtered, 'seq', split_axis=1, concat_axis=0, tiled=True)  6.52 us
    pallas_call x1, Pallas kernels, filter_spectrum(): pl.pallas_call(_filter_body, grid=(ch // ch_block,), in_specs=[pl.BlockSp...  5.91 us
    ppermute x1, starting transfers between devices, passed_along(): return lax.ppermute(x, axis, pairs)  4.92 us
  transfers between devices with their start and end apart: 3, of which 3 were waited for; matrix products, arithmetic and copies ran while one was open for 8% of the time, Pallas kernels for 5%

profile of v8, /device:TPU:1, one launch (start us, length us, event | category | flops | bytes accessed | tf_op | source)
XLA Modules:
  0.0 126.5 jit_solution(6286746390174214053)
XLA Ops:
  0.0 0.0 copy-start
  0.0 0.8 slice.3
  0.8 4.9 %collective-permute-start = (bf16[3,6,512]{2,1,0:T(8,128)(2,1)S(1)}, bf16[3,6,512]{2,1,0:T(8,128)(2,1)S(1)}, u32[]{:S(2)}, u32[]{:S(2)}) collective-permute-start(bf16[3,6,512]{2,1,0:T(8,128)(2,1)S(1)} %slice.3), channel_id=1, source_target_pairs={{0,8},{8,16},{16,24},{24,32},{32,40},{40,48},{48,56},{56,64},{64,7... | collective-permute-start | bytes 55304 | tf_op jit(solution)/shard_map/ppermute | solution.py:20
  5.7 3.9 %collective-permute-done.prior_ref = bf16[3,6,512]{2,1,0:T(8,128)(2,1)S(1)} collective-permute-done((bf16[3,6,512]{2,1,0:T(8,128)(2,1)S(1)}, bf16[3,6,512]{2,1,0:T(8,128)(2,1)S(1)}, u32[]{:S(2)}, u32[]{:S(2)}) %collective-permute-start) | collective-permute-done | bytes 18464 | tf_op jit(solution)/shard_map/ppermute | solution.py:20
  9.6 0.0 copy-start.2
  9.6 0.6 copy-done.2
  10.2 4.0 %shard_map.64 = (bf16[512,256]{1,0:T(8,128)(2,1)}, bf16[512,256]{1,0:T(8,128)(2,1)}) custom-call(bf16[3,256,512]{2,1,0:T(8,128)(2,1)} %proj_ref.1, bf16[3,6,512]{2,1,0:T(8,128)(2,1)} %copy-done.2, f32[3,7,512]{2,1,0:T(8,128)} %w_ref.2), custom_call_target="tpu_custom_call" | custom-call | tf_op jit(solution)/shard_map/pallas_call | solution.py:118
  14.2 17.2 %all-to-all-start = ((bf16[64,8,256]{2,1,0:T(8,128)(2,1)}), bf16[64,8,256]{2,1,0:T(8,128)(2,1)S(1)}, u32[]{:S(2)}, u32[]{:S(2)}) async-start(bf16[64,8,256]{2,1,0:T(8,128)(2,1)} %bitcast.20), calls=%async_computation | async-start | bytes 524288 | tf_op jit(solution)/shard_map/all_to_all | solution.py:308
  31.4 0.1 copy.13
  31.5 0.0 copy-start.3
  31.5 2.0 %copy.20 = f32[1,8,64,256]{3,2,1,0:T(8,128)} copy(f32[1,8,64,256]{3,1,2,0:T(8,128)} %bitcast.19) | data formatting | bytes 1048576
  33.5 1.8 %subtract_convert_fusion = (bf16[256,256]{1,0:T(8,128)(2,1)}, bf16[256,256]{1,0:T(8,128)(2,1)}) fusion(), kind=kLoop, calls=%fused_computation.8 | loop fusion | flops 1441792 | bytes 262144 | tf_op jit(solution)/shard_map/convert_element_type | solution.py:138
  35.2 1.7 %fusion.13 = (bf16[256,256]{1,0:T(8,128)(2,1)}, bf16[256,256]{1,0:T(8,128)(2,1)}) fusion(), kind=kLoop, calls=%fused_computation.23 | loop fusion | flops 1048576 | bytes 262144 | tf_op jit(solution)/shard_map/convert_element_type | solution.py:137
  37.0 1.2 fusion.16
  38.2 0.9 subtract_convert_fusion.3
  39.1 5.9 %shard_map.65 = (f32[8,128,256]{2,1,0:T(8,128)}, f32[8,128,256]{2,1,0:T(8,128)}) custom-call(f32[8,64,256]{2,1,0:T(8,128)} %bitcast.16, bf16[128,64]{1,0:T(8,128)(2,1)} %get-tuple-element.16.ca_h, bf16[128,64]{1,0:T(8,128)(2,1)} %get-tuple-element.14.ca_l, bf16[128,64]{1,0:T(8,128)(2,1)} %get-tuple-element.15.sa_h, bf16[128,64]{1,0:T(8,128)(2,1)} %get-tuple-element.13.sa_l, ...), custom_call_target="tpu_custom_call" | custom-call | tf_op jit(solution)/shard_map/pallas_call | solution.py:225
  45.0 0.1 sine_negate_fusion
  45.2 0.6 fusion.20.inv_h
  45.8 0.6 subtract_convert_fusion.2.inv_l
  46.4 8.7 %all-to-all-done = bf16[64,8,256]{2,1,0:T(8,128)(2,1)S(1)} async-done(((bf16[64,8,256]{2,1,0:T(8,128)(2,1)}), bf16[64,8,256]{2,1,0:T(8,128)(2,1)S(1)}, u32[]{:S(2)}, u32[]{:S(2)}) %all-to-all-start) | async-done | bytes 262176 | tf_op jit(solution)/shard_map/all_to_all | solution.py:308
  55.1 0.7 copy.21
  55.8 0.0 copy-done.3
  55.8 0.7 broadcast_in_dim.4.g_ref
  56.5 13.3 %shard_map.66 = bf16[8,64,256]{2,1,0:T(8,128)(2,1)} custom-call(bf16[8,64,256]{2,1,0:T(8,128)(2,1)} %bitcast.18, f32[8,128,256]{2,1,0:T(8,128)} %get-tuple-element.10.fh_re_ref, f32[8,128,256]{2,1,0:T(8,128)} %get-tuple-element.11.fh_im_ref, f32[8,1,256]{2,1,0:T(1,128)} %broadcast_in_dim.4.g_ref, bf16[128,64]{1,0:T(8,128)(2,1)} %get-tuple-element.16.ca_h, ...), custom_call_target="tpu_custom_call" | custom-call | tf_op jit(solution)/shard_map/pallas_call | solution.py:243
  69.8 1.8 %copy.14 = bf16[8,64,256]{2,0,1:T(8,128)(2,1)} copy(bf16[8,64,256]{2,1,0:T(8,128)(2,1)} %shard_map.66) | data formatting | bytes 524288 | tf_op jit(solution)/shard_map/pallas_call | solution.py:243
  71.6 6.5 %all-to-all-start.1 = ((bf16[8,64,256]{2,0,1:T(8,128)(2,1)}), bf16[8,64,256]{2,0,1:T(8,128)(2,1)S(1)}, u32[]{:S(2)}, u32[]{:S(2)}) async-start(bf16[8,64,256]{2,0,1:T(8,128)(2,1)} %copy.14), calls=%async_computation.1 | async-start | bytes 524288 | tf_op jit(solution)/shard_map/all_to_all | solution.py:310
  78.1 0.0 copy-done
  78.1 0.1 broadcast_bitcast_fusion
  78.2 0.6 copy.22
  78.8 23.0 %all-to-all-done.1 = bf16[8,64,256]{2,0,1:T(8,128)(2,1)S(1)} async-done(((bf16[8,64,256]{2,0,1:T(8,128)(2,1)}), bf16[8,64,256]{2,0,1:T(8,128)(2,1)S(1)}, u32[]{:S(2)}, u32[]{:S(2)}) %all-to-all-start.1) | async-done | bytes 262176 | tf_op jit(solution)/shard_map/all_to_all | solution.py:310
  101.9 0.0 copy-start.1
  101.9 0.7 copy-done.1
  102.5 3.8 %shard_map.67 = bf16[8,256,256]{2,1,0:T(8,128)(2,1)} custom-call(bf16[512,256]{1,0:T(8,128)(2,1)} %bitcast.17, bf16[512,256]{1,0:T(8,128)(2,1)} %get-tuple-element.12.q_ref, bf16[512,2048]{1,0:T(8,128)(2,1)} %w_ref.3, f32[4,2048]{1,0:T(4,128)} %bitcast.21), custom_call_target="tpu_custom_call" | custom-call | tf_op jit(solution)/shard_map/pallas_call | solution.py:279
  106.3 19.4 %all_to_all.37 = bf16[8,256,256]{2,1,0:T(8,128)(2,1)S(1)} all-to-all(bf16[8,256,256]{2,1,0:T(8,128)(2,1)} %shard_map.67), channel_id=1, replica_groups=mesh['seq'=64,'tensor'=8] {'tensor'}, dimensions={0} | all-to-all | bytes 2097152 | tf_op jit(solution)/shard_map/all_to_all | solution.py:314
  125.7 0.8 reduce_sum.12
  (1 shorter events, 0.0 us)
Async XLA Ops:
  0.0 78.1 %copy-start = (f32[4,16]{1,0:T(4,128)S(1)}, f32[4,16]{1,0:T(4,128)}, u32[]{:S(2)}) copy-start(f32[4,16]{1,0:T(4,128)} %param.11) | copy-start | bytes 772
  0.8 8.8 %collective-permute-start = (bf16[3,6,512]{2,1,0:T(8,128)(2,1)S(1)}, bf16[3,6,512]{2,1,0:T(8,128)(2,1)S(1)}, u32[]{:S(2)}, u32[]{:S(2)}) collective-permute-start(bf16[3,6,512]{2,1,0:T(8,128)(2,1)S(1)} %slice.3), channel_id=1, source_target_pairs={{0,8},{8,16},{16,24},{24,32},{32,40},{40,48},{48,56},{56,64},{64,7... | collective-permute-start | bytes 55304 | tf_op jit(solution)/shard_map/ppermute | solution.py:20
  9.6 0.6 copy-start.2
  14.2 40.9 %all-to-all-start = ((bf16[64,8,256]{2,1,0:T(8,128)(2,1)}), bf16[64,8,256]{2,1,0:T(8,128)(2,1)S(1)}, u32[]{:S(2)}, u32[]{:S(2)}) async-start(bf16[64,8,256]{2,1,0:T(8,128)(2,1)} %bitcast.20), calls=%async_computation | async-start | bytes 524288 | tf_op jit(solution)/shard_map/all_to_all | solution.py:308
  31.5 24.4 %copy-start.3 = (f32[8]{0:T(128)S(1)}, f32[8]{0:T(128)}, u32[]{:S(2)}) copy-start(f32[8]{0:T(128)} %param.9) | copy-start | bytes 100
  71.6 30.3 %all-to-all-start.1 = ((bf16[8,64,256]{2,0,1:T(8,128)(2,1)}), bf16[8,64,256]{2,0,1:T(8,128)(2,1)S(1)}, u32[]{:S(2)}, u32[]{:S(2)}) async-start(bf16[8,64,256]{2,0,1:T(8,128)(2,1)} %copy.14), calls=%async_computation.1 | async-start | bytes 524288 | tf_op jit(solution)/shard_map/all_to_all | solution.py:310
  101.9 0.7 copy-start.1

commit v9 on v8

--- a/solution.py
+++ b/solution.py
@@ -152,50 +152,65 @@
     return _mm(v_hi, t_hi) + _mm(v_lo, t_hi) + _mm(v_hi, t_lo)
 
 
-def _spectrum(a_re, a_im, ct, st, cb_h, cb_l, sb_h, sb_l):
-    rows = ct.shape[0]
+def _spectrum(a_re, a_im, ct, st, cbsb_h, cbsb_l):
+    rows, width = ct.shape
     t_re = a_re * ct + a_im * st
     t_im = a_im * ct - a_re * st
-    stacked = jnp.concatenate([t_re, t_im], axis=0)
-    r_c = _right3(stacked, cb_h, cb_l)
-    r_s = _right3(stacked, sb_h, sb_l)
-    return r_c[:rows] + r_s[rows:], r_c[rows:] - r_s[:rows]
-
-
-def _filter_body(h_ref, ca_h, ca_l, sa_h, sa_l, cb_h, cb_l, sb_h, sb_l, ct_ref, st_ref, re_ref, im_ref):
+    r = _right3(jnp.concatenate([t_re, t_im], axis=0), cbsb_h, cbsb_l)
+    f_re = r[:rows, :width] + r[rows:, width:]
+    f_im = r[rows:, :width] - r[:rows, width:]
+    return f_re, f_im
+
+
+def _filter_body(h_ref, casa_h, casa_l, cbsb_h, cbsb_l, ct_ref, st_ref, re_ref, im_ref):
     ct = ct_ref[...]
     st = st_ref[...]
+    rows = ct.shape[0]
     for c in range(h_ref.shape[0]):
-        h = h_ref[c]
-        a_re = _left3(ca_h[...], ca_l[...], h)
-        a_im = -_left3(sa_h[...], sa_l[...], h)
-        re_ref[c], im_ref[c] = _spectrum(a_re, a_im, ct, st, cb_h[...], cb_l[...], sb_h[...], sb_l[...])
-
-
-def _conv_body(x_ref, fh_re_ref, fh_im_ref, g_ref, ca_h, ca_l, sa_h, sa_l, cb_h, cb_l, sb_h, sb_l,
-               ct_ref, st_ref, inv_h, inv_l, o_ref):
-    rows = ct_ref.shape[0]
+        a = _left3(casa_h[...], casa_l[...], h_ref[c])
+        re_ref[c], im_ref[c] = _spectrum(a[:rows], -a[rows:], ct, st, cbsb_h[...], cbsb_l[...])
+
+
+def _conv_body(x_ref, fh_re_ref, fh_im_ref, g_ref, casa_h, casa_l, cbsb_h, cbsb_l,
+               ct_ref, st_ref, ctw_ref, stw_ref, inv_h, inv_l, o_ref):
     ct = ct_ref[...]
     st = st_ref[...]
-    for c in range(x_ref.shape[0]):
-        x_b = x_ref[c]
-        a_re = _mm(ca_h[...], x_b) + _mm(ca_l[...], x_b)
-        a_im = -(_mm(sa_h[...], x_b) + _mm(sa_l[...], x_b))
-        fx_re, fx_im = _spectrum(a_re, a_im, ct, st, cb_h[...], cb_l[...], sb_h[...], sb_l[...])
+    rows, width = ct.shape
+    chans = fh_re_ref.shape[0]
+    x_b = x_ref[...]
+    a = _mm(casa_h[...], x_b) + _mm(casa_l[...], x_b)
+    ctw = ctw_ref[...]
+    stw = stw_ref[...]
+    a_re = a[:rows]
+    a_im = -a[rows:]
+    t_re = a_re * ctw + a_im * stw
+    t_im = a_im * ctw - a_re * stw
+    pieces = []
+    for c in range(chans):
+        pieces.append(t_re[:, c * width : (c + 1) * width])
+        pieces.append(t_im[:, c * width : (c + 1) * width])
+    r = _right3(jnp.concatenate(pieces, axis=0), cbsb_h[...], cbsb_l[...])
+    prods = []
+    for c in range(chans):
+        lo = 2 * rows * c
+        f_re = r[lo : lo + rows, :width] + r[lo + rows : lo + 2 * rows, width:]
+        f_im = r[lo + rows : lo + 2 * rows, :width] - r[lo : lo + rows, width:]
         fh_re = fh_re_ref[c]
         fh_im = fh_im_ref[c]
-        p_re = fx_re * fh_re - fx_im * fh_im
-        p_im = fx_re * fh_im + fx_im * fh_re
-        stacked = jnp.concatenate([p_re, p_im], axis=0)
-        q_c = _right3(stacked, cb_h[...], cb_l[...])
-        q_s = _right3(stacked, sb_h[...], sb_l[...])
-        z_re = q_c[:rows] - q_s[rows:]
-        z_im = q_c[rows:] + q_s[:rows]
+        prods.append(f_re * fh_re - f_im * fh_im)
+        prods.append(f_re * fh_im + f_im * fh_re)
+    q = _right3(jnp.concatenate(prods, axis=0), cbsb_h[...], cbsb_l[...])
+    cols = []
+    for c in range(chans):
+        lo = 2 * rows * c
+        z_re = q[lo : lo + rows, :width] - q[lo + rows : lo + 2 * rows, width:]
+        z_im = q[lo + rows : lo + 2 * rows, :width] + q[lo : lo + rows, width:]
         w_re = z_re * ct - z_im * st
         w_im = z_im * ct + z_re * st
-        out = _left3(inv_h[...], inv_l[...], jnp.concatenate([w_re, w_im], axis=0))
-        x_f = x_b.astype(jnp.float32)
-        o_ref[c] = (out * (1.0 / (rows * ct_ref.shape[1])) + g_ref[c] * x_f).astype(jnp.bfloat16)
+        cols.append(jnp.concatenate([w_re, w_im], axis=0))
+    out = _left3(inv_h[...], inv_l[...], jnp.concatenate(cols, axis=1))
+    x_f = x_b.astype(jnp.float32)
+    o_ref[...] = (out * (1.0 / (rows * width)) + g_ref[...] * x_f).astype(jnp.bfloat16)
 
 
 def conv_tables(size_a, size_b):
@@ -212,7 +227,9 @@
     cos_b, sin_b = pair(size_b, size_b, size_b)
     cos_t, sin_t = pair(size_a, size_b, whole)
     inv = jnp.concatenate([cos_a.T, -sin_a.T], axis=1)
-    return (*_split(cos_a), *_split(sin_a), *_split(cos_b), *_split(sin_b), cos_t, sin_t, *_split(inv))
+    casa = jnp.concatenate([cos_a, sin_a], axis=0)
+    cbsb = jnp.concatenate([cos_b, sin_b], axis=1)
+    return (*_split(casa), *_split(cbsb), cos_t, sin_t, *_split(inv))
 
 
 def filter_spectrum(filt, tabs, ch_block=2, size_b=256):
@@ -226,33 +243,24 @@
         _filter_body,
         grid=(ch // ch_block,),
         in_specs=[pl.BlockSpec((ch_block, half_a, size_b), lambda i: (i, 0, 0))]
-        + [full(t) for t in tabs[:10]],
+        + [full(t) for t in tabs[:6]],
         out_specs=[blk_out, blk_out],
         out_shape=[jax.ShapeDtypeStruct((ch, size_a, size_b), jnp.float32)] * 2,
-    )(h, *tabs[:10])
-
-
-def long_conv(kv, spectrum, gain, tabs, ch_block=2, size_b=256):
-    ch, length = kv.shape
-    half_a = length // size_b
-    size_a = 2 * half_a
-    x = kv.reshape(ch, half_a, size_b)
-    g = jnp.broadcast_to(gain[:, None, None], (ch, 1, size_b))
-    full = lambda t: pl.BlockSpec(t.shape, lambda i: (0,) * t.ndim)
-    blk_spec = pl.BlockSpec((ch_block, size_a, size_b), lambda i: (i, 0, 0))
-    out = pl.pallas_call(
+    )(h, *tabs[:6])
+
+
+def long_conv(x, spectrum, gain, tabs):
+    blocks, lanes = x.shape
+    ch = gain.shape[0]
+    size_b = lanes // ch
+    g = jnp.repeat(gain, size_b)[None, :]
+    casa_h, casa_l, cbsb_h, cbsb_l, cos_t, sin_t, inv_h, inv_l = tabs
+    ctw = jnp.tile(cos_t, (1, ch))
+    stw = jnp.tile(sin_t, (1, ch))
+    return pl.pallas_call(
         _conv_body,
-        grid=(ch // ch_block,),
-        in_specs=[
-            pl.BlockSpec((ch_block, half_a, size_b), lambda i: (i, 0, 0)),
-            blk_spec,
-            blk_spec,
-            pl.BlockSpec((ch_block, 1, size_b), lambda i: (i, 0, 0)),
-        ] + [full(t) for t in tabs],
-        out_specs=pl.BlockSpec((ch_block, half_a, size_b), lambda i: (i, 0, 0)),
-        out_shape=jax.ShapeDtypeStruct((ch, half_a, size_b), jnp.bfloat16),
-    )(x, *spectrum, g, *tabs)
-    return out.reshape(ch, length)
+        out_shape=jax.ShapeDtypeStruct((blocks, lanes), jnp.bfloat16),
+    )(x, *spectrum, g, casa_h, casa_l, cbsb_h, cbsb_l, cos_t, sin_t, ctw, stw, inv_h, inv_l)
 
 
 def _proj_body(f_ref, q_ref, w_ref, s_ref, o_ref, g_scr):
@@ -305,9 +313,9 @@
     q_feat, gated_kv = featurize_kv(projected, prior_rows, feat_weight)
     tabs = conv_tables(2 * length // 256, 256)
     spectrum = filter_spectrum(long_filter, tabs)
-    kv_owned = lax.all_to_all(gated_kv, "seq", split_axis=0, concat_axis=1, tiled=True)
-    filtered = long_conv(kv_owned, spectrum, skip_gain, tabs)
-    filtered_home = lax.all_to_all(filtered, "seq", split_axis=1, concat_axis=0, tiled=True)
+    kv_owned = lax.all_to_all(gated_kv.reshape(groups, -1, tok_rows), "seq", 0, 0, tiled=True)
+    filtered = long_conv(kv_owned.reshape(groups, -1), spectrum, skip_gain, tabs)
+    filtered_home = lax.all_to_all(filtered, "seq", 0, 0, tiled=True).reshape(local_ch, tok_rows)
     n_tensor = lax.axis_size("tensor")
     scale_cols = jnp.repeat(out_scales, BLK, axis=1)
     pieces = project(filtered_home, q_feat, out_values, scale_cols, n_tensor)

time: 127 us -> 128 us (level)
  local copies, waits for them, and re-layouts: 8.1 us -> 11.5 us
  Pallas kernels: 27 us -> 24.5 us
  other arithmetic: 7.82 us -> 10 us
  starting transfers between devices: 28.6 us -> 26.6 us
    unnamed x11 -> x18, local copies, waits for them, and re-layouts: 4.04 us -> 9.26 us
    ppermute x1, waiting for transfers between devices: 3.87 us -> 0.01 us  [passed_along(): return lax.ppermute(x, axis, pairs)]
    all_to_all x2, waiting for transfers between devices: 31.7 us -> 35.4 us  [the longest x1 22.9 us: local(): lax.all_to_all(filtered, 'seq', 0, 0, tiled=True)]
    all_to_all x0 -> x2, other arithmetic: none -> 3.25 us  [local(): lax.all_to_all(filtered, 'seq', 0, 0, tiled=True)]
    pallas_call x1, Pallas kernels: 13.3 us -> 11 us  [long_conv(): pl.pallas_call(_conv_body, out_shape=jax.ShapeDtypeStruct((blocks, lanes)...]
    all_to_all x2, starting transfers between devices: 23.7 us -> 21.7 us  [the longest x1 17.3 us: local(): lax.all_to_all(gated_kv.reshape(groups, -1, tok_rows), 'seq', 0, 0, tiled...]
    pallas_call x1 -> x0, local copies, waits for them, and re-layouts: 1.8 us -> none  [long_conv(): pl.pallas_call(_conv_body, grid=(ch // ch_block,), in_specs=[pl.BlockSpec...]
  transfers between devices with their start and end apart: 3 -> 3, of which waited for: 3 -> 2; matrix products, arithmetic and copies ran while one was open for 8% -> 10% of each run, Pallas kernels for 5% -> 5%
where the time goes in v9:
time: 128 us
  waiting for transfers between devices  35.4 us (28%)
  starting transfers between devices  26.6 us (21%)
  Pallas kernels  24.5 us (19%)
  blocking collectives  19.4 us (15%)
  local copies, waits for them, and re-layouts  11.5 us (9%)
  other arithmetic  10 us (8%)
    all_to_all x1, waiting for transfers between devices, local(): lax.all_to_all(filtered, 'seq', 0, 0, tiled=True)  22.9 us
    all_to_all x1, blocking collectives, local(): gathered = lax.all_to_all(pieces, 'tensor', 0, 0, tiled=True)  19.4 us
    all_to_all x1, starting transfers between devices, local(): lax.all_to_all(gated_kv.reshape(groups, -1, tok_rows), 'seq', 0, 0, tiled...  17.3 us
    all_to_all x1, waiting for transfers between devices, local(): lax.all_to_all(gated_kv.reshape(groups, -1, tok_rows), 'seq', 0, 0, tiled...  12.5 us
    pallas_call x1, Pallas kernels, long_conv(): pl.pallas_call(_conv_body, out_shape=jax.ShapeDtypeStruct((blocks, lanes)...  11 us
    unnamed x18, local copies, waits for them, and re-layouts  9.26 us
    pallas_call x1, Pallas kernels, filter_spectrum(): pl.pallas_call(_filter_body, grid=(ch // ch_block,), in_specs=[pl.BlockSp...  5.8 us
    ppermute x1, starting transfers between devices, passed_along(): return lax.ppermute(x, axis, pairs)  4.92 us
  transfers between devices with their start and end apart: 3, of which 2 were waited for; matrix products, arithmetic and copies ran while one was open for 10% of the time, Pallas kernels for 5%

profile of v9, /device:TPU:1, one launch (start us, length us, event | category | flops | bytes accessed | tf_op | source)
XLA Modules:
  0.0 127.6 jit_solution(11498128518590633532)
XLA Ops:
  0.0 0.0 copy-start
  0.0 0.8 slice.3
  0.8 4.9 %collective-permute-start = (bf16[3,6,512]{2,1,0:T(8,128)(2,1)S(1)}, bf16[3,6,512]{2,1,0:T(8,128)(2,1)S(1)}, u32[]{:S(2)}, u32[]{:S(2)}) collective-permute-start(bf16[3,6,512]{2,1,0:T(8,128)(2,1)S(1)} %slice.3), channel_id=1, source_target_pairs={{0,8},{8,16},{16,24},{24,32},{32,40},{40,48},{48,56},{56,64},{64,7... | collective-permute-start | bytes 55304 | tf_op jit(solution)/shard_map/ppermute | solution.py:20
  5.7 0.7 broadcast_bitcast_fusion.1
  6.4 0.5 fusion.19
  6.9 0.0 copy-start.2
  7.0 0.0 copy-start.1
  7.0 2.1 %copy.17 = f32[1,8,64,256]{3,2,1,0:T(8,128)} copy(f32[1,8,64,256]{3,1,2,0:T(8,128)} %bitcast.29) | data formatting | bytes 1048576
  9.1 0.1 tile.8
  9.2 1.3 %copy.12 = f32[16,8,8,256]{3,1,2,0:T(8,128)} copy(f32[16,8,8,256]{3,2,1,0:T(8,128)S(1)} %bitcast.21) | data formatting | bytes 2097152
  10.5 0.0 copy-done.2
  10.5 0.0 copy-done.1
  10.5 0.1 tile.20
  10.6 1.3 %copy.13 = f32[16,8,8,256]{3,1,2,0:T(8,128)} copy(f32[16,8,8,256]{3,2,1,0:T(8,128)S(1)} %bitcast.22) | data formatting | bytes 2097152
  11.9 0.6 copy.11
  12.5 0.0 collective-permute-done.prior_ref
  12.5 0.0 copy-start.3
  12.5 0.6 copy-done.3
  13.1 4.0 %shard_map.64 = (bf16[512,256]{1,0:T(8,128)(2,1)}, bf16[512,256]{1,0:T(8,128)(2,1)}) custom-call(bf16[3,256,512]{2,1,0:T(8,128)(2,1)} %proj_ref.1, bf16[3,6,512]{2,1,0:T(8,128)(2,1)} %copy-done.3, f32[3,7,512]{2,1,0:T(8,128)} %w_ref.2), custom_call_target="tpu_custom_call" | custom-call | tf_op jit(solution)/shard_map/pallas_call | solution.py:118
  17.1 17.3 %all-to-all-start = ((bf16[64,8,256]{2,1,0:T(8,128)(2,1)}), bf16[64,8,256]{2,1,0:T(8,128)(2,1)S(1)}, u32[]{:S(2)}, u32[]{:S(2)}) async-start(bf16[64,8,256]{2,1,0:T(8,128)(2,1)} %bitcast.30), calls=%async_computation | async-start | bytes 524288 | tf_op jit(solution)/shard_map/all_to_all | solution.py:316
  34.4 0.3 fusion.30
  34.7 0.6 fusion.15.casa_h
  35.3 0.6 subtract_convert_fusion.1.casa_l
  36.0 1.0 fusion.12
  37.0 0.7 fusion.cbsb_h
  37.7 0.8 subtract_convert_fusion.cbsb_l
  38.5 5.8 %shard_map.65 = (f32[8,128,256]{2,1,0:T(8,128)}, f32[8,128,256]{2,1,0:T(8,128)}) custom-call(f32[8,64,256]{2,1,0:T(8,128)} %bitcast.25, bf16[256,64]{1,0:T(8,128)(2,1)} %fusion.15.casa_h, bf16[256,64]{1,0:T(8,128)(2,1)} %subtract_convert_fusion.1.casa_l, bf16[256,512]{1,0:T(8,128)(2,1)} %fusion.cbsb_h, bf16[256,512]{1,0:T(8,128)(2,1)} %subtract_convert_fusion.cbsb_l, ...), custom_call_target="tpu_custom_call" | custom-call | tf_op jit(solution)/shard_map/pallas_call | solution.py:242
  44.3 0.1 sine_negate_fusion
  44.4 0.6 fusion.24.inv_h
  45.1 0.6 subtract_convert_fusion.2.inv_l
  45.7 12.5 %all-to-all-done = bf16[64,8,256]{2,1,0:T(8,128)(2,1)S(1)} async-done(((bf16[64,8,256]{2,1,0:T(8,128)(2,1)}), bf16[64,8,256]{2,1,0:T(8,128)(2,1)S(1)}, u32[]{:S(2)}, u32[]{:S(2)}) %all-to-all-start) | async-done | bytes 262176 | tf_op jit(solution)/shard_map/all_to_all | solution.py:316
  58.2 0.8 copy.9
  58.9 11.0 %shard_map.66 = bf16[64,2048]{1,0:T(8,128)(2,1)} custom-call(bf16[64,2048]{1,0:T(8,128)(2,1)} %bitcast.27, f32[8,128,256]{2,1,0:T(8,128)} %get-tuple-element.10.fh_re_ref, f32[8,128,256]{2,1,0:T(8,128)} %get-tuple-element.11.fh_im_ref, f32[1,2048]{1,0:T(1,128)} %bitcast.32, bf16[256,64]{1,0:T(8,128)(2,1)} %fusion.15.casa_h, ...), custom_call_target="tpu_custom_call" | custom-call | tf_op jit(solution)/shard_map/pallas_call | solution.py:260
  69.9 0.5 broadcast.99
  70.4 1.7 %reduce.2 = bf16[64,2048]{1,0:T(8,128)(2,1)S(1)} reduce(bf16[64,1,2048]{2,0,1:T(8,128)(2,1)} %bitcast.26, bf16[]{:T(256)} %broadcast.99), dimensions={1}, to_apply=%copy.8.reduce_sub_computation | reduce | bytes 524290 | tf_op jit(solution)/shard_map/all_to_all | solution.py:318
  72.2 0.9 reshape.56
  73.0 4.4 %all-to-all-start.1 = ((bf16[64,2,1024]{2,1,0:T(2,128)(2,1)}), bf16[64,2,1024]{2,1,0:T(2,128)(2,1)S(1)}, u32[]{:S(2)}, u32[]{:S(2)}) async-start(bf16[64,2,1024]{2,1,0:T(2,128)(2,1)} %reshape.56), calls=%async_computation.1 | async-start | bytes 524288 | tf_op jit(solution)/shard_map/all_to_all | solution.py:318
  77.4 0.0 copy-done
  77.4 0.1 broadcast_bitcast_fusion
  77.5 0.6 copy.18
  78.1 22.9 %all-to-all-done.1 = bf16[64,2,1024]{2,1,0:T(2,128)(2,1)S(1)} async-done(((bf16[64,2,1024]{2,1,0:T(2,128)(2,1)}), bf16[64,2,1024]{2,1,0:T(2,128)(2,1)S(1)}, u32[]{:S(2)}, u32[]{:S(2)}) %all-to-all-start.1) | async-done | bytes 262176 | tf_op jit(solution)/shard_map/all_to_all | solution.py:318
  101.0 0.2 reshape.57
  101.2 1.5 %reduce.1 = bf16[64,2048]{1,0:T(8,128)(2,1)S(1)} reduce(bf16[64,1,2048]{2,1,0:T(2,128)(2,1)S(1)} %reshape.57, bf16[]{:T(256)} %constant.59), dimensions={1}, to_apply=%all_to_all.14.reduce_sub_computation | reduce | bytes 524290 | tf_op jit(solution)/shard_map/all_to_all | solution.py:318
  102.7 0.8 reshape.53.f_ref
  103.6 3.7 %shard_map.67 = bf16[8,256,256]{2,1,0:T(8,128)(2,1)} custom-call(bf16[512,256]{1,0:T(8,128)(2,1)} %reshape.53.f_ref, bf16[512,256]{1,0:T(8,128)(2,1)} %get-tuple-element.12.q_ref, bf16[512,2048]{1,0:T(8,128)(2,1)} %w_ref.3, f32[4,2048]{1,0:T(4,128)} %bitcast.31), custom_call_target="tpu_custom_call" | custom-call | tf_op jit(solution)/shard_map/pallas_call | solution.py:287
  107.3 19.4 %all_to_all.19 = bf16[8,256,256]{2,1,0:T(8,128)(2,1)S(1)} all-to-all(bf16[8,256,256]{2,1,0:T(8,128)(2,1)} %shard_map.67), channel_id=1, replica_groups=mesh['seq'=64,'tensor'=8] {'tensor'}, dimensions={0} | all-to-all | bytes 2097152 | tf_op jit(solution)/shard_map/all_to_all | solution.py:322
  126.8 0.8 reduce_sum.12
Async XLA Ops:
  0.0 77.4 %copy-start = (f32[4,16]{1,0:T(4,128)S(1)}, f32[4,16]{1,0:T(4,128)}, u32[]{:S(2)}) copy-start(f32[4,16]{1,0:T(4,128)} %param.11) | copy-start | bytes 772
  0.8 11.7 %collective-permute-start = (bf16[3,6,512]{2,1,0:T(8,128)(2,1)S(1)}, bf16[3,6,512]{2,1,0:T(8,128)(2,1)S(1)}, u32[]{:S(2)}, u32[]{:S(2)}) collective-permute-start(bf16[3,6,512]{2,1,0:T(8,128)(2,1)S(1)} %slice.3), channel_id=1, source_target_pairs={{0,8},{8,16},{16,24},{24,32},{32,40},{40,48},{48,56},{56,64},{64,7... | collective-permute-start | bytes 55304 | tf_op jit(solution)/shard_map/ppermute | solution.py:20
  6.9 3.5 %copy-start.2 = (f32[128,256]{1,0:T(8,128)}, f32[128,256]{1,0:T(8,128)S(1)}, u32[]{:S(2)}) copy-start(f32[128,256]{1,0:T(8,128)S(1)} %get-tuple-element.18.ct_ref) | copy-start | bytes 393220
  7.0 3.5 %copy-start.1 = (f32[128,256]{1,0:T(8,128)}, f32[128,256]{1,0:T(8,128)S(1)}, u32[]{:S(2)}) copy-start(f32[128,256]{1,0:T(8,128)S(1)} %get-tuple-element.17.st_ref) | copy-start | bytes 393220
  12.5 0.6 copy-start.3
  17.1 41.1 %all-to-all-start = ((bf16[64,8,256]{2,1,0:T(8,128)(2,1)}), bf16[64,8,256]{2,1,0:T(8,128)(2,1)S(1)}, u32[]{:S(2)}, u32[]{:S(2)}) async-start(bf16[64,8,256]{2,1,0:T(8,128)(2,1)} %bitcast.30), calls=%async_computation | async-start | bytes 524288 | tf_op jit(solution)/shard_map/all_to_all | solution.py:316
  73.0 27.9 %all-to-all-start.1 = ((bf16[64,2,1024]{2,1,0:T(2,128)(2,1)}), bf16[64,2,1024]{2,1,0:T(2,128)(2,1)S(1)}, u32[]{:S(2)}, u32[]{:S(2)}) async-start(bf16[64,2,1024]{2,1,0:T(2,128)(2,1)} %reshape.56), calls=%async_computation.1 | async-start | bytes 524288 | tf_op jit(solution)/shard_map/all_to_all | solution.py:318

commit v10 on v9

--- a/solution.py
+++ b/solution.py
@@ -172,23 +172,19 @@
 
 
 def _conv_body(x_ref, fh_re_ref, fh_im_ref, g_ref, casa_h, casa_l, cbsb_h, cbsb_l,
-               ct_ref, st_ref, ctw_ref, stw_ref, inv_h, inv_l, o_ref):
+               ct_ref, st_ref, inv_h, inv_l, o_ref):
     ct = ct_ref[...]
     st = st_ref[...]
     rows, width = ct.shape
     chans = fh_re_ref.shape[0]
     x_b = x_ref[...]
     a = _mm(casa_h[...], x_b) + _mm(casa_l[...], x_b)
-    ctw = ctw_ref[...]
-    stw = stw_ref[...]
-    a_re = a[:rows]
-    a_im = -a[rows:]
-    t_re = a_re * ctw + a_im * stw
-    t_im = a_im * ctw - a_re * stw
     pieces = []
     for c in range(chans):
-        pieces.append(t_re[:, c * width : (c + 1) * width])
-        pieces.append(t_im[:, c * width : (c + 1) * width])
+        a_re = a[:rows, c * width : (c + 1) * width]
+        a_im = -a[rows:, c * width : (c + 1) * width]
+        pieces.append(a_re * ct + a_im * st)
+        pieces.append(a_im * ct - a_re * st)
     r = _right3(jnp.concatenate(pieces, axis=0), cbsb_h[...], cbsb_l[...])
     prods = []
     for c in range(chans):
@@ -255,12 +251,10 @@
     size_b = lanes // ch
     g = jnp.repeat(gain, size_b)[None, :]
     casa_h, casa_l, cbsb_h, cbsb_l, cos_t, sin_t, inv_h, inv_l = tabs
-    ctw = jnp.tile(cos_t, (1, ch))
-    stw = jnp.tile(sin_t, (1, ch))
     return pl.pallas_call(
         _conv_body,
         out_shape=jax.ShapeDtypeStruct((blocks, lanes), jnp.bfloat16),
-    )(x, *spectrum, g, casa_h, casa_l, cbsb_h, cbsb_l, cos_t, sin_t, ctw, stw, inv_h, inv_l)
+    )(x, *spectrum, g, casa_h, casa_l, cbsb_h, cbsb_l, cos_t, sin_t, inv_h, inv_l)
 
 
 def _proj_body(f_ref, q_ref, w_ref, s_ref, o_ref, g_scr):
@@ -315,6 +309,7 @@
     spectrum = filter_spectrum(long_filter, tabs)
     kv_owned = lax.all_to_all(gated_kv.reshape(groups, -1, tok_rows), "seq", 0, 0, tiled=True)
     filtered = long_conv(kv_owned.reshape(groups, -1), spectrum, skip_gain, tabs)
+    filtered = filtered.reshape(groups, -1, tok_rows)
     filtered_home = lax.all_to_all(filtered, "seq", 0, 0, tiled=True).reshape(local_ch, tok_rows)
     n_tensor = lax.axis_size("tensor")
     scale_cols = jnp.repeat(out_scales, BLK, axis=1)

time: 128 us -> 121 us (0.945)
  local copies, waits for them, and re-layouts: 11.5 us -> 8.56 us
  other arithmetic: 10 us -> 7.5 us
    all_to_all x2 -> x0, other arithmetic: 3.25 us -> none  [local(): lax.all_to_all(filtered, 'seq', 0, 0, tiled=True)]
    unnamed x18 -> x13, local copies, waits for them, and re-layouts: 9.26 us -> 7.8 us
  transfers between devices with their start and end apart: 3 -> 3, of which waited for: 2 -> 3; matrix products, arithmetic and copies ran while one was open for 10% -> 9% of each run, Pallas kernels for 5% -> 5%
where the time goes in v10:
time: 121 us; the launch traced here: 120 us
  waiting for transfers between devices  34.7 us (29%)
  starting transfers between devices  26.2 us (22%)
  Pallas kernels  23.8 us (20%)
  blocking collectives  19.4 us (16%)
  local copies, waits for them, and re-layouts  8.56 us (7%)
  other arithmetic  7.5 us (6%)
    all_to_all x1, waiting for transfers between devices, local(): lax.all_to_all(filtered, 'seq', 0, 0, tiled=True)  22.9 us
    all_to_all x1, blocking collectives, local(): gathered = lax.all_to_all(pieces, 'tensor', 0, 0, tiled=True)  19.4 us
    all_to_all x1, starting transfers between devices, local(): lax.all_to_all(gated_kv.reshape(groups, -1, tok_rows), 'seq', 0, 0, tiled...  17.2 us
    all_to_all x1, waiting for transfers between devices, local(): lax.all_to_all(gated_kv.reshape(groups, -1, tok_rows), 'seq', 0, 0, tiled...  11.5 us
    pallas_call x1, Pallas kernels, long_conv(): pl.pallas_call(_conv_body, out_shape=jax.ShapeDtypeStruct((blocks, lanes)...  10.3 us
    unnamed x13, local copies, waits for them, and re-layouts  7.8 us
    pallas_call x1, Pallas kernels, filter_spectrum(): pl.pallas_call(_filter_body, grid=(ch // ch_block,), in_specs=[pl.BlockSp...  5.8 us
    ppermute x1, starting transfers between devices, passed_along(): return lax.ppermute(x, axis, pairs)  4.92 us
  transfers between devices with their start and end apart: 3, of which 3 were waited for; matrix products, arithmetic and copies ran while one was open for 9% of the time, Pallas kernels for 5%

profile of v10, /device:TPU:1, one launch (start us, length us, event | category | flops | bytes accessed | tf_op | source)
XLA Modules:
  0.0 120.3 jit_solution(14295635195616409783)
XLA Ops:
  0.0 0.0 copy-start
  0.0 0.8 slice.3
  0.8 4.9 %collective-permute-start = (bf16[3,6,512]{2,1,0:T(8,128)(2,1)S(1)}, bf16[3,6,512]{2,1,0:T(8,128)(2,1)S(1)}, u32[]{:S(2)}, u32[]{:S(2)}) collective-permute-start(bf16[3,6,512]{2,1,0:T(8,128)(2,1)S(1)} %slice.3), channel_id=1, source_target_pairs={{0,8},{8,16},{16,24},{24,32},{32,40},{40,48},{48,56},{56,64},{64,7... | collective-permute-start | bytes 55304 | tf_op jit(solution)/shard_map/ppermute | solution.py:20
  5.7 0.7 broadcast_bitcast_fusion.1
  6.4 0.3 fusion.30
  6.7 2.0 %copy.14 = f32[1,8,64,256]{3,2,1,0:T(8,128)} copy(f32[1,8,64,256]{3,1,2,0:T(8,128)} %bitcast.24) | data formatting | bytes 1048576
  8.7 0.6 copy.9
  9.3 0.2 collective-permute-done.prior_ref
  9.6 0.0 copy-start.2
  9.6 0.6 copy-done.2
  10.2 4.0 %shard_map.64 = (bf16[512,256]{1,0:T(8,128)(2,1)}, bf16[512,256]{1,0:T(8,128)(2,1)}) custom-call(bf16[3,256,512]{2,1,0:T(8,128)(2,1)} %proj_ref.1, bf16[3,6,512]{2,1,0:T(8,128)(2,1)} %copy-done.2, f32[3,7,512]{2,1,0:T(8,128)} %w_ref.2), custom_call_target="tpu_custom_call" | custom-call | tf_op jit(solution)/shard_map/pallas_call | solution.py:118
  14.2 17.2 %all-to-all-start = ((bf16[64,8,256]{2,1,0:T(8,128)(2,1)}), bf16[64,8,256]{2,1,0:T(8,128)(2,1)S(1)}, u32[]{:S(2)}, u32[]{:S(2)}) async-start(bf16[64,8,256]{2,1,0:T(8,128)(2,1)} %bitcast.25), calls=%async_computation | async-start | bytes 524288 | tf_op jit(solution)/shard_map/all_to_all | solution.py:310
  31.3 0.6 fusion.15.casa_h
  32.0 0.6 subtract_convert_fusion.1.casa_l
  32.6 1.0 fusion.12
  33.7 0.7 fusion.cbsb_h
  34.4 0.7 subtract_convert_fusion.cbsb_l
  35.1 1.2 %fusion.19 = (f32[128,256]{1,0:T(8,128)}, f32[128,256]{1,0:T(8,128)}) fusion(), kind=kLoop, calls=%fused_computation.35 | loop fusion | flops 458752 | bytes 262144 | tf_op jit(solution)/shard_map/sin | solution.py:220
  36.4 5.8 %shard_map.65 = (f32[8,128,256]{2,1,0:T(8,128)}, f32[8,128,256]{2,1,0:T(8,128)}) custom-call(f32[8,64,256]{2,1,0:T(8,128)} %bitcast.19, bf16[256,64]{1,0:T(8,128)(2,1)} %fusion.15.casa_h, bf16[256,64]{1,0:T(8,128)(2,1)} %subtract_convert_fusion.1.casa_l, bf16[256,512]{1,0:T(8,128)(2,1)} %fusion.cbsb_h, bf16[256,512]{1,0:T(8,128)(2,1)} %subtract_convert_fusion.cbsb_l, ...), custom_call_target="tpu_custom_call" | custom-call | tf_op jit(solution)/shard_map/pallas_call | solution.py:238
  42.2 0.1 sine_negate_fusion
  42.3 0.6 fusion.24.inv_h
  42.9 0.6 subtract_convert_fusion.2.inv_l
  43.5 11.5 %all-to-all-done = bf16[64,8,256]{2,1,0:T(8,128)(2,1)S(1)} async-done(((bf16[64,8,256]{2,1,0:T(8,128)(2,1)}), bf16[64,8,256]{2,1,0:T(8,128)(2,1)S(1)}, u32[]{:S(2)}, u32[]{:S(2)}) %all-to-all-start) | async-done | bytes 262176 | tf_op jit(solution)/shard_map/all_to_all | solution.py:310
  55.1 0.7 copy.7
  55.8 10.3 %shard_map.66 = bf16[64,2048]{1,0:T(8,128)(2,1)} custom-call(bf16[64,2048]{1,0:T(8,128)(2,1)} %bitcast.21, f32[8,128,256]{2,1,0:T(8,128)} %get-tuple-element.10.fh_re_ref, f32[8,128,256]{2,1,0:T(8,128)} %get-tuple-element.11.fh_im_ref, f32[1,2048]{1,0:T(1,128)} %bitcast.27, bf16[256,64]{1,0:T(8,128)(2,1)} %fusion.15.casa_h, ...), custom_call_target="tpu_custom_call" | custom-call | tf_op jit(solution)/shard_map/pallas_call | solution.py:254
  66.1 1.7 %copy.10 = bf16[8,8,8,256]{3,2,1,0:T(8,128)(2,1)} copy(bf16[8,8,8,256]{3,1,2,0:T(8,128)(2,1)} %bitcast.22) | data formatting | bytes 524288
  67.8 4.2 %all-to-all-start.1 = ((bf16[64,8,256]{2,1,0:T(8,128)(2,1)}), bf16[64,8,256]{2,1,0:T(8,128)(2,1)S(1)}, u32[]{:S(2)}, u32[]{:S(2)}) async-start(bf16[64,8,256]{2,1,0:T(8,128)(2,1)} %bitcast.10), calls=%async_computation.1 | async-start | bytes 524288 | tf_op jit(solution)/shard_map/all_to_all | solution.py:313
  72.0 0.0 copy-done
  72.0 0.1 broadcast_bitcast_fusion
  72.1 0.6 copy.15
  72.7 22.9 %all-to-all-done.1 = bf16[64,8,256]{2,1,0:T(8,128)(2,1)S(1)} async-done(((bf16[64,8,256]{2,1,0:T(8,128)(2,1)}), bf16[64,8,256]{2,1,0:T(8,128)(2,1)S(1)}, u32[]{:S(2)}, u32[]{:S(2)}) %all-to-all-start.1) | async-done | bytes 262176 | tf_op jit(solution)/shard_map/all_to_all | solution.py:313
  95.6 0.0 copy-start.1
  95.6 0.7 copy-done.1
  96.3 3.7 %shard_map.67 = bf16[8,256,256]{2,1,0:T(8,128)(2,1)} custom-call(bf16[512,256]{1,0:T(8,128)(2,1)} %bitcast.20, bf16[512,256]{1,0:T(8,128)(2,1)} %get-tuple-element.12.q_ref, bf16[512,2048]{1,0:T(8,128)(2,1)} %w_ref.3, f32[4,2048]{1,0:T(4,128)} %bitcast.26), custom_call_target="tpu_custom_call" | custom-call | tf_op jit(solution)/shard_map/pallas_call | solution.py:281
  100.0 19.4 %all_to_all.15 = bf16[8,256,256]{2,1,0:T(8,128)(2,1)S(1)} all-to-all(bf16[8,256,256]{2,1,0:T(8,128)(2,1)} %shard_map.67), channel_id=1, replica_groups=mesh['seq'=64,'tensor'=8] {'tensor'}, dimensions={0} | all-to-all | bytes 2097152 | tf_op jit(solution)/shard_map/all_to_all | solution.py:317
  119.4 0.8 reduce_sum.12
Async XLA Ops:
  0.0 72.0 %copy-start = (f32[4,16]{1,0:T(4,128)S(1)}, f32[4,16]{1,0:T(4,128)}, u32[]{:S(2)}) copy-start(f32[4,16]{1,0:T(4,128)} %param.11) | copy-start | bytes 772
  0.8 8.8 %collective-permute-start = (bf16[3,6,512]{2,1,0:T(8,128)(2,1)S(1)}, bf16[3,6,512]{2,1,0:T(8,128)(2,1)S(1)}, u32[]{:S(2)}, u32[]{:S(2)}) collective-permute-start(bf16[3,6,512]{2,1,0:T(8,128)(2,1)S(1)} %slice.3), channel_id=1, source_target_pairs={{0,8},{8,16},{16,24},{24,32},{32,40},{40,48},{48,56},{56,64},{64,7... | collective-permute-start | bytes 55304 | tf_op jit(solution)/shard_map/ppermute | solution.py:20
  9.6 0.6 copy-start.2
  14.2 40.9 %all-to-all-start = ((bf16[64,8,256]{2,1,0:T(8,128)(2,1)}), bf16[64,8,256]{2,1,0:T(8,128)(2,1)S(1)}, u32[]{:S(2)}, u32[]{:S(2)}) async-start(bf16[64,8,256]{2,1,0:T(8,128)(2,1)} %bitcast.25), calls=%async_computation | async-start | bytes 524288 | tf_op jit(solution)/shard_map/all_to_all | solution.py:310
  67.8 27.8 %all-to-all-start.1 = ((bf16[64,8,256]{2,1,0:T(8,128)(2,1)}), bf16[64,8,256]{2,1,0:T(8,128)(2,1)S(1)}, u32[]{:S(2)}, u32[]{:S(2)}) async-start(bf16[64,8,256]{2,1,0:T(8,128)(2,1)} %bitcast.10), calls=%async_computation.1 | async-start | bytes 524288 | tf_op jit(solution)/shard_map/all_to_all | solution.py:313
  95.6 0.7 copy-start.1

commit v11 on v10

--- a/solution.py
+++ b/solution.py
@@ -177,7 +177,7 @@
     st = st_ref[...]
     rows, width = ct.shape
     chans = fh_re_ref.shape[0]
-    x_b = x_ref[...]
+    x_b = jnp.concatenate([x_ref[:, c, :] for c in range(chans)], axis=1)
     a = _mm(casa_h[...], x_b) + _mm(casa_l[...], x_b)
     pieces = []
     for c in range(chans):
@@ -205,8 +205,9 @@
         w_im = z_im * ct + z_re * st
         cols.append(jnp.concatenate([w_re, w_im], axis=0))
     out = _left3(inv_h[...], inv_l[...], jnp.concatenate(cols, axis=1))
-    x_f = x_b.astype(jnp.float32)
-    o_ref[...] = (out * (1.0 / (rows * width)) + g_ref[...] * x_f).astype(jnp.bfloat16)
+    res = (out * (1.0 / (rows * width)) + g_ref[...] * x_b.astype(jnp.float32)).astype(jnp.bfloat16)
+    for c in range(chans):
+        o_ref[:, c, :] = res[:, c * width : (c + 1) * width]
 
 
 def conv_tables(size_a, size_b):
@@ -246,14 +247,12 @@
 
 
 def long_conv(x, spectrum, gain, tabs):
-    blocks, lanes = x.shape
-    ch = gain.shape[0]
-    size_b = lanes // ch
+    blocks, ch, size_b = x.shape
     g = jnp.repeat(gain, size_b)[None, :]
     casa_h, casa_l, cbsb_h, cbsb_l, cos_t, sin_t, inv_h, inv_l = tabs
     return pl.pallas_call(
         _conv_body,
-        out_shape=jax.ShapeDtypeStruct((blocks, lanes), jnp.bfloat16),
+        out_shape=jax.ShapeDtypeStruct((blocks, ch, size_b), jnp.bfloat16),
     )(x, *spectrum, g, casa_h, casa_l, cbsb_h, cbsb_l, cos_t, sin_t, inv_h, inv_l)
 
 
@@ -308,8 +307,7 @@
     tabs = conv_tables(2 * length // 256, 256)
     spectrum = filter_spectrum(long_filter, tabs)
     kv_owned = lax.all_to_all(gated_kv.reshape(groups, -1, tok_rows), "seq", 0, 0, tiled=True)
-    filtered = long_conv(kv_owned.reshape(groups, -1), spectrum, skip_gain, tabs)
-    filtered = filtered.reshape(groups, -1, tok_rows)
+    filtered = long_conv(kv_owned, spectrum, skip_gain, tabs)
     filtered_home = lax.all_to_all(filtered, "seq", 0, 0, tiled=True).reshape(local_ch, tok_rows)
     n_tensor = lax.axis_size("tensor")
     scale_cols = jnp.repeat(out_scales, BLK, axis=1)

time: 121 us -> 120 us (level)
  local copies, waits for them, and re-layouts: 8.56 us -> 6.83 us
    unnamed x13, local copies, waits for them, and re-layouts: 7.8 us -> 6.07 us
where the time goes in v11:
time: 120 us; the launch traced here: 119 us
  waiting for transfers between devices  34.6 us (29%)
  starting transfers between devices  26.3 us (22%)
  Pallas kernels  24.2 us (20%)
  blocking collectives  19.4 us (16%)
  other arithmetic  7.51 us (6%)
  local copies, waits for them, and re-layouts  6.83 us (6%)
    all_to_all x1, waiting for transfers between devices, local(): lax.all_to_all(filtered, 'seq', 0, 0, tiled=True)  22.9 us
    all_to_all x1, blocking collectives, local(): gathered = lax.all_to_all(pieces, 'tensor', 0, 0, tiled=True)  19.4 us
    all_to_all x1, starting transfers between devices, local(): lax.all_to_all(gated_kv.reshape(groups, -1, tok_rows), 'seq', 0, 0, tiled...  17.2 us
    all_to_all x1, waiting for transfers between devices, local(): lax.all_to_all(gated_kv.reshape(groups, -1, tok_rows), 'seq', 0, 0, tiled...  11.5 us
    pallas_call x1, Pallas kernels, long_conv(): pl.pallas_call(_conv_body, out_shape=jax.ShapeDtypeStruct((blocks, ch, si...  10.6 us
    unnamed x13, local copies, waits for them, and re-layouts  6.07 us
    pallas_call x1, Pallas kernels, filter_spectrum(): pl.pallas_call(_filter_body, grid=(ch // ch_block,), in_specs=[pl.BlockSp...  5.81 us
    ppermute x1, starting transfers between devices, passed_along(): return lax.ppermute(x, axis, pairs)  4.92 us
  transfers between devices with their start and end apart: 3, of which 3 were waited for; matrix products, arithmetic and copies ran while one was open for 9% of the time, Pallas kernels for 5%

profile of v11, /device:TPU:1, one launch (start us, length us, event | category | flops | bytes accessed | tf_op | source)
XLA Modules:
  0.0 118.9 jit_solution(15450616242161257717)
XLA Ops:
  0.0 0.0 copy-start
  0.0 0.8 slice.3
  0.8 4.9 %collective-permute-start = (bf16[3,6,512]{2,1,0:T(8,128)(2,1)S(1)}, bf16[3,6,512]{2,1,0:T(8,128)(2,1)S(1)}, u32[]{:S(2)}, u32[]{:S(2)}) collective-permute-start(bf16[3,6,512]{2,1,0:T(8,128)(2,1)S(1)} %slice.3), channel_id=1, source_target_pairs={{0,8},{8,16},{16,24},{24,32},{32,40},{40,48},{48,56},{56,64},{64,7... | collective-permute-start | bytes 55304 | tf_op jit(solution)/shard_map/ppermute | solution.py:20
  5.7 0.7 broadcast_bitcast_fusion.1
  6.4 0.3 fusion.30
  6.7 2.0 %copy.12 = f32[1,8,64,256]{3,2,1,0:T(8,128)} copy(f32[1,8,64,256]{3,1,2,0:T(8,128)} %bitcast.17) | data formatting | bytes 1048576
  8.7 0.6 copy.8
  9.3 0.2 collective-permute-done.prior_ref
  9.6 0.0 copy-start.3
  9.6 0.6 copy-done.3
  10.2 4.0 %shard_map.64 = (bf16[512,256]{1,0:T(8,128)(2,1)}, bf16[512,256]{1,0:T(8,128)(2,1)}) custom-call(bf16[3,256,512]{2,1,0:T(8,128)(2,1)} %proj_ref.1, bf16[3,6,512]{2,1,0:T(8,128)(2,1)} %copy-done.3, f32[3,7,512]{2,1,0:T(8,128)} %w_ref.2), custom_call_target="tpu_custom_call" | custom-call | tf_op jit(solution)/shard_map/pallas_call | solution.py:118
  14.2 17.2 %all-to-all-start = ((bf16[64,8,256]{2,1,0:T(8,128)(2,1)}), bf16[64,8,256]{2,1,0:T(8,128)(2,1)S(1)}, u32[]{:S(2)}, u32[]{:S(2)}) async-start(bf16[64,8,256]{2,1,0:T(8,128)(2,1)} %bitcast.18), calls=%async_computation | async-start | bytes 524288 | tf_op jit(solution)/shard_map/all_to_all | solution.py:309
  31.3 0.6 fusion.15.casa_h
  32.0 0.7 subtract_convert_fusion.1.casa_l
  32.6 1.0 fusion.12
  33.7 0.8 fusion.cbsb_h
  34.4 0.7 subtract_convert_fusion.cbsb_l
  35.2 1.2 %fusion.19 = (f32[128,256]{1,0:T(8,128)}, f32[128,256]{1,0:T(8,128)}) fusion(), kind=kLoop, calls=%fused_computation.35 | loop fusion | flops 458752 | bytes 262144 | tf_op jit(solution)/shard_map/sin | solution.py:221
  36.4 5.8 %shard_map.65 = (f32[8,128,256]{2,1,0:T(8,128)}, f32[8,128,256]{2,1,0:T(8,128)}) custom-call(f32[8,64,256]{2,1,0:T(8,128)} %bitcast.15, bf16[256,64]{1,0:T(8,128)(2,1)} %fusion.15.casa_h, bf16[256,64]{1,0:T(8,128)(2,1)} %subtract_convert_fusion.1.casa_l, bf16[256,512]{1,0:T(8,128)(2,1)} %fusion.cbsb_h, bf16[256,512]{1,0:T(8,128)(2,1)} %subtract_convert_fusion.cbsb_l, ...), custom_call_target="tpu_custom_call" | custom-call | tf_op jit(solution)/shard_map/pallas_call | solution.py:239
  42.2 0.1 sine_negate_fusion
  42.4 0.6 fusion.24.inv_h
  43.0 0.6 subtract_convert_fusion.2.inv_l
  43.6 11.5 %all-to-all-done.x_ref = bf16[64,8,256]{2,1,0:T(8,128)(2,1)S(1)} async-done(((bf16[64,8,256]{2,1,0:T(8,128)(2,1)}), bf16[64,8,256]{2,1,0:T(8,128)(2,1)S(1)}, u32[]{:S(2)}, u32[]{:S(2)}) %all-to-all-start) | async-done | bytes 262176 | tf_op jit(solution)/shard_map/all_to_all | solution.py:309
  55.1 0.0 copy-start.2
  55.1 0.7 copy-done.2
  55.8 10.6 %shard_map.66 = bf16[64,8,256]{2,1,0:T(8,128)(2,1)} custom-call(bf16[64,8,256]{2,1,0:T(8,128)(2,1)} %copy-done.2, f32[8,128,256]{2,1,0:T(8,128)} %get-tuple-element.10.fh_re_ref, f32[8,128,256]{2,1,0:T(8,128)} %get-tuple-element.11.fh_im_ref, f32[1,2048]{1,0:T(1,128)} %bitcast.20, bf16[256,64]{1,0:T(8,128)(2,1)} %fusion.15.casa_h, ...), custom_call_target="tpu_custom_call" | custom-call | tf_op jit(solution)/shard_map/pallas_call | solution.py:253
  66.4 4.2 %all-to-all-start.1 = ((bf16[64,8,256]{2,1,0:T(8,128)(2,1)}), bf16[64,8,256]{2,1,0:T(8,128)(2,1)S(1)}, u32[]{:S(2)}, u32[]{:S(2)}) async-start(bf16[64,8,256]{2,1,0:T(8,128)(2,1)} %shard_map.66), calls=%async_computation.1 | async-start | bytes 524288 | tf_op jit(solution)/shard_map/all_to_all | solution.py:311
  70.6 0.0 copy-done
  70.6 0.1 broadcast_bitcast_fusion
  70.7 0.6 copy.13
  71.3 22.9 %all-to-all-done.1 = bf16[64,8,256]{2,1,0:T(8,128)(2,1)S(1)} async-done(((bf16[64,8,256]{2,1,0:T(8,128)(2,1)}), bf16[64,8,256]{2,1,0:T(8,128)(2,1)S(1)}, u32[]{:S(2)}, u32[]{:S(2)}) %all-to-all-start.1) | async-done | bytes 262176 | tf_op jit(solution)/shard_map/all_to_all | solution.py:311
  94.2 0.0 copy-start.1
  94.2 0.7 copy-done.1
  94.9 3.7 %shard_map.67 = bf16[8,256,256]{2,1,0:T(8,128)(2,1)} custom-call(bf16[512,256]{1,0:T(8,128)(2,1)} %bitcast.16, bf16[512,256]{1,0:T(8,128)(2,1)} %get-tuple-element.12.q_ref, bf16[512,2048]{1,0:T(8,128)(2,1)} %w_ref.3, f32[4,2048]{1,0:T(4,128)} %bitcast.19), custom_call_target="tpu_custom_call" | custom-call | tf_op jit(solution)/shard_map/pallas_call | solution.py:280
  98.7 19.4 %all_to_all.15 = bf16[8,256,256]{2,1,0:T(8,128)(2,1)S(1)} all-to-all(bf16[8,256,256]{2,1,0:T(8,128)(2,1)} %shard_map.67), channel_id=1, replica_groups=mesh['seq'=64,'tensor'=8] {'tensor'}, dimensions={0} | all-to-all | bytes 2097152 | tf_op jit(solution)/shard_map/all_to_all | solution.py:315
  118.1 0.8 reduce_sum.12
Async XLA Ops:
  0.0 70.6 %copy-start = (f32[4,16]{1,0:T(4,128)S(1)}, f32[4,16]{1,0:T(4,128)}, u32[]{:S(2)}) copy-start(f32[4,16]{1,0:T(4,128)} %param.11) | copy-start | bytes 772
  0.8 8.8 %collective-permute-start = (bf16[3,6,512]{2,1,0:T(8,128)(2,1)S(1)}, bf16[3,6,512]{2,1,0:T(8,128)(2,1)S(1)}, u32[]{:S(2)}, u32[]{:S(2)}) collective-permute-start(bf16[3,6,512]{2,1,0:T(8,128)(2,1)S(1)} %slice.3), channel_id=1, source_target_pairs={{0,8},{8,16},{16,24},{24,32},{32,40},{40,48},{48,56},{56,64},{64,7... | collective-permute-start | bytes 55304 | tf_op jit(solution)/shard_map/ppermute | solution.py:20
  9.6 0.6 copy-start.3
  14.2 40.9 %all-to-all-start = ((bf16[64,8,256]{2,1,0:T(8,128)(2,1)}), bf16[64,8,256]{2,1,0:T(8,128)(2,1)S(1)}, u32[]{:S(2)}, u32[]{:S(2)}) async-start(bf16[64,8,256]{2,1,0:T(8,128)(2,1)} %bitcast.18), calls=%async_computation | async-start | bytes 524288 | tf_op jit(solution)/shard_map/all_to_all | solution.py:309
  55.1 0.7 copy-start.2
  66.4 27.8 %all-to-all-start.1 = ((bf16[64,8,256]{2,1,0:T(8,128)(2,1)}), bf16[64,8,256]{2,1,0:T(8,128)(2,1)S(1)}, u32[]{:S(2)}, u32[]{:S(2)}) async-start(bf16[64,8,256]{2,1,0:T(8,128)(2,1)} %shard_map.66), calls=%async_computation.1 | async-start | bytes 524288 | tf_op jit(solution)/shard_map/all_to_all | solution.py:311
  94.2 0.7 copy-start.1

commit v12 on v11

--- a/solution.py
+++ b/solution.py
@@ -152,6 +152,11 @@
     return _mm(v_hi, t_hi) + _mm(v_lo, t_hi) + _mm(v_hi, t_lo)
 
 
+def _right2(v, t_hi, t_lo):
+    v_hi = v.astype(jnp.bfloat16)
+    return _mm(v_hi, t_hi) + _mm(v_hi, t_lo)
+
+
 def _spectrum(a_re, a_im, ct, st, cbsb_h, cbsb_l):
     rows, width = ct.shape
     t_re = a_re * ct + a_im * st
@@ -185,7 +190,7 @@
         a_im = -a[rows:, c * width : (c + 1) * width]
         pieces.append(a_re * ct + a_im * st)
         pieces.append(a_im * ct - a_re * st)
-    r = _right3(jnp.concatenate(pieces, axis=0), cbsb_h[...], cbsb_l[...])
+    r = _right2(jnp.concatenate(pieces, axis=0), cbsb_h[...], cbsb_l[...])
     prods = []
     for c in range(chans):
         lo = 2 * rows * c
@@ -195,7 +200,7 @@
         fh_im = fh_im_ref[c]
         prods.append(f_re * fh_re - f_im * fh_im)
         prods.append(f_re * fh_im + f_im * fh_re)
-    q = _right3(jnp.concatenate(prods, axis=0), cbsb_h[...], cbsb_l[...])
+    q = _right2(jnp.concatenate(prods, axis=0), cbsb_h[...], cbsb_l[...])
     cols = []
     for c in range(chans):
         lo = 2 * rows * c

time: 120 us -> 117 us (0.975)
  Pallas kernels: 24.2 us -> 21.9 us
    pallas_call x1, Pallas kernels: 10.6 us -> 8.31 us  [long_conv(): pl.pallas_call(_conv_body, out_shape=jax.ShapeDtypeStruct((blocks, ch, si...]
where the time goes in v12:
time: 117 us
  waiting for transfers between devices  34.6 us (30%)
  starting transfers between devices  26.3 us (22%)
  Pallas kernels  21.9 us (19%)
  blocking collectives  19.4 us (17%)
  other arithmetic  7.51 us (6%)
  local copies, waits for them, and re-layouts  6.83 us (6%)
    all_to_all x1, waiting for transfers between devices, local(): lax.all_to_all(filtered, 'seq', 0, 0, tiled=True)  22.9 us
    all_to_all x1, blocking collectives, local(): gathered = lax.all_to_all(pieces, 'tensor', 0, 0, tiled=True)  19.4 us
    all_to_all x1, starting transfers between devices, local(): lax.all_to_all(gated_kv.reshape(groups, -1, tok_rows), 'seq', 0, 0, tiled...  17.2 us
    all_to_all x1, waiting for transfers between devices, local(): lax.all_to_all(gated_kv.reshape(groups, -1, tok_rows), 'seq', 0, 0, tiled...  11.5 us
    pallas_call x1, Pallas kernels, long_conv(): pl.pallas_call(_conv_body, out_shape=jax.ShapeDtypeStruct((blocks, ch, si...  8.31 us
    unnamed x13, local copies, waits for them, and re-layouts  6.07 us
    pallas_call x1, Pallas kernels, filter_spectrum(): pl.pallas_call(_filter_body, grid=(ch // ch_block,), in_specs=[pl.BlockSp...  5.81 us
    ppermute x1, starting transfers between devices, passed_along(): return lax.ppermute(x, axis, pairs)  4.92 us
  transfers between devices with their start and end apart: 3, of which 3 were waited for; matrix products, arithmetic and copies ran while one was open for 9% of the time, Pallas kernels for 5%

profile of v12, /device:TPU:1, one launch (start us, length us, event | category | flops | bytes accessed | tf_op | source)
XLA Modules:
  0.0 116.6 jit_solution(7021565197105506877)
XLA Ops:
  0.0 0.0 copy-start
  0.0 0.8 slice.3
  0.8 4.9 %collective-permute-start = (bf16[3,6,512]{2,1,0:T(8,128)(2,1)S(1)}, bf16[3,6,512]{2,1,0:T(8,128)(2,1)S(1)}, u32[]{:S(2)}, u32[]{:S(2)}) collective-permute-start(bf16[3,6,512]{2,1,0:T(8,128)(2,1)S(1)} %slice.3), channel_id=1, source_target_pairs={{0,8},{8,16},{16,24},{24,32},{32,40},{40,48},{48,56},{56,64},{64,7... | collective-permute-start | bytes 55304 | tf_op jit(solution)/shard_map/ppermute | solution.py:20
  5.7 0.7 broadcast_bitcast_fusion.1
  6.4 0.3 fusion.30
  6.7 2.0 %copy.12 = f32[1,8,64,256]{3,2,1,0:T(8,128)} copy(f32[1,8,64,256]{3,1,2,0:T(8,128)} %bitcast.17) | data formatting | bytes 1048576
  8.7 0.6 copy.8
  9.3 0.2 collective-permute-done.prior_ref
  9.6 0.0 copy-start.3
  9.6 0.6 copy-done.3
  10.2 4.0 %shard_map.64 = (bf16[512,256]{1,0:T(8,128)(2,1)}, bf16[512,256]{1,0:T(8,128)(2,1)}) custom-call(bf16[3,256,512]{2,1,0:T(8,128)(2,1)} %proj_ref.1, bf16[3,6,512]{2,1,0:T(8,128)(2,1)} %copy-done.3, f32[3,7,512]{2,1,0:T(8,128)} %w_ref.2), custom_call_target="tpu_custom_call" | custom-call | tf_op jit(solution)/shard_map/pallas_call | solution.py:118
  14.2 17.2 %all-to-all-start = ((bf16[64,8,256]{2,1,0:T(8,128)(2,1)}), bf16[64,8,256]{2,1,0:T(8,128)(2,1)S(1)}, u32[]{:S(2)}, u32[]{:S(2)}) async-start(bf16[64,8,256]{2,1,0:T(8,128)(2,1)} %bitcast.18), calls=%async_computation | async-start | bytes 524288 | tf_op jit(solution)/shard_map/all_to_all | solution.py:314
  31.3 0.6 fusion.15.casa_h
  32.0 0.7 subtract_convert_fusion.1.casa_l
  32.6 1.0 fusion.12
  33.7 0.8 fusion.cbsb_h
  34.4 0.7 subtract_convert_fusion.cbsb_l
  35.2 1.2 %fusion.19 = (f32[128,256]{1,0:T(8,128)}, f32[128,256]{1,0:T(8,128)}) fusion(), kind=kLoop, calls=%fused_computation.35 | loop fusion | flops 458752 | bytes 262144 | tf_op jit(solution)/shard_map/sin | solution.py:226
  36.4 5.8 %shard_map.65 = (f32[8,128,256]{2,1,0:T(8,128)}, f32[8,128,256]{2,1,0:T(8,128)}) custom-call(f32[8,64,256]{2,1,0:T(8,128)} %bitcast.15, bf16[256,64]{1,0:T(8,128)(2,1)} %fusion.15.casa_h, bf16[256,64]{1,0:T(8,128)(2,1)} %subtract_convert_fusion.1.casa_l, bf16[256,512]{1,0:T(8,128)(2,1)} %fusion.cbsb_h, bf16[256,512]{1,0:T(8,128)(2,1)} %subtract_convert_fusion.cbsb_l, ...), custom_call_target="tpu_custom_call" | custom-call | tf_op jit(solution)/shard_map/pallas_call | solution.py:244
  42.2 0.1 sine_negate_fusion
  42.4 0.6 fusion.24.inv_h
  43.0 0.6 subtract_convert_fusion.2.inv_l
  43.6 11.5 %all-to-all-done.x_ref = bf16[64,8,256]{2,1,0:T(8,128)(2,1)S(1)} async-done(((bf16[64,8,256]{2,1,0:T(8,128)(2,1)}), bf16[64,8,256]{2,1,0:T(8,128)(2,1)S(1)}, u32[]{:S(2)}, u32[]{:S(2)}) %all-to-all-start) | async-done | bytes 262176 | tf_op jit(solution)/shard_map/all_to_all | solution.py:314
  55.1 0.0 copy-start.2
  55.1 0.7 copy-done.2
  55.8 8.3 %shard_map.66 = bf16[64,8,256]{2,1,0:T(8,128)(2,1)} custom-call(bf16[64,8,256]{2,1,0:T(8,128)(2,1)} %copy-done.2, f32[8,128,256]{2,1,0:T(8,128)} %get-tuple-element.10.fh_re_ref, f32[8,128,256]{2,1,0:T(8,128)} %get-tuple-element.11.fh_im_ref, f32[1,2048]{1,0:T(1,128)} %bitcast.20, bf16[256,64]{1,0:T(8,128)(2,1)} %fusion.15.casa_h, ...), custom_call_target="tpu_custom_call" | custom-call | tf_op jit(solution)/shard_map/pallas_call | solution.py:258
  64.1 4.2 %all-to-all-start.1 = ((bf16[64,8,256]{2,1,0:T(8,128)(2,1)}), bf16[64,8,256]{2,1,0:T(8,128)(2,1)S(1)}, u32[]{:S(2)}, u32[]{:S(2)}) async-start(bf16[64,8,256]{2,1,0:T(8,128)(2,1)} %shard_map.66), calls=%async_computation.1 | async-start | bytes 524288 | tf_op jit(solution)/shard_map/all_to_all | solution.py:316
  68.3 0.0 copy-done
  68.3 0.1 broadcast_bitcast_fusion
  68.4 0.6 copy.13
  69.0 22.9 %all-to-all-done.1 = bf16[64,8,256]{2,1,0:T(8,128)(2,1)S(1)} async-done(((bf16[64,8,256]{2,1,0:T(8,128)(2,1)}), bf16[64,8,256]{2,1,0:T(8,128)(2,1)S(1)}, u32[]{:S(2)}, u32[]{:S(2)}) %all-to-all-start.1) | async-done | bytes 262176 | tf_op jit(solution)/shard_map/all_to_all | solution.py:316
  91.9 0.0 copy-start.1
  91.9 0.7 copy-done.1
  92.6 3.7 %shard_map.67 = bf16[8,256,256]{2,1,0:T(8,128)(2,1)} custom-call(bf16[512,256]{1,0:T(8,128)(2,1)} %bitcast.16, bf16[512,256]{1,0:T(8,128)(2,1)} %get-tuple-element.12.q_ref, bf16[512,2048]{1,0:T(8,128)(2,1)} %w_ref.3, f32[4,2048]{1,0:T(4,128)} %bitcast.19), custom_call_target="tpu_custom_call" | custom-call | tf_op jit(solution)/shard_map/pallas_call | solution.py:285
  96.3 19.4 %all_to_all.15 = bf16[8,256,256]{2,1,0:T(8,128)(2,1)S(1)} all-to-all(bf16[8,256,256]{2,1,0:T(8,128)(2,1)} %shard_map.67), channel_id=1, replica_groups=mesh['seq'=64,'tensor'=8] {'tensor'}, dimensions={0} | all-to-all | bytes 2097152 | tf_op jit(solution)/shard_map/all_to_all | solution.py:320
  115.8 0.8 reduce_sum.12
Async XLA Ops:
  0.0 68.3 %copy-start = (f32[4,16]{1,0:T(4,128)S(1)}, f32[4,16]{1,0:T(4,128)}, u32[]{:S(2)}) copy-start(f32[4,16]{1,0:T(4,128)} %param.11) | copy-start | bytes 772
  0.8 8.8 %collective-permute-start = (bf16[3,6,512]{2,1,0:T(8,128)(2,1)S(1)}, bf16[3,6,512]{2,1,0:T(8,128)(2,1)S(1)}, u32[]{:S(2)}, u32[]{:S(2)}) collective-permute-start(bf16[3,6,512]{2,1,0:T(8,128)(2,1)S(1)} %slice.3), channel_id=1, source_target_pairs={{0,8},{8,16},{16,24},{24,32},{32,40},{40,48},{48,56},{56,64},{64,7... | collective-permute-start | bytes 55304 | tf_op jit(solution)/shard_map/ppermute | solution.py:20
  9.6 0.6 copy-start.3
  14.2 40.9 %all-to-all-start = ((bf16[64,8,256]{2,1,0:T(8,128)(2,1)}), bf16[64,8,256]{2,1,0:T(8,128)(2,1)S(1)}, u32[]{:S(2)}, u32[]{:S(2)}) async-start(bf16[64,8,256]{2,1,0:T(8,128)(2,1)} %bitcast.18), calls=%async_computation | async-start | bytes 524288 | tf_op jit(solution)/shard_map/all_to_all | solution.py:314
  55.1 0.7 copy-start.2
  64.1 27.8 %all-to-all-start.1 = ((bf16[64,8,256]{2,1,0:T(8,128)(2,1)}), bf16[64,8,256]{2,1,0:T(8,128)(2,1)S(1)}, u32[]{:S(2)}, u32[]{:S(2)}) async-start(bf16[64,8,256]{2,1,0:T(8,128)(2,1)} %shard_map.66), calls=%async_computation.1 | async-start | bytes 524288 | tf_op jit(solution)/shard_map/all_to_all | solution.py:316
  91.9 0.7 copy-start.1

commit v13 on v12

--- a/solution.py
+++ b/solution.py
@@ -309,6 +309,7 @@
     rim_width = KS - 1
     prior_rows = passed_along(projected[:, tok_rows - rim_width :, :], "seq", 1)
     q_feat, gated_kv = featurize_kv(projected, prior_rows, feat_weight)
+    gated_kv, long_filter, skip_gain = lax.optimization_barrier((gated_kv, long_filter, skip_gain))
     tabs = conv_tables(2 * length // 256, 256)
     spectrum = filter_spectrum(long_filter, tabs)
     kv_owned = lax.all_to_all(gated_kv.reshape(groups, -1, tok_rows), "seq", 0, 0, tiled=True)

time: 117 us -> 118 us (level)
  waiting for transfers between devices: 34.6 us -> 36.5 us
  local copies, waits for them, and re-layouts: 6.83 us -> 5.15 us
    ppermute x1, waiting for transfers between devices: 0.24 us -> 2.82 us  [passed_along(): return lax.ppermute(x, axis, pairs)]
    unnamed x13 -> x17, local copies, waits for them, and re-layouts: 6.07 us -> 4.39 us
  transfers between devices with their start and end apart: 3 -> 3, of which waited for: 3 -> 3; matrix products, arithmetic and copies ran while one was open for 9% -> 8% of each run, Pallas kernels for 5% -> 5%
where the time goes in v13:
time: 118 us; the launch traced here: 117 us
  waiting for transfers between devices  36.5 us (31%)
  starting transfers between devices  26.8 us (23%)
  Pallas kernels  21.9 us (19%)
  blocking collectives  19.4 us (16%)
  other arithmetic  7.51 us (6%)
  local copies, waits for them, and re-layouts  5.15 us (4%)
    all_to_all x1, waiting for transfers between devices, local(): lax.all_to_all(filtered, 'seq', 0, 0, tiled=True)  23 us
    all_to_all x1, blocking collectives, local(): gathered = lax.all_to_all(pieces, 'tensor', 0, 0, tiled=True)  19.4 us
    all_to_all x1, starting transfers between devices, local(): lax.all_to_all(gated_kv.reshape(groups, -1, tok_rows), 'seq', 0, 0, tiled...  17.3 us
    all_to_all x1, waiting for transfers between devices, local(): lax.all_to_all(gated_kv.reshape(groups, -1, tok_rows), 'seq', 0, 0, tiled...  10.6 us
    pallas_call x1, Pallas kernels, long_conv(): pl.pallas_call(_conv_body, out_shape=jax.ShapeDtypeStruct((blocks, ch, si...  8.32 us
    pallas_call x1, Pallas kernels, filter_spectrum(): pl.pallas_call(_filter_body, grid=(ch // ch_block,), in_specs=[pl.BlockSp...  5.81 us
    ppermute x1, starting transfers between devices, passed_along(): return lax.ppermute(x, axis, pairs)  4.92 us
    all_to_all x1, starting transfers between devices, local(): lax.all_to_all(filtered, 'seq', 0, 0, tiled=True)  4.56 us
  transfers between devices with their start and end apart: 3, of which 3 were waited for; matrix products, arithmetic and copies ran while one was open for 8% of the time, Pallas kernels for 5%

profile of v13, /device:TPU:1, one launch (start us, length us, event | category | flops | bytes accessed | tf_op | source)
XLA Modules:
  0.0 117.3 jit_solution(10846173598145864741)
XLA Ops:
  0.0 0.0 copy-start
  0.0 0.8 slice.3
  0.8 4.9 %collective-permute-start = (bf16[3,6,512]{2,1,0:T(8,128)(2,1)S(1)}, bf16[3,6,512]{2,1,0:T(8,128)(2,1)S(1)}, u32[]{:S(2)}, u32[]{:S(2)}) collective-permute-start(bf16[3,6,512]{2,1,0:T(8,128)(2,1)S(1)} %slice.3), channel_id=1, source_target_pairs={{0,8},{8,16},{16,24},{24,32},{32,40},{40,48},{48,56},{56,64},{64,7... | collective-permute-start | bytes 55304 | tf_op jit(solution)/shard_map/ppermute | solution.py:20
  5.7 0.3 fusion.30
  6.0 0.1 sine_negate_fusion
  6.1 0.6 fusion.24.inv_h
  6.7 0.0 copy-start.3
  6.7 2.8 %collective-permute-done.prior_ref = bf16[3,6,512]{2,1,0:T(8,128)(2,1)S(1)} collective-permute-done((bf16[3,6,512]{2,1,0:T(8,128)(2,1)S(1)}, bf16[3,6,512]{2,1,0:T(8,128)(2,1)S(1)}, u32[]{:S(2)}, u32[]{:S(2)}) %collective-permute-start) | collective-permute-done | bytes 18464 | tf_op jit(solution)/shard_map/ppermute | solution.py:20
  9.6 0.0 copy-start.4
  9.6 0.6 copy-done.4
  10.2 4.0 %shard_map.64 = (bf16[512,256]{1,0:T(8,128)(2,1)}, bf16[512,256]{1,0:T(8,128)(2,1)}) custom-call(bf16[3,256,512]{2,1,0:T(8,128)(2,1)} %proj_ref.1, bf16[3,6,512]{2,1,0:T(8,128)(2,1)} %copy-done.4, f32[3,7,512]{2,1,0:T(8,128)} %w_ref.2), custom_call_target="tpu_custom_call" | custom-call | tf_op jit(solution)/shard_map/pallas_call | solution.py:118
  14.2 0.0 copy-start.5
  14.2 17.3 %all-to-all-start = ((bf16[64,8,256]{2,1,0:T(8,128)(2,1)}), bf16[64,8,256]{2,1,0:T(8,128)(2,1)S(1)}, u32[]{:S(2)}, u32[]{:S(2)}) async-start(bf16[64,8,256]{2,1,0:T(8,128)(2,1)} %bitcast.18), calls=%async_computation | async-start | bytes 524288 | tf_op jit(solution)/shard_map/all_to_all | solution.py:315
  31.5 0.6 subtract_convert_fusion.2.inv_l
  32.1 0.6 fusion.15.casa_h
  32.7 0.6 subtract_convert_fusion.1.casa_l
  33.4 1.0 fusion.12
  34.4 0.7 fusion.cbsb_h
  35.2 0.7 subtract_convert_fusion.cbsb_l
  35.9 1.2 %fusion.19 = (f32[128,256]{1,0:T(8,128)}, f32[128,256]{1,0:T(8,128)}) fusion(), kind=kLoop, calls=%fused_computation.35 | loop fusion | flops 458752 | bytes 262144 | tf_op jit(solution)/shard_map/sin | solution.py:226
  37.1 0.0 copy-done.3
  37.1 1.0 copy.12
  38.1 0.0 copy-done.5
  38.1 0.1 broadcast_bitcast_fusion.1
  38.2 0.6 copy.8
  38.8 5.8 %shard_map.65 = (f32[8,128,256]{2,1,0:T(8,128)}, f32[8,128,256]{2,1,0:T(8,128)}) custom-call(f32[8,64,256]{2,1,0:T(8,128)} %bitcast.15, bf16[256,64]{1,0:T(8,128)(2,1)} %fusion.15.casa_h, bf16[256,64]{1,0:T(8,128)(2,1)} %subtract_convert_fusion.1.casa_l, bf16[256,512]{1,0:T(8,128)(2,1)} %fusion.cbsb_h, bf16[256,512]{1,0:T(8,128)(2,1)} %subtract_convert_fusion.cbsb_l, ...), custom_call_target="tpu_custom_call" | custom-call | tf_op jit(solution)/shard_map/pallas_call | solution.py:244
  44.6 10.6 %all-to-all-done.x_ref = bf16[64,8,256]{2,1,0:T(8,128)(2,1)S(1)} async-done(((bf16[64,8,256]{2,1,0:T(8,128)(2,1)}), bf16[64,8,256]{2,1,0:T(8,128)(2,1)S(1)}, u32[]{:S(2)}, u32[]{:S(2)}) %all-to-all-start) | async-done | bytes 262176 | tf_op jit(solution)/shard_map/all_to_all | solution.py:315
  55.2 0.0 copy-start.2
  55.2 0.7 copy-done.2
  55.9 8.3 %shard_map.66 = bf16[64,8,256]{2,1,0:T(8,128)(2,1)} custom-call(bf16[64,8,256]{2,1,0:T(8,128)(2,1)} %copy-done.2, f32[8,128,256]{2,1,0:T(8,128)} %get-tuple-element.15.fh_re_ref, f32[8,128,256]{2,1,0:T(8,128)} %get-tuple-element.16.fh_im_ref, f32[1,2048]{1,0:T(1,128)} %bitcast.20, bf16[256,64]{1,0:T(8,128)(2,1)} %fusion.15.casa_h, ...), custom_call_target="tpu_custom_call" | custom-call | tf_op jit(solution)/shard_map/pallas_call | solution.py:258
  64.2 4.6 %all-to-all-start.1 = ((bf16[64,8,256]{2,1,0:T(8,128)(2,1)}), bf16[64,8,256]{2,1,0:T(8,128)(2,1)S(1)}, u32[]{:S(2)}, u32[]{:S(2)}) async-start(bf16[64,8,256]{2,1,0:T(8,128)(2,1)} %shard_map.66), calls=%async_computation.1 | async-start | bytes 524288 | tf_op jit(solution)/shard_map/all_to_all | solution.py:317
  68.8 0.0 copy-done
  68.8 0.1 broadcast_bitcast_fusion
  68.9 0.6 copy.13
  69.5 23.0 %all-to-all-done.1 = bf16[64,8,256]{2,1,0:T(8,128)(2,1)S(1)} async-done(((bf16[64,8,256]{2,1,0:T(8,128)(2,1)}), bf16[64,8,256]{2,1,0:T(8,128)(2,1)S(1)}, u32[]{:S(2)}, u32[]{:S(2)}) %all-to-all-start.1) | async-done | bytes 262176 | tf_op jit(solution)/shard_map/all_to_all | solution.py:317
  92.5 0.0 copy-start.1
  92.5 0.7 copy-done.1
  93.3 3.7 %shard_map.67 = bf16[8,256,256]{2,1,0:T(8,128)(2,1)} custom-call(bf16[512,256]{1,0:T(8,128)(2,1)} %bitcast.16, bf16[512,256]{1,0:T(8,128)(2,1)} %get-tuple-element.18.q_ref, bf16[512,2048]{1,0:T(8,128)(2,1)} %w_ref.3, f32[4,2048]{1,0:T(4,128)} %bitcast.19), custom_call_target="tpu_custom_call" | custom-call | tf_op jit(solution)/shard_map/pallas_call | solution.py:285
  97.0 19.4 %all_to_all.15 = bf16[8,256,256]{2,1,0:T(8,128)(2,1)S(1)} all-to-all(bf16[8,256,256]{2,1,0:T(8,128)(2,1)} %shard_map.67), channel_id=1, replica_groups=mesh['seq'=64,'tensor'=8] {'tensor'}, dimensions={0} | all-to-all | bytes 2097152 | tf_op jit(solution)/shard_map/all_to_all | solution.py:321
  116.5 0.8 reduce_sum.12
Async XLA Ops:
  0.0 68.8 %copy-start = (f32[4,16]{1,0:T(4,128)S(1)}, f32[4,16]{1,0:T(4,128)}, u32[]{:S(2)}) copy-start(f32[4,16]{1,0:T(4,128)} %param.11) | copy-start | bytes 772
  0.8 8.8 %collective-permute-start = (bf16[3,6,512]{2,1,0:T(8,128)(2,1)S(1)}, bf16[3,6,512]{2,1,0:T(8,128)(2,1)S(1)}, u32[]{:S(2)}, u32[]{:S(2)}) collective-permute-start(bf16[3,6,512]{2,1,0:T(8,128)(2,1)S(1)} %slice.3), channel_id=1, source_target_pairs={{0,8},{8,16},{16,24},{24,32},{32,40},{40,48},{48,56},{56,64},{64,7... | collective-permute-start | bytes 55304 | tf_op jit(solution)/shard_map/ppermute | solution.py:20
  6.7 30.4 %copy-start.3 = (f32[8,16384]{1,0:T(8,128)S(1)}, f32[8,16384]{1,0:T(8,128)}, u32[]{:S(2)}) copy-start(f32[8,16384]{1,0:T(8,128)} %param.8) | copy-start | bytes 1572868
  9.6 0.6 copy-start.4
  14.2 23.9 %copy-start.5 = (f32[8]{0:T(128)S(1)}, f32[8]{0:T(128)}, u32[]{:S(2)}) copy-start(f32[8]{0:T(128)} %param.9) | copy-start | bytes 100
  14.2 41.0 %all-to-all-start = ((bf16[64,8,256]{2,1,0:T(8,128)(2,1)}), bf16[64,8,256]{2,1,0:T(8,128)(2,1)S(1)}, u32[]{:S(2)}, u32[]{:S(2)}) async-start(bf16[64,8,256]{2,1,0:T(8,128)(2,1)} %bitcast.18), calls=%async_computation | async-start | bytes 524288 | tf_op jit(solution)/shard_map/all_to_all | solution.py:315
  55.2 0.7 copy-start.2
  64.2 28.3 %all-to-all-start.1 = ((bf16[64,8,256]{2,1,0:T(8,128)(2,1)}), bf16[64,8,256]{2,1,0:T(8,128)(2,1)S(1)}, u32[]{:S(2)}, u32[]{:S(2)}) async-start(bf16[64,8,256]{2,1,0:T(8,128)(2,1)} %shard_map.66), calls=%async_computation.1 | async-start | bytes 524288 | tf_op jit(solution)/shard_map/all_to_all | solution.py:317
  92.5 0.7 copy-start.1

commit v14 on v12

--- a/solution.py
+++ b/solution.py
@@ -150,6 +150,11 @@
 def _right3(v, t_hi, t_lo):
     v_hi, v_lo = _split(v)
     return _mm(v_hi, t_hi) + _mm(v_lo, t_hi) + _mm(v_hi, t_lo)
+
+
+def _left2(t_hi, t_lo, v):
+    v_hi = v.astype(jnp.bfloat16)
+    return _mm(t_hi, v_hi) + _mm(t_lo, v_hi)
 
 
 def _right2(v, t_hi, t_lo):
@@ -209,7 +214,7 @@
         w_re = z_re * ct - z_im * st
         w_im = z_im * ct + z_re * st
         cols.append(jnp.concatenate([w_re, w_im], axis=0))
-    out = _left3(inv_h[...], inv_l[...], jnp.concatenate(cols, axis=1))
+    out = _left2(inv_h[...], inv_l[...], jnp.concatenate(cols, axis=1))
     res = (out * (1.0 / (rows * width)) + g_ref[...] * x_b.astype(jnp.float32)).astype(jnp.bfloat16)
     for c in range(chans):
         o_ref[:, c, :] = res[:, c * width : (c + 1) * width]

time: 117 us -> 117 us (level)
  no operation moved by 1% of the time
where the time goes in v14:
time: 117 us; the launch traced here: 116 us
  waiting for transfers between devices  34.6 us (30%)
  starting transfers between devices  26.3 us (22%)
  Pallas kernels  21.7 us (19%)
  blocking collectives  19.4 us (17%)
  other arithmetic  7.51 us (6%)
  local copies, waits for them, and re-layouts  6.83 us (6%)
    all_to_all x1, waiting for transfers between devices, local(): lax.all_to_all(filtered, 'seq', 0, 0, tiled=True)  22.9 us
    all_to_all x1, blocking collectives, local(): gathered = lax.all_to_all(pieces, 'tensor', 0, 0, tiled=True)  19.4 us
    all_to_all x1, starting transfers between devices, local(): lax.all_to_all(gated_kv.reshape(groups, -1, tok_rows), 'seq', 0, 0, tiled...  17.2 us
    all_to_all x1, waiting for transfers between devices, local(): lax.all_to_all(gated_kv.reshape(groups, -1, tok_rows), 'seq', 0, 0, tiled...  11.5 us
    pallas_call x1, Pallas kernels, long_conv(): pl.pallas_call(_conv_body, out_shape=jax.ShapeDtypeStruct((blocks, ch, si...  8.11 us
    unnamed x13, local copies, waits for them, and re-layouts  6.07 us
    pallas_call x1, Pallas kernels, filter_spectrum(): pl.pallas_call(_filter_body, grid=(ch // ch_block,), in_specs=[pl.BlockSp...  5.81 us
    ppermute x1, starting transfers between devices, passed_along(): return lax.ppermute(x, axis, pairs)  4.92 us
  transfers between devices with their start and end apart: 3, of which 3 were waited for; matrix products, arithmetic and copies ran while one was open for 9% of the time, Pallas kernels for 5%

profile of v14, /device:TPU:1, one launch (start us, length us, event | category | flops | bytes accessed | tf_op | source)
XLA Modules:
  0.0 116.4 jit_solution(4447436482835166784)
XLA Ops:
  0.0 0.0 copy-start
  0.0 0.8 slice.3
  0.8 4.9 %collective-permute-start = (bf16[3,6,512]{2,1,0:T(8,128)(2,1)S(1)}, bf16[3,6,512]{2,1,0:T(8,128)(2,1)S(1)}, u32[]{:S(2)}, u32[]{:S(2)}) collective-permute-start(bf16[3,6,512]{2,1,0:T(8,128)(2,1)S(1)} %slice.3), channel_id=1, source_target_pairs={{0,8},{8,16},{16,24},{24,32},{32,40},{40,48},{48,56},{56,64},{64,7... | collective-permute-start | bytes 55304 | tf_op jit(solution)/shard_map/ppermute | solution.py:20
  5.7 0.7 broadcast_bitcast_fusion.1
  6.4 0.3 fusion.30
  6.7 2.0 %copy.12 = f32[1,8,64,256]{3,2,1,0:T(8,128)} copy(f32[1,8,64,256]{3,1,2,0:T(8,128)} %bitcast.17) | data formatting | bytes 1048576
  8.7 0.6 copy.8
  9.3 0.2 collective-permute-done.prior_ref
  9.6 0.0 copy-start.3
  9.6 0.6 copy-done.3
  10.2 4.0 %shard_map.64 = (bf16[512,256]{1,0:T(8,128)(2,1)}, bf16[512,256]{1,0:T(8,128)(2,1)}) custom-call(bf16[3,256,512]{2,1,0:T(8,128)(2,1)} %proj_ref.1, bf16[3,6,512]{2,1,0:T(8,128)(2,1)} %copy-done.3, f32[3,7,512]{2,1,0:T(8,128)} %w_ref.2), custom_call_target="tpu_custom_call" | custom-call | tf_op jit(solution)/shard_map/pallas_call | solution.py:118
  14.2 17.2 %all-to-all-start = ((bf16[64,8,256]{2,1,0:T(8,128)(2,1)}), bf16[64,8,256]{2,1,0:T(8,128)(2,1)S(1)}, u32[]{:S(2)}, u32[]{:S(2)}) async-start(bf16[64,8,256]{2,1,0:T(8,128)(2,1)} %bitcast.18), calls=%async_computation | async-start | bytes 524288 | tf_op jit(solution)/shard_map/all_to_all | solution.py:319
  31.3 0.6 fusion.15.casa_h
  32.0 0.7 subtract_convert_fusion.1.casa_l
  32.6 1.0 fusion.12
  33.7 0.8 fusion.cbsb_h
  34.4 0.7 subtract_convert_fusion.cbsb_l
  35.2 1.2 %fusion.19 = (f32[128,256]{1,0:T(8,128)}, f32[128,256]{1,0:T(8,128)}) fusion(), kind=kLoop, calls=%fused_computation.35 | loop fusion | flops 458752 | bytes 262144 | tf_op jit(solution)/shard_map/sin | solution.py:231
  36.4 5.8 %shard_map.65 = (f32[8,128,256]{2,1,0:T(8,128)}, f32[8,128,256]{2,1,0:T(8,128)}) custom-call(f32[8,64,256]{2,1,0:T(8,128)} %bitcast.15, bf16[256,64]{1,0:T(8,128)(2,1)} %fusion.15.casa_h, bf16[256,64]{1,0:T(8,128)(2,1)} %subtract_convert_fusion.1.casa_l, bf16[256,512]{1,0:T(8,128)(2,1)} %fusion.cbsb_h, bf16[256,512]{1,0:T(8,128)(2,1)} %subtract_convert_fusion.cbsb_l, ...), custom_call_target="tpu_custom_call" | custom-call | tf_op jit(solution)/shard_map/pallas_call | solution.py:249
  42.2 0.1 sine_negate_fusion
  42.4 0.6 fusion.24.inv_h
  43.0 0.6 subtract_convert_fusion.2.inv_l
  43.6 11.5 %all-to-all-done.x_ref = bf16[64,8,256]{2,1,0:T(8,128)(2,1)S(1)} async-done(((bf16[64,8,256]{2,1,0:T(8,128)(2,1)}), bf16[64,8,256]{2,1,0:T(8,128)(2,1)S(1)}, u32[]{:S(2)}, u32[]{:S(2)}) %all-to-all-start) | async-done | bytes 262176 | tf_op jit(solution)/shard_map/all_to_all | solution.py:319
  55.1 0.0 copy-start.2
  55.1 0.7 copy-done.2
  55.8 8.1 %shard_map.66 = bf16[64,8,256]{2,1,0:T(8,128)(2,1)} custom-call(bf16[64,8,256]{2,1,0:T(8,128)(2,1)} %copy-done.2, f32[8,128,256]{2,1,0:T(8,128)} %get-tuple-element.10.fh_re_ref, f32[8,128,256]{2,1,0:T(8,128)} %get-tuple-element.11.fh_im_ref, f32[1,2048]{1,0:T(1,128)} %bitcast.20, bf16[256,64]{1,0:T(8,128)(2,1)} %fusion.15.casa_h, ...), custom_call_target="tpu_custom_call" | custom-call | tf_op jit(solution)/shard_map/pallas_call | solution.py:263
  63.9 4.2 %all-to-all-start.1 = ((bf16[64,8,256]{2,1,0:T(8,128)(2,1)}), bf16[64,8,256]{2,1,0:T(8,128)(2,1)S(1)}, u32[]{:S(2)}, u32[]{:S(2)}) async-start(bf16[64,8,256]{2,1,0:T(8,128)(2,1)} %shard_map.66), calls=%async_computation.1 | async-start | bytes 524288 | tf_op jit(solution)/shard_map/all_to_all | solution.py:321
  68.1 0.0 copy-done
  68.1 0.1 broadcast_bitcast_fusion
  68.2 0.6 copy.13
  68.8 22.9 %all-to-all-done.1 = bf16[64,8,256]{2,1,0:T(8,128)(2,1)S(1)} async-done(((bf16[64,8,256]{2,1,0:T(8,128)(2,1)}), bf16[64,8,256]{2,1,0:T(8,128)(2,1)S(1)}, u32[]{:S(2)}, u32[]{:S(2)}) %all-to-all-start.1) | async-done | bytes 262176 | tf_op jit(solution)/shard_map/all_to_all | solution.py:321
  91.7 0.0 copy-start.1
  91.7 0.7 copy-done.1
  92.4 3.7 %shard_map.67 = bf16[8,256,256]{2,1,0:T(8,128)(2,1)} custom-call(bf16[512,256]{1,0:T(8,128)(2,1)} %bitcast.16, bf16[512,256]{1,0:T(8,128)(2,1)} %get-tuple-element.12.q_ref, bf16[512,2048]{1,0:T(8,128)(2,1)} %w_ref.3, f32[4,2048]{1,0:T(4,128)} %bitcast.19), custom_call_target="tpu_custom_call" | custom-call | tf_op jit(solution)/shard_map/pallas_call | solution.py:290
  96.1 19.4 %all_to_all.15 = bf16[8,256,256]{2,1,0:T(8,128)(2,1)S(1)} all-to-all(bf16[8,256,256]{2,1,0:T(8,128)(2,1)} %shard_map.67), channel_id=1, replica_groups=mesh['seq'=64,'tensor'=8] {'tensor'}, dimensions={0} | all-to-all | bytes 2097152 | tf_op jit(solution)/shard_map/all_to_all | solution.py:325
  115.5 0.8 reduce_sum.12
Async XLA Ops:
  0.0 68.1 %copy-start = (f32[4,16]{1,0:T(4,128)S(1)}, f32[4,16]{1,0:T(4,128)}, u32[]{:S(2)}) copy-start(f32[4,16]{1,0:T(4,128)} %param.11) | copy-start | bytes 772
  0.8 8.8 %collective-permute-start = (bf16[3,6,512]{2,1,0:T(8,128)(2,1)S(1)}, bf16[3,6,512]{2,1,0:T(8,128)(2,1)S(1)}, u32[]{:S(2)}, u32[]{:S(2)}) collective-permute-start(bf16[3,6,512]{2,1,0:T(8,128)(2,1)S(1)} %slice.3), channel_id=1, source_target_pairs={{0,8},{8,16},{16,24},{24,32},{32,40},{40,48},{48,56},{56,64},{64,7... | collective-permute-start | bytes 55304 | tf_op jit(solution)/shard_map/ppermute | solution.py:20
  9.6 0.6 copy-start.3
  14.2 40.9 %all-to-all-start = ((bf16[64,8,256]{2,1,0:T(8,128)(2,1)}), bf16[64,8,256]{2,1,0:T(8,128)(2,1)S(1)}, u32[]{:S(2)}, u32[]{:S(2)}) async-start(bf16[64,8,256]{2,1,0:T(8,128)(2,1)} %bitcast.18), calls=%async_computation | async-start | bytes 524288 | tf_op jit(solution)/shard_map/all_to_all | solution.py:319
  55.1 0.7 copy-start.2
  63.9 27.8 %all-to-all-start.1 = ((bf16[64,8,256]{2,1,0:T(8,128)(2,1)}), bf16[64,8,256]{2,1,0:T(8,128)(2,1)S(1)}, u32[]{:S(2)}, u32[]{:S(2)}) async-start(bf16[64,8,256]{2,1,0:T(8,128)(2,1)} %shard_map.66), calls=%async_computation.1 | async-start | bytes 524288 | tf_op jit(solution)/shard_map/all_to_all | solution.py:321
  91.7 0.7 copy-start.1

commit v15 on v12

--- a/solution.py
+++ b/solution.py
@@ -316,9 +316,14 @@
     filtered_home = lax.all_to_all(filtered, "seq", 0, 0, tiled=True).reshape(local_ch, tok_rows)
     n_tensor = lax.axis_size("tensor")
     scale_cols = jnp.repeat(out_scales, BLK, axis=1)
-    pieces = project(filtered_home, q_feat, out_values, scale_cols, n_tensor)
-    gathered = lax.all_to_all(pieces, "tensor", 0, 0, tiled=True)
-    return jnp.sum(gathered.astype(jnp.float32), axis=0).astype(jnp.bfloat16)
+    half = tok_rows // 2
+    outs = []
+    for h in range(2):
+        cols = slice(h * half, (h + 1) * half)
+        pieces = project(filtered_home[:, cols], q_feat[:, cols], out_values, scale_cols, n_tensor)
+        gathered = lax.all_to_all(pieces, "tensor", 0, 0, tiled=True)
+        outs.append(jnp.sum(gathered.astype(jnp.float32), axis=0).astype(jnp.bfloat16))
+    return jnp.concatenate(outs, axis=0)
 
 
 def solution(mesh):

time: 117 us -> 123 us (1.051)
  blocking collectives: 19.4 us -> 0 us
  waiting for transfers between devices: 34.6 us -> 48 us
  starting transfers between devices: 26.3 us -> 34.5 us
  Pallas kernels: 21.9 us -> 24.1 us
    all_to_all x1 -> x0, blocking collectives: 19.4 us -> none  [local(): gathered = lax.all_to_all(pieces, 'tensor', 0, 0, tiled=True)]
    all_to_all x0 -> x2, waiting for transfers between devices: none -> 14.1 us  [local(): gathered = lax.all_to_all(pieces, 'tensor', 0, 0, tiled=True)]
    all_to_all x0 -> x2, starting transfers between devices: none -> 8.28 us  [local(): gathered = lax.all_to_all(pieces, 'tensor', 0, 0, tiled=True)]
    pallas_call x1 -> x2, Pallas kernels: 3.74 us -> 6 us  [project(): pl.pallas_call(_proj_body, grid=(steps,), in_specs=[pl.BlockSpec((chans,...]
    slice x0 -> x2, local copies, waits for them, and re-layouts: none -> 1.43 us  [the longest x1 0.72 us: local(): q_feat[:, cols]]
  transfers between devices with their start and end apart: 3 -> 5, of which waited for: 3 -> 5; matrix products, arithmetic and copies ran while one was open for 9% -> 10% of each run, Pallas kernels for 5% -> 7%
where the time goes in v15:
time: 123 us; the launch traced here: 122 us
  waiting for transfers between devices  48 us (39%)
  starting transfers between devices  34.5 us (28%)
  Pallas kernels  24.1 us (20%)
  other arithmetic  7.56 us (6%)
  local copies, waits for them, and re-layouts  7.54 us (6%)
    all_to_all x1, waiting for transfers between devices, local(): lax.all_to_all(filtered, 'seq', 0, 0, tiled=True)  22.2 us
    all_to_all x1, starting transfers between devices, local(): lax.all_to_all(gated_kv.reshape(groups, -1, tok_rows), 'seq', 0, 0, tiled...  17.2 us
    all_to_all x2, waiting for transfers between devices, local(): gathered = lax.all_to_all(pieces, 'tensor', 0, 0, tiled=True)  14.1 us
    all_to_all x1, waiting for transfers between devices, local(): lax.all_to_all(gated_kv.reshape(groups, -1, tok_rows), 'seq', 0, 0, tiled...  11.5 us
    pallas_call x1, Pallas kernels, long_conv(): pl.pallas_call(_conv_body, out_shape=jax.ShapeDtypeStruct((blocks, ch, si...  8.36 us
    all_to_all x2, starting transfers between devices, local(): gathered = lax.all_to_all(pieces, 'tensor', 0, 0, tiled=True)  8.28 us
    pallas_call x2, Pallas kernels, project(): pl.pallas_call(_proj_body, grid=(steps,), in_specs=[pl.BlockSpec((chans,...  6 us
    pallas_call x1, Pallas kernels, filter_spectrum(): pl.pallas_call(_filter_body, grid=(ch // ch_block,), in_specs=[pl.BlockSp...  5.78 us
  transfers between devices with their start and end apart: 5, of which 5 were waited for; matrix products, arithmetic and copies ran while one was open for 10% of the time, Pallas kernels for 7%

profile of v15, /device:TPU:1, one launch (start us, length us, event | category | flops | bytes accessed | tf_op | source)
XLA Modules:
  0.0 121.8 jit_solution(13584975737773068352)
XLA Ops:
  0.0 0.0 copy-start
  0.0 0.8 slice.15
  0.8 4.9 %collective-permute-start = (bf16[3,6,512]{2,1,0:T(8,128)(2,1)S(1)}, bf16[3,6,512]{2,1,0:T(8,128)(2,1)S(1)}, u32[]{:S(2)}, u32[]{:S(2)}) collective-permute-start(bf16[3,6,512]{2,1,0:T(8,128)(2,1)S(1)} %slice.15), channel_id=1, source_target_pairs={{0,8},{8,16},{16,24},{24,32},{32,40},{40,48},{48,56},{56,64},{64,7... | collective-permute-start | bytes 55304 | tf_op jit(solution)/shard_map/ppermute | solution.py:20
  5.7 0.7 broadcast_bitcast_fusion.1
  6.4 0.3 fusion.30
  6.7 2.0 %copy.12 = f32[1,8,64,256]{3,2,1,0:T(8,128)} copy(f32[1,8,64,256]{3,1,2,0:T(8,128)} %bitcast.17) | data formatting | bytes 1048576
  8.7 0.6 copy.8
  9.3 0.2 collective-permute-done.prior_ref
  9.6 0.0 copy-start.3
  9.6 0.6 copy-done.3
  10.2 4.0 %shard_map.64 = (bf16[512,256]{1,0:T(8,128)(2,1)}, bf16[512,256]{1,0:T(8,128)(2,1)}) custom-call(bf16[3,256,512]{2,1,0:T(8,128)(2,1)} %proj_ref.1, bf16[3,6,512]{2,1,0:T(8,128)(2,1)} %copy-done.3, f32[3,7,512]{2,1,0:T(8,128)} %w_ref.3), custom_call_target="tpu_custom_call" | custom-call | tf_op jit(solution)/shard_map/pallas_call | solution.py:118
  14.2 17.2 %all-to-all-start = ((bf16[64,8,256]{2,1,0:T(8,128)(2,1)}), bf16[64,8,256]{2,1,0:T(8,128)(2,1)S(1)}, u32[]{:S(2)}, u32[]{:S(2)}) async-start(bf16[64,8,256]{2,1,0:T(8,128)(2,1)} %bitcast.20), calls=%async_computation | async-start | bytes 524288 | tf_op jit(solution)/shard_map/all_to_all | solution.py:314
  31.3 0.6 fusion.15.casa_h
  32.0 0.6 subtract_convert_fusion.1.casa_l
  32.6 1.0 fusion.12
  33.6 0.8 fusion.cbsb_h
  34.4 0.7 subtract_convert_fusion.cbsb_l
  35.2 1.2 %fusion.19 = (f32[128,256]{1,0:T(8,128)}, f32[128,256]{1,0:T(8,128)}) fusion(), kind=kLoop, calls=%fused_computation.36 | loop fusion | flops 458752 | bytes 262144 | tf_op jit(solution)/shard_map/sin | solution.py:226
  36.4 5.8 %shard_map.65 = (f32[8,128,256]{2,1,0:T(8,128)}, f32[8,128,256]{2,1,0:T(8,128)}) custom-call(f32[8,64,256]{2,1,0:T(8,128)} %bitcast.15, bf16[256,64]{1,0:T(8,128)(2,1)} %fusion.15.casa_h, bf16[256,64]{1,0:T(8,128)(2,1)} %subtract_convert_fusion.1.casa_l, bf16[256,512]{1,0:T(8,128)(2,1)} %fusion.cbsb_h, bf16[256,512]{1,0:T(8,128)(2,1)} %subtract_convert_fusion.cbsb_l, ...), custom_call_target="tpu_custom_call" | custom-call | tf_op jit(solution)/shard_map/pallas_call | solution.py:244
  42.2 0.1 sine_negate_fusion
  42.3 0.6 fusion.24.inv_h
  43.0 0.6 subtract_convert_fusion.2.inv_l
  43.6 11.5 %all-to-all-done.x_ref = bf16[64,8,256]{2,1,0:T(8,128)(2,1)S(1)} async-done(((bf16[64,8,256]{2,1,0:T(8,128)(2,1)}), bf16[64,8,256]{2,1,0:T(8,128)(2,1)S(1)}, u32[]{:S(2)}, u32[]{:S(2)}) %all-to-all-start) | async-done | bytes 262176 | tf_op jit(solution)/shard_map/all_to_all | solution.py:314
  55.1 0.0 copy-start.1
  55.1 0.7 copy-done.1
  55.8 0.0 copy-start.2
  55.8 8.4 %shard_map.66 = bf16[64,8,256]{2,1,0:T(8,128)(2,1)} custom-call(bf16[64,8,256]{2,1,0:T(8,128)(2,1)} %copy-done.1, f32[8,128,256]{2,1,0:T(8,128)} %get-tuple-element.10.fh_re_ref, f32[8,128,256]{2,1,0:T(8,128)} %get-tuple-element.11.fh_im_ref, f32[1,2048]{1,0:T(1,128)} %bitcast.21, bf16[256,64]{1,0:T(8,128)(2,1)} %fusion.15.casa_h, ...), custom_call_target="tpu_custom_call" | custom-call | tf_op jit(solution)/shard_map/pallas_call | solution.py:258
  64.1 4.2 %all-to-all-start.1 = ((bf16[64,8,256]{2,1,0:T(8,128)(2,1)}), bf16[64,8,256]{2,1,0:T(8,128)(2,1)S(1)}, u32[]{:S(2)}, u32[]{:S(2)}) async-start(bf16[64,8,256]{2,1,0:T(8,128)(2,1)} %shard_map.66), calls=%async_computation.1 | async-start | bytes 524288 | tf_op jit(solution)/shard_map/all_to_all | solution.py:316
  68.3 0.0 copy-done
  68.3 0.1 broadcast_bitcast_fusion
  68.4 0.6 copy.13
  69.0 0.0 copy-done.2
  69.0 0.7 fusion.34
  69.7 22.2 %all-to-all-done.1 = bf16[64,8,256]{2,1,0:T(8,128)(2,1)S(1)} async-done(((bf16[64,8,256]{2,1,0:T(8,128)(2,1)}), bf16[64,8,256]{2,1,0:T(8,128)(2,1)S(1)}, u32[]{:S(2)}, u32[]{:S(2)}) %all-to-all-start.1) | async-done | bytes 262176 | tf_op jit(solution)/shard_map/all_to_all | solution.py:316
  91.9 0.7 fusion.35
  92.6 3.0 %shard_map.67 = bf16[8,128,256]{2,1,0:T(8,128)(2,1)} custom-call(bf16[512,128]{1,0:T(8,128)(2,1)} %get-tuple-element.15.f_ref, bf16[512,128]{1,0:T(8,128)(2,1)} %get-tuple-element.13.q_ref, bf16[512,2048]{1,0:T(8,128)(2,1)} %w_ref.5, f32[4,2048]{1,0:T(4,128)} %bitcast.18), custom_call_target="tpu_custom_call" | custom-call | tf_op jit(solution)/shard_map/pallas_call | solution.py:285
  95.6 4.2 %all-to-all-start.2 = ((bf16[8,128,256]{2,1,0:T(8,128)(2,1)}), bf16[8,128,256]{2,1,0:T(8,128)(2,1)S(1)}, u32[]{:S(2)}, u32[]{:S(2)}) async-start(bf16[8,128,256]{2,1,0:T(8,128)(2,1)} %shard_map.67), calls=%async_computation.2 | async-start | bytes 1048576 | tf_op jit(solution)/shard_map/all_to_all | solution.py:324
  99.9 3.0 %shard_map.68 = bf16[8,128,256]{2,1,0:T(8,128)(2,1)} custom-call(bf16[512,128]{1,0:T(8,128)(2,1)} %get-tuple-element.16.f_ref, bf16[512,128]{1,0:T(8,128)(2,1)} %get-tuple-element.14.q_ref, bf16[512,2048]{1,0:T(8,128)(2,1)} %w_ref.5, f32[4,2048]{1,0:T(4,128)} %bitcast.19), custom_call_target="tpu_custom_call" | custom-call | tf_op jit(solution)/shard_map/pallas_call | solution.py:285
  102.8 6.0 %all-to-all-done.2 = bf16[8,128,256]{2,1,0:T(8,128)(2,1)S(1)} async-done(((bf16[8,128,256]{2,1,0:T(8,128)(2,1)}), bf16[8,128,256]{2,1,0:T(8,128)(2,1)S(1)}, u32[]{:S(2)}, u32[]{:S(2)}) %all-to-all-start.2) | async-done | bytes 524320 | tf_op jit(solution)/shard_map/all_to_all | solution.py:324
  108.9 4.0 %all-to-all-start.3 = ((bf16[8,128,256]{2,1,0:T(8,128)(2,1)}), bf16[8,128,256]{2,1,0:T(8,128)(2,1)S(1)}, u32[]{:S(2)}, u32[]{:S(2)}) async-start(bf16[8,128,256]{2,1,0:T(8,128)(2,1)} %shard_map.68), calls=%async_computation.3 | async-start | bytes 1048576 | tf_op jit(solution)/shard_map/all_to_all | solution.py:324
  112.9 0.1 reduce_sum.24
  113.0 8.1 %all-to-all-done.3 = bf16[8,128,256]{2,1,0:T(8,128)(2,1)S(1)} async-done(((bf16[8,128,256]{2,1,0:T(8,128)(2,1)}), bf16[8,128,256]{2,1,0:T(8,128)(2,1)S(1)}, u32[]{:S(2)}, u32[]{:S(2)}) %all-to-all-start.3) | async-done | bytes 524320 | tf_op jit(solution)/shard_map/all_to_all | solution.py:324
  121.1 0.1 reduce_sum.25
  121.2 0.7 pad_maximum_fusion.2
Async XLA Ops:
  0.0 68.3 %copy-start = (f32[4,16]{1,0:T(4,128)S(1)}, f32[4,16]{1,0:T(4,128)}, u32[]{:S(2)}) copy-start(f32[4,16]{1,0:T(4,128)} %param.11) | copy-start | bytes 772
  0.8 8.8 %collective-permute-start = (bf16[3,6,512]{2,1,0:T(8,128)(2,1)S(1)}, bf16[3,6,512]{2,1,0:T(8,128)(2,1)S(1)}, u32[]{:S(2)}, u32[]{:S(2)}) collective-permute-start(bf16[3,6,512]{2,1,0:T(8,128)(2,1)S(1)} %slice.15), channel_id=1, source_target_pairs={{0,8},{8,16},{16,24},{24,32},{32,40},{40,48},{48,56},{56,64},{64,7... | collective-permute-start | bytes 55304 | tf_op jit(solution)/shard_map/ppermute | solution.py:20
  9.6 0.6 copy-start.3
  14.2 40.9 %all-to-all-start = ((bf16[64,8,256]{2,1,0:T(8,128)(2,1)}), bf16[64,8,256]{2,1,0:T(8,128)(2,1)S(1)}, u32[]{:S(2)}, u32[]{:S(2)}) async-start(bf16[64,8,256]{2,1,0:T(8,128)(2,1)} %bitcast.20), calls=%async_computation | async-start | bytes 524288 | tf_op jit(solution)/shard_map/all_to_all | solution.py:314
  55.1 0.7 copy-start.1
  55.8 13.2 %copy-start.2 = (bf16[512,256]{1,0:T(8,128)(2,1)S(1)}, bf16[512,256]{1,0:T(8,128)(2,1)}, u32[]{:S(2)}) copy-start(bf16[512,256]{1,0:T(8,128)(2,1)} %get-tuple-element.12) | copy-start | bytes 786436
  64.1 27.8 %all-to-all-start.1 = ((bf16[64,8,256]{2,1,0:T(8,128)(2,1)}), bf16[64,8,256]{2,1,0:T(8,128)(2,1)S(1)}, u32[]{:S(2)}, u32[]{:S(2)}) async-start(bf16[64,8,256]{2,1,0:T(8,128)(2,1)} %shard_map.66), calls=%async_computation.1 | async-start | bytes 524288 | tf_op jit(solution)/shard_map/all_to_all | solution.py:316
  95.6 13.3 %all-to-all-start.2 = ((bf16[8,128,256]{2,1,0:T(8,128)(2,1)}), bf16[8,128,256]{2,1,0:T(8,128)(2,1)S(1)}, u32[]{:S(2)}, u32[]{:S(2)}) async-start(bf16[8,128,256]{2,1,0:T(8,128)(2,1)} %shard_map.67), calls=%async_computation.2 | async-start | bytes 1048576 | tf_op jit(solution)/shard_map/all_to_all | solution.py:324
  108.9 12.2 %all-to-all-start.3 = ((bf16[8,128,256]{2,1,0:T(8,128)(2,1)}), bf16[8,128,256]{2,1,0:T(8,128)(2,1)S(1)}, u32[]{:S(2)}, u32[]{:S(2)}) async-start(bf16[8,128,256]{2,1,0:T(8,128)(2,1)} %shard_map.68), calls=%async_computation.3 | async-start | bytes 1048576 | tf_op jit(solution)/shard_map/all_to_all | solution.py:324

commit v16 on v12

--- a/solution.py
+++ b/solution.py
@@ -176,13 +176,14 @@
         re_ref[c], im_ref[c] = _spectrum(a[:rows], -a[rows:], ct, st, cbsb_h[...], cbsb_l[...])
 
 
-def _conv_body(x_ref, fh_re_ref, fh_im_ref, g_ref, casa_h, casa_l, cbsb_h, cbsb_l,
+def _conv_half(first, x_ref, fh_re_ref, fh_im_ref, g_ref, casa_h, casa_l, cbsb_h, cbsb_l,
                ct_ref, st_ref, inv_h, inv_l, o_ref):
     ct = ct_ref[...]
     st = st_ref[...]
     rows, width = ct.shape
     chans = fh_re_ref.shape[0]
-    x_b = jnp.concatenate([x_ref[:, c, :] for c in range(chans)], axis=1)
+    chan_ids = range(first, first + chans)
+    x_b = jnp.concatenate([x_ref[:, c, :] for c in chan_ids], axis=1)
     a = _mm(casa_h[...], x_b) + _mm(casa_l[...], x_b)
     pieces = []
     for c in range(chans):
@@ -210,9 +211,15 @@
         w_im = z_im * ct + z_re * st
         cols.append(jnp.concatenate([w_re, w_im], axis=0))
     out = _left3(inv_h[...], inv_l[...], jnp.concatenate(cols, axis=1))
-    res = (out * (1.0 / (rows * width)) + g_ref[...] * x_b.astype(jnp.float32)).astype(jnp.bfloat16)
+    res = (out * (1.0 / (rows * width)) + g_ref[:, first * width : (first + chans) * width] * x_b.astype(jnp.float32)).astype(jnp.bfloat16)
     for c in range(chans):
-        o_ref[:, c, :] = res[:, c * width : (c + 1) * width]
+        o_ref[:, first + c, :] = res[:, c * width : (c + 1) * width]
+
+
+def _conv_body(*refs):
+    half = refs[1].shape[0]
+    for step in range(2):
+        pl.when(pl.program_id(0) == step)(lambda step=step: _conv_half(step * half, *refs))
 
 
 def conv_tables(size_a, size_b):
@@ -255,10 +262,16 @@
     blocks, ch, size_b = x.shape
     g = jnp.repeat(gain, size_b)[None, :]
     casa_h, casa_l, cbsb_h, cbsb_l, cos_t, sin_t, inv_h, inv_l = tabs
+    tables = (casa_h, casa_l, cbsb_h, cbsb_l, cos_t, sin_t, inv_h, inv_l)
+    full = lambda t: pl.BlockSpec(t.shape, lambda i: (0,) * t.ndim)
+    half = pl.BlockSpec((ch // 2,) + spectrum[0].shape[1:], lambda i: (i, 0, 0))
     return pl.pallas_call(
         _conv_body,
+        grid=(2,),
+        in_specs=[full(x), half, half, full(g)] + [full(t) for t in tables],
+        out_specs=pl.BlockSpec((blocks, ch, size_b), lambda i: (0, 0, 0)),
         out_shape=jax.ShapeDtypeStruct((blocks, ch, size_b), jnp.bfloat16),
-    )(x, *spectrum, g, casa_h, casa_l, cbsb_h, cbsb_l, cos_t, sin_t, inv_h, inv_l)
+    )(x, *spectrum, g, *tables)
 
 
 def _proj_body(f_ref, q_ref, w_ref, s_ref, o_ref, g_scr):

time: 117 us -> 117 us (level)
  no operation moved by 1% of the time
where the time goes in v16:
time: 117 us
  waiting for transfers between devices  34.6 us (30%)
  starting transfers between devices  26.3 us (22%)
  Pallas kernels  22.1 us (19%)
  blocking collectives  19.4 us (17%)
  other arithmetic  7.51 us (6%)
  local copies, waits for them, and re-layouts  6.83 us (6%)
    all_to_all x1, waiting for transfers between devices, local(): lax.all_to_all(filtered, 'seq', 0, 0, tiled=True)  22.9 us
    all_to_all x1, blocking collectives, local(): gathered = lax.all_to_all(pieces, 'tensor', 0, 0, tiled=True)  19.4 us
    all_to_all x1, starting transfers between devices, local(): lax.all_to_all(gated_kv.reshape(groups, -1, tok_rows), 'seq', 0, 0, tiled...  17.2 us
    all_to_all x1, waiting for transfers between devices, local(): lax.all_to_all(gated_kv.reshape(groups, -1, tok_rows), 'seq', 0, 0, tiled...  11.5 us
    pallas_call x1, Pallas kernels, long_conv(): pl.pallas_call(_conv_body, grid=(2,), in_specs=[full(x), half, half, full...  8.51 us
    unnamed x13, local copies, waits for them, and re-layouts  6.07 us
    pallas_call x1, Pallas kernels, filter_spectrum(): pl.pallas_call(_filter_body, grid=(ch // ch_block,), in_specs=[pl.BlockSp...  5.81 us
    ppermute x1, starting transfers between devices, passed_along(): return lax.ppermute(x, axis, pairs)  4.92 us
  transfers between devices with their start and end apart: 3, of which 3 were waited for; matrix products, arithmetic and copies ran while one was open for 9% of the time, Pallas kernels for 5%

profile of v16, /device:TPU:1, one launch (start us, length us, event | category | flops | bytes accessed | tf_op | source)
XLA Modules:
  0.0 116.8 jit_solution(1721309924599864564)
XLA Ops:
  0.0 0.0 copy-start
  0.0 0.8 slice.3
  0.8 4.9 %collective-permute-start = (bf16[3,6,512]{2,1,0:T(8,128)(2,1)S(1)}, bf16[3,6,512]{2,1,0:T(8,128)(2,1)S(1)}, u32[]{:S(2)}, u32[]{:S(2)}) collective-permute-start(bf16[3,6,512]{2,1,0:T(8,128)(2,1)S(1)} %slice.3), channel_id=1, source_target_pairs={{0,8},{8,16},{16,24},{24,32},{32,40},{40,48},{48,56},{56,64},{64,7... | collective-permute-start | bytes 55304 | tf_op jit(solution)/shard_map/ppermute | solution.py:20
  5.7 0.7 broadcast_bitcast_fusion.1
  6.4 0.3 fusion.30
  6.7 2.0 %copy.12 = f32[1,8,64,256]{3,2,1,0:T(8,128)} copy(f32[1,8,64,256]{3,1,2,0:T(8,128)} %bitcast.17) | data formatting | bytes 1048576
  8.7 0.6 copy.8
  9.3 0.2 collective-permute-done.prior_ref
  9.6 0.0 copy-start.3
  9.6 0.6 copy-done.3
  10.2 4.0 %shard_map.64 = (bf16[512,256]{1,0:T(8,128)(2,1)}, bf16[512,256]{1,0:T(8,128)(2,1)}) custom-call(bf16[3,256,512]{2,1,0:T(8,128)(2,1)} %proj_ref.1, bf16[3,6,512]{2,1,0:T(8,128)(2,1)} %copy-done.3, f32[3,7,512]{2,1,0:T(8,128)} %w_ref.2), custom_call_target="tpu_custom_call" | custom-call | tf_op jit(solution)/shard_map/pallas_call | solution.py:118
  14.2 17.2 %all-to-all-start = ((bf16[64,8,256]{2,1,0:T(8,128)(2,1)}), bf16[64,8,256]{2,1,0:T(8,128)(2,1)S(1)}, u32[]{:S(2)}, u32[]{:S(2)}) async-start(bf16[64,8,256]{2,1,0:T(8,128)(2,1)} %bitcast.18), calls=%async_computation | async-start | bytes 524288 | tf_op jit(solution)/shard_map/all_to_all | solution.py:327
  31.3 0.6 fusion.15.casa_h.refs_4_
  32.0 0.7 subtract_convert_fusion.1.casa_l.refs_5_
  32.6 1.0 fusion.12
  33.7 0.8 fusion.cbsb_h.refs_6_
  34.4 0.7 subtract_convert_fusion.cbsb_l.refs_7_
  35.2 1.2 %fusion.19 = (f32[128,256]{1,0:T(8,128)}, f32[128,256]{1,0:T(8,128)}) fusion(), kind=kLoop, calls=%fused_computation.35 | loop fusion | flops 458752 | bytes 262144 | tf_op jit(solution)/shard_map/sin | solution.py:233
  36.4 5.8 %shard_map.65 = (f32[8,128,256]{2,1,0:T(8,128)}, f32[8,128,256]{2,1,0:T(8,128)}) custom-call(f32[8,64,256]{2,1,0:T(8,128)} %bitcast.15, bf16[256,64]{1,0:T(8,128)(2,1)} %fusion.15.casa_h.refs_4_, bf16[256,64]{1,0:T(8,128)(2,1)} %subtract_convert_fusion.1.casa_l.refs_5_, bf16[256,512]{1,0:T(8,128)(2,1)} %fusion.cbsb_h.refs_6_, ...), custom_call_target="tpu_custom_call" | custom-call | tf_op jit(solution)/shard_map/pallas_call | solution.py:251
  42.2 0.1 sine_negate_fusion
  42.4 0.6 fusion.24.refs_10_
  43.0 0.6 subtract_convert_fusion.2.refs_11_
  43.6 11.5 %all-to-all-done.refs_0_ = bf16[64,8,256]{2,1,0:T(8,128)(2,1)S(1)} async-done(((bf16[64,8,256]{2,1,0:T(8,128)(2,1)}), bf16[64,8,256]{2,1,0:T(8,128)(2,1)S(1)}, u32[]{:S(2)}, u32[]{:S(2)}) %all-to-all-start) | async-done | bytes 262176 | tf_op jit(solution)/shard_map/all_to_all | solution.py:327
  55.1 0.0 copy-start.2
  55.1 0.7 copy-done.2
  55.8 8.5 %shard_map.66 = bf16[64,8,256]{2,1,0:T(8,128)(2,1)} custom-call(bf16[64,8,256]{2,1,0:T(8,128)(2,1)} %copy-done.2, f32[8,128,256]{2,1,0:T(8,128)} %get-tuple-element.10.refs_1_, f32[8,128,256]{2,1,0:T(8,128)} %get-tuple-element.11.refs_2_, f32[1,2048]{1,0:T(1,128)} %bitcast.20, bf16[256,64]{1,0:T(8,128)(2,1)} %fusion.15.casa_h.refs_4_, ...), custom_call_target="tpu_custom_call" | custom-call | tf_op jit(solution)/shard_map/pallas_call | solution.py:268
  64.3 4.2 %all-to-all-start.1 = ((bf16[64,8,256]{2,1,0:T(8,128)(2,1)}), bf16[64,8,256]{2,1,0:T(8,128)(2,1)S(1)}, u32[]{:S(2)}, u32[]{:S(2)}) async-start(bf16[64,8,256]{2,1,0:T(8,128)(2,1)} %shard_map.66), calls=%async_computation.1 | async-start | bytes 524288 | tf_op jit(solution)/shard_map/all_to_all | solution.py:329
  68.5 0.0 copy-done
  68.5 0.1 broadcast_bitcast_fusion
  68.6 0.6 copy.13
  69.2 22.9 %all-to-all-done.1 = bf16[64,8,256]{2,1,0:T(8,128)(2,1)S(1)} async-done(((bf16[64,8,256]{2,1,0:T(8,128)(2,1)}), bf16[64,8,256]{2,1,0:T(8,128)(2,1)S(1)}, u32[]{:S(2)}, u32[]{:S(2)}) %all-to-all-start.1) | async-done | bytes 262176 | tf_op jit(solution)/shard_map/all_to_all | solution.py:329
  92.1 0.0 copy-start.1
  92.1 0.7 copy-done.1
  92.8 3.7 %shard_map.67 = bf16[8,256,256]{2,1,0:T(8,128)(2,1)} custom-call(bf16[512,256]{1,0:T(8,128)(2,1)} %bitcast.16, bf16[512,256]{1,0:T(8,128)(2,1)} %get-tuple-element.12.q_ref, bf16[512,2048]{1,0:T(8,128)(2,1)} %w_ref.3, f32[4,2048]{1,0:T(4,128)} %bitcast.19), custom_call_target="tpu_custom_call" | custom-call | tf_op jit(solution)/shard_map/pallas_call | solution.py:298
  96.5 19.4 %all_to_all.15 = bf16[8,256,256]{2,1,0:T(8,128)(2,1)S(1)} all-to-all(bf16[8,256,256]{2,1,0:T(8,128)(2,1)} %shard_map.67), channel_id=1, replica_groups=mesh['seq'=64,'tensor'=8] {'tensor'}, dimensions={0} | all-to-all | bytes 2097152 | tf_op jit(solution)/shard_map/all_to_all | solution.py:333
  115.9 0.8 reduce_sum.12
Async XLA Ops:
  0.0 68.5 %copy-start = (f32[4,16]{1,0:T(4,128)S(1)}, f32[4,16]{1,0:T(4,128)}, u32[]{:S(2)}) copy-start(f32[4,16]{1,0:T(4,128)} %param.11) | copy-start | bytes 772
  0.8 8.8 %collective-permute-start = (bf16[3,6,512]{2,1,0:T(8,128)(2,1)S(1)}, bf16[3,6,512]{2,1,0:T(8,128)(2,1)S(1)}, u32[]{:S(2)}, u32[]{:S(2)}) collective-permute-start(bf16[3,6,512]{2,1,0:T(8,128)(2,1)S(1)} %slice.3), channel_id=1, source_target_pairs={{0,8},{8,16},{16,24},{24,32},{32,40},{40,48},{48,56},{56,64},{64,7... | collective-permute-start | bytes 55304 | tf_op jit(solution)/shard_map/ppermute | solution.py:20
  9.6 0.6 copy-start.3
  14.2 40.9 %all-to-all-start = ((bf16[64,8,256]{2,1,0:T(8,128)(2,1)}), bf16[64,8,256]{2,1,0:T(8,128)(2,1)S(1)}, u32[]{:S(2)}, u32[]{:S(2)}) async-start(bf16[64,8,256]{2,1,0:T(8,128)(2,1)} %bitcast.18), calls=%async_computation | async-start | bytes 524288 | tf_op jit(solution)/shard_map/all_to_all | solution.py:327
  55.1 0.7 copy-start.2
  64.3 27.8 %all-to-all-start.1 = ((bf16[64,8,256]{2,1,0:T(8,128)(2,1)}), bf16[64,8,256]{2,1,0:T(8,128)(2,1)S(1)}, u32[]{:S(2)}, u32[]{:S(2)}) async-start(bf16[64,8,256]{2,1,0:T(8,128)(2,1)} %shard_map.66), calls=%async_computation.1 | async-start | bytes 524288 | tf_op jit(solution)/shard_map/all_to_all | solution.py:329
  92.1 0.7 copy-start.1

commit v17 on v12

--- a/solution.py
+++ b/solution.py
@@ -112,7 +112,7 @@
     kv = feats[1].astype(jnp.float32) * feats[2].astype(jnp.float32)
     kv_ref[...] = kv.astype(jnp.bfloat16).astype(jnp.float32).T.astype(jnp.bfloat16)
 
-def featurize_kv(projected, prior, weights, lane_block=128, interpret=False):
+def featurize_kv(projected, prior, weights, lane_block=256, interpret=False):
     _, rows, chans = projected.shape
     grid = (chans // lane_block,)
     return pl.pallas_call(

time: 117 us -> 117 us (level)
  no operation moved by 1% of the time
where the time goes in v17:
time: 117 us; the launch traced here: 116 us
  waiting for transfers between devices  34.6 us (30%)
  starting transfers between devices  26.3 us (22%)
  Pallas kernels  21.3 us (18%)
  blocking collectives  19.4 us (17%)
  other arithmetic  7.51 us (6%)
  local copies, waits for them, and re-layouts  6.83 us (6%)
    all_to_all x1, waiting for transfers between devices, local(): lax.all_to_all(filtered, 'seq', 0, 0, tiled=True)  22.9 us
    all_to_all x1, blocking collectives, local(): gathered = lax.all_to_all(pieces, 'tensor', 0, 0, tiled=True)  19.4 us
    all_to_all x1, starting transfers between devices, local(): lax.all_to_all(gated_kv.reshape(groups, -1, tok_rows), 'seq', 0, 0, tiled...  17.2 us
    all_to_all x1, waiting for transfers between devices, local(): lax.all_to_all(gated_kv.reshape(groups, -1, tok_rows), 'seq', 0, 0, tiled...  11.5 us
    pallas_call x1, Pallas kernels, long_conv(): pl.pallas_call(_conv_body, out_shape=jax.ShapeDtypeStruct((blocks, ch, si...  8.32 us
    unnamed x13, local copies, waits for them, and re-layouts  6.07 us
    pallas_call x1, Pallas kernels, filter_spectrum(): pl.pallas_call(_filter_body, grid=(ch // ch_block,), in_specs=[pl.BlockSp...  5.82 us
    ppermute x1, starting transfers between devices, passed_along(): return lax.ppermute(x, axis, pairs)  4.92 us
  transfers between devices with their start and end apart: 3, of which 3 were waited for; matrix products, arithmetic and copies ran while one was open for 9% of the time, Pallas kernels for 5%

profile of v17, /device:TPU:1, one launch (start us, length us, event | category | flops | bytes accessed | tf_op | source)
XLA Modules:
  0.0 116.0 jit_solution(17417896130452165283)
XLA Ops:
  0.0 0.0 copy-start
  0.0 0.8 slice.3
  0.8 4.9 %collective-permute-start = (bf16[3,6,512]{2,1,0:T(8,128)(2,1)S(1)}, bf16[3,6,512]{2,1,0:T(8,128)(2,1)S(1)}, u32[]{:S(2)}, u32[]{:S(2)}) collective-permute-start(bf16[3,6,512]{2,1,0:T(8,128)(2,1)S(1)} %slice.3), channel_id=1, source_target_pairs={{0,8},{8,16},{16,24},{24,32},{32,40},{40,48},{48,56},{56,64},{64,7... | collective-permute-start | bytes 55304 | tf_op jit(solution)/shard_map/ppermute | solution.py:20
  5.7 0.7 broadcast_bitcast_fusion.1
  6.4 0.3 fusion.30
  6.7 2.0 %copy.12 = f32[1,8,64,256]{3,2,1,0:T(8,128)} copy(f32[1,8,64,256]{3,1,2,0:T(8,128)} %bitcast.17) | data formatting | bytes 1048576
  8.7 0.6 copy.8
  9.3 0.2 collective-permute-done.prior_ref
  9.6 0.0 copy-start.3
  9.6 0.6 copy-done.3
  10.2 3.5 %shard_map.64 = (bf16[512,256]{1,0:T(8,128)(2,1)}, bf16[512,256]{1,0:T(8,128)(2,1)}) custom-call(bf16[3,256,512]{2,1,0:T(8,128)(2,1)} %proj_ref.1, bf16[3,6,512]{2,1,0:T(8,128)(2,1)} %copy-done.3, f32[3,7,512]{2,1,0:T(8,128)} %w_ref.2), custom_call_target="tpu_custom_call" | custom-call | tf_op jit(solution)/shard_map/pallas_call | solution.py:118
  13.6 17.2 %all-to-all-start = ((bf16[64,8,256]{2,1,0:T(8,128)(2,1)}), bf16[64,8,256]{2,1,0:T(8,128)(2,1)S(1)}, u32[]{:S(2)}, u32[]{:S(2)}) async-start(bf16[64,8,256]{2,1,0:T(8,128)(2,1)} %bitcast.18), calls=%async_computation | async-start | bytes 524288 | tf_op jit(solution)/shard_map/all_to_all | solution.py:314
  30.8 0.6 fusion.15.casa_h
  31.4 0.7 subtract_convert_fusion.1.casa_l
  32.1 1.0 fusion.12
  33.1 0.8 fusion.cbsb_h
  33.9 0.7 subtract_convert_fusion.cbsb_l
  34.6 1.2 %fusion.19 = (f32[128,256]{1,0:T(8,128)}, f32[128,256]{1,0:T(8,128)}) fusion(), kind=kLoop, calls=%fused_computation.35 | loop fusion | flops 458752 | bytes 262144 | tf_op jit(solution)/shard_map/sin | solution.py:226
  35.8 5.8 %shard_map.65 = (f32[8,128,256]{2,1,0:T(8,128)}, f32[8,128,256]{2,1,0:T(8,128)}) custom-call(f32[8,64,256]{2,1,0:T(8,128)} %bitcast.15, bf16[256,64]{1,0:T(8,128)(2,1)} %fusion.15.casa_h, bf16[256,64]{1,0:T(8,128)(2,1)} %subtract_convert_fusion.1.casa_l, bf16[256,512]{1,0:T(8,128)(2,1)} %fusion.cbsb_h, bf16[256,512]{1,0:T(8,128)(2,1)} %subtract_convert_fusion.cbsb_l, ...), custom_call_target="tpu_custom_call" | custom-call | tf_op jit(solution)/shard_map/pallas_call | solution.py:244
  41.7 0.1 sine_negate_fusion
  41.8 0.6 fusion.24.inv_h
  42.4 0.6 subtract_convert_fusion.2.inv_l
  43.0 11.5 %all-to-all-done.x_ref = bf16[64,8,256]{2,1,0:T(8,128)(2,1)S(1)} async-done(((bf16[64,8,256]{2,1,0:T(8,128)(2,1)}), bf16[64,8,256]{2,1,0:T(8,128)(2,1)S(1)}, u32[]{:S(2)}, u32[]{:S(2)}) %all-to-all-start) | async-done | bytes 262176 | tf_op jit(solution)/shard_map/all_to_all | solution.py:314
  54.5 0.0 copy-start.2
  54.5 0.7 copy-done.2
  55.2 8.3 %shard_map.66 = bf16[64,8,256]{2,1,0:T(8,128)(2,1)} custom-call(bf16[64,8,256]{2,1,0:T(8,128)(2,1)} %copy-done.2, f32[8,128,256]{2,1,0:T(8,128)} %get-tuple-element.10.fh_re_ref, f32[8,128,256]{2,1,0:T(8,128)} %get-tuple-element.11.fh_im_ref, f32[1,2048]{1,0:T(1,128)} %bitcast.20, bf16[256,64]{1,0:T(8,128)(2,1)} %fusion.15.casa_h, ...), custom_call_target="tpu_custom_call" | custom-call | tf_op jit(solution)/shard_map/pallas_call | solution.py:258
  63.5 4.2 %all-to-all-start.1 = ((bf16[64,8,256]{2,1,0:T(8,128)(2,1)}), bf16[64,8,256]{2,1,0:T(8,128)(2,1)S(1)}, u32[]{:S(2)}, u32[]{:S(2)}) async-start(bf16[64,8,256]{2,1,0:T(8,128)(2,1)} %shard_map.66), calls=%async_computation.1 | async-start | bytes 524288 | tf_op jit(solution)/shard_map/all_to_all | solution.py:316
  67.7 0.0 copy-done
  67.7 0.1 broadcast_bitcast_fusion
  67.8 0.6 copy.13
  68.4 22.9 %all-to-all-done.1 = bf16[64,8,256]{2,1,0:T(8,128)(2,1)S(1)} async-done(((bf16[64,8,256]{2,1,0:T(8,128)(2,1)}), bf16[64,8,256]{2,1,0:T(8,128)(2,1)S(1)}, u32[]{:S(2)}, u32[]{:S(2)}) %all-to-all-start.1) | async-done | bytes 262176 | tf_op jit(solution)/shard_map/all_to_all | solution.py:316
  91.3 0.0 copy-start.1
  91.3 0.7 copy-done.1
  92.0 3.7 %shard_map.67 = bf16[8,256,256]{2,1,0:T(8,128)(2,1)} custom-call(bf16[512,256]{1,0:T(8,128)(2,1)} %bitcast.16, bf16[512,256]{1,0:T(8,128)(2,1)} %get-tuple-element.12.q_ref, bf16[512,2048]{1,0:T(8,128)(2,1)} %w_ref.3, f32[4,2048]{1,0:T(4,128)} %bitcast.19), custom_call_target="tpu_custom_call" | custom-call | tf_op jit(solution)/shard_map/pallas_call | solution.py:285
  95.8 19.4 %all_to_all.15 = bf16[8,256,256]{2,1,0:T(8,128)(2,1)S(1)} all-to-all(bf16[8,256,256]{2,1,0:T(8,128)(2,1)} %shard_map.67), channel_id=1, replica_groups=mesh['seq'=64,'tensor'=8] {'tensor'}, dimensions={0} | all-to-all | bytes 2097152 | tf_op jit(solution)/shard_map/all_to_all | solution.py:320
  115.2 0.8 reduce_sum.12
Async XLA Ops:
  0.0 67.7 %copy-start = (f32[4,16]{1,0:T(4,128)S(1)}, f32[4,16]{1,0:T(4,128)}, u32[]{:S(2)}) copy-start(f32[4,16]{1,0:T(4,128)} %param.11) | copy-start | bytes 772
  0.8 8.8 %collective-permute-start = (bf16[3,6,512]{2,1,0:T(8,128)(2,1)S(1)}, bf16[3,6,512]{2,1,0:T(8,128)(2,1)S(1)}, u32[]{:S(2)}, u32[]{:S(2)}) collective-permute-start(bf16[3,6,512]{2,1,0:T(8,128)(2,1)S(1)} %slice.3), channel_id=1, source_target_pairs={{0,8},{8,16},{16,24},{24,32},{32,40},{40,48},{48,56},{56,64},{64,7... | collective-permute-start | bytes 55304 | tf_op jit(solution)/shard_map/ppermute | solution.py:20
  9.6 0.6 copy-start.3
  13.6 40.9 %all-to-all-start = ((bf16[64,8,256]{2,1,0:T(8,128)(2,1)}), bf16[64,8,256]{2,1,0:T(8,128)(2,1)S(1)}, u32[]{:S(2)}, u32[]{:S(2)}) async-start(bf16[64,8,256]{2,1,0:T(8,128)(2,1)} %bitcast.18), calls=%async_computation | async-start | bytes 524288 | tf_op jit(solution)/shard_map/all_to_all | solution.py:314
  54.5 0.7 copy-start.2
  63.5 27.8 %all-to-all-start.1 = ((bf16[64,8,256]{2,1,0:T(8,128)(2,1)}), bf16[64,8,256]{2,1,0:T(8,128)(2,1)S(1)}, u32[]{:S(2)}, u32[]{:S(2)}) async-start(bf16[64,8,256]{2,1,0:T(8,128)(2,1)} %shard_map.66), calls=%async_computation.1 | async-start | bytes 524288 | tf_op jit(solution)/shard_map/all_to_all | solution.py:316
  91.3 0.7 copy-start.1

commit v18 on v17

--- a/solution.py
+++ b/solution.py
@@ -112,7 +112,7 @@
     kv = feats[1].astype(jnp.float32) * feats[2].astype(jnp.float32)
     kv_ref[...] = kv.astype(jnp.bfloat16).astype(jnp.float32).T.astype(jnp.bfloat16)
 
-def featurize_kv(projected, prior, weights, lane_block=256, interpret=False):
+def featurize_kv(projected, prior, weights, lane_block=512, interpret=False):
     _, rows, chans = projected.shape
     grid = (chans // lane_block,)
     return pl.pallas_call(

time: 117 us -> 117 us (level)
  no operation moved by 1% of the time
where the time goes in v18:
time: 117 us; the launch traced here: 116 us
  waiting for transfers between devices  34.6 us (30%)
  starting transfers between devices  26.3 us (22%)
  Pallas kernels  21.5 us (18%)
  blocking collectives  19.4 us (17%)
  other arithmetic  7.51 us (6%)
  local copies, waits for them, and re-layouts  6.83 us (6%)
    all_to_all x1, waiting for transfers between devices, local(): lax.all_to_all(filtered, 'seq', 0, 0, tiled=True)  22.9 us
    all_to_all x1, blocking collectives, local(): gathered = lax.all_to_all(pieces, 'tensor', 0, 0, tiled=True)  19.4 us
    all_to_all x1, starting transfers between devices, local(): lax.all_to_all(gated_kv.reshape(groups, -1, tok_rows), 'seq', 0, 0, tiled...  17.2 us
    all_to_all x1, waiting for transfers between devices, local(): lax.all_to_all(gated_kv.reshape(groups, -1, tok_rows), 'seq', 0, 0, tiled...  11.5 us
    pallas_call x1, Pallas kernels, long_conv(): pl.pallas_call(_conv_body, out_shape=jax.ShapeDtypeStruct((blocks, ch, si...  8.31 us
    unnamed x13, local copies, waits for them, and re-layouts  6.07 us
    pallas_call x1, Pallas kernels, filter_spectrum(): pl.pallas_call(_filter_body, grid=(ch // ch_block,), in_specs=[pl.BlockSp...  5.82 us
    ppermute x1, starting transfers between devices, passed_along(): return lax.ppermute(x, axis, pairs)  4.92 us
  transfers between devices with their start and end apart: 3, of which 3 were waited for; matrix products, arithmetic and copies ran while one was open for 9% of the time, Pallas kernels for 5%

profile of v18, /device:TPU:1, one launch (start us, length us, event | category | flops | bytes accessed | tf_op | source)
XLA Modules:
  0.0 116.1 jit_solution(3115109581889555231)
XLA Ops:
  0.0 0.0 copy-start
  0.0 0.8 slice.3
  0.8 4.9 %collective-permute-start = (bf16[3,6,512]{2,1,0:T(8,128)(2,1)S(1)}, bf16[3,6,512]{2,1,0:T(8,128)(2,1)S(1)}, u32[]{:S(2)}, u32[]{:S(2)}) collective-permute-start(bf16[3,6,512]{2,1,0:T(8,128)(2,1)S(1)} %slice.3), channel_id=1, source_target_pairs={{0,8},{8,16},{16,24},{24,32},{32,40},{40,48},{48,56},{56,64},{64,7... | collective-permute-start | bytes 55304 | tf_op jit(solution)/shard_map/ppermute | solution.py:20
  5.7 0.7 broadcast_bitcast_fusion.1
  6.4 0.3 fusion.30
  6.7 2.0 %copy.12 = f32[1,8,64,256]{3,2,1,0:T(8,128)} copy(f32[1,8,64,256]{3,1,2,0:T(8,128)} %bitcast.17) | data formatting | bytes 1048576
  8.7 0.6 copy.8
  9.3 0.2 collective-permute-done.prior_ref
  9.6 0.0 copy-start.3
  9.6 0.6 copy-done.3
  10.2 3.6 %shard_map.64 = (bf16[512,256]{1,0:T(8,128)(2,1)}, bf16[512,256]{1,0:T(8,128)(2,1)}) custom-call(bf16[3,256,512]{2,1,0:T(8,128)(2,1)} %proj_ref.1, bf16[3,6,512]{2,1,0:T(8,128)(2,1)} %copy-done.3, f32[3,7,512]{2,1,0:T(8,128)} %w_ref.2), custom_call_target="tpu_custom_call" | custom-call | tf_op jit(solution)/shard_map/pallas_call | solution.py:118
  13.8 17.2 %all-to-all-start = ((bf16[64,8,256]{2,1,0:T(8,128)(2,1)}), bf16[64,8,256]{2,1,0:T(8,128)(2,1)S(1)}, u32[]{:S(2)}, u32[]{:S(2)}) async-start(bf16[64,8,256]{2,1,0:T(8,128)(2,1)} %bitcast.18), calls=%async_computation | async-start | bytes 524288 | tf_op jit(solution)/shard_map/all_to_all | solution.py:314
  30.9 0.6 fusion.15.casa_h
  31.6 0.7 subtract_convert_fusion.1.casa_l
  32.2 1.0 fusion.12
  33.2 0.8 fusion.cbsb_h
  34.0 0.7 subtract_convert_fusion.cbsb_l
  34.7 1.2 %fusion.19 = (f32[128,256]{1,0:T(8,128)}, f32[128,256]{1,0:T(8,128)}) fusion(), kind=kLoop, calls=%fused_computation.35 | loop fusion | flops 458752 | bytes 262144 | tf_op jit(solution)/shard_map/sin | solution.py:226
  36.0 5.8 %shard_map.65 = (f32[8,128,256]{2,1,0:T(8,128)}, f32[8,128,256]{2,1,0:T(8,128)}) custom-call(f32[8,64,256]{2,1,0:T(8,128)} %bitcast.15, bf16[256,64]{1,0:T(8,128)(2,1)} %fusion.15.casa_h, bf16[256,64]{1,0:T(8,128)(2,1)} %subtract_convert_fusion.1.casa_l, bf16[256,512]{1,0:T(8,128)(2,1)} %fusion.cbsb_h, bf16[256,512]{1,0:T(8,128)(2,1)} %subtract_convert_fusion.cbsb_l, ...), custom_call_target="tpu_custom_call" | custom-call | tf_op jit(solution)/shard_map/pallas_call | solution.py:244
  41.8 0.1 sine_negate_fusion
  41.9 0.6 fusion.24.inv_h
  42.5 0.6 subtract_convert_fusion.2.inv_l
  43.2 11.5 %all-to-all-done.x_ref = bf16[64,8,256]{2,1,0:T(8,128)(2,1)S(1)} async-done(((bf16[64,8,256]{2,1,0:T(8,128)(2,1)}), bf16[64,8,256]{2,1,0:T(8,128)(2,1)S(1)}, u32[]{:S(2)}, u32[]{:S(2)}) %all-to-all-start) | async-done | bytes 262176 | tf_op jit(solution)/shard_map/all_to_all | solution.py:314
  54.7 0.0 copy-start.2
  54.7 0.7 copy-done.2
  55.3 8.3 %shard_map.66 = bf16[64,8,256]{2,1,0:T(8,128)(2,1)} custom-call(bf16[64,8,256]{2,1,0:T(8,128)(2,1)} %copy-done.2, f32[8,128,256]{2,1,0:T(8,128)} %get-tuple-element.10.fh_re_ref, f32[8,128,256]{2,1,0:T(8,128)} %get-tuple-element.11.fh_im_ref, f32[1,2048]{1,0:T(1,128)} %bitcast.20, bf16[256,64]{1,0:T(8,128)(2,1)} %fusion.15.casa_h, ...), custom_call_target="tpu_custom_call" | custom-call | tf_op jit(solution)/shard_map/pallas_call | solution.py:258
  63.7 4.2 %all-to-all-start.1 = ((bf16[64,8,256]{2,1,0:T(8,128)(2,1)}), bf16[64,8,256]{2,1,0:T(8,128)(2,1)S(1)}, u32[]{:S(2)}, u32[]{:S(2)}) async-start(bf16[64,8,256]{2,1,0:T(8,128)(2,1)} %shard_map.66), calls=%async_computation.1 | async-start | bytes 524288 | tf_op jit(solution)/shard_map/all_to_all | solution.py:316
  67.9 0.0 copy-done
  67.9 0.1 broadcast_bitcast_fusion
  67.9 0.6 copy.13
  68.6 22.9 %all-to-all-done.1 = bf16[64,8,256]{2,1,0:T(8,128)(2,1)S(1)} async-done(((bf16[64,8,256]{2,1,0:T(8,128)(2,1)}), bf16[64,8,256]{2,1,0:T(8,128)(2,1)S(1)}, u32[]{:S(2)}, u32[]{:S(2)}) %all-to-all-start.1) | async-done | bytes 262176 | tf_op jit(solution)/shard_map/all_to_all | solution.py:316
  91.4 0.0 copy-start.1
  91.4 0.7 copy-done.1
  92.2 3.7 %shard_map.67 = bf16[8,256,256]{2,1,0:T(8,128)(2,1)} custom-call(bf16[512,256]{1,0:T(8,128)(2,1)} %bitcast.16, bf16[512,256]{1,0:T(8,128)(2,1)} %get-tuple-element.12.q_ref, bf16[512,2048]{1,0:T(8,128)(2,1)} %w_ref.3, f32[4,2048]{1,0:T(4,128)} %bitcast.19), custom_call_target="tpu_custom_call" | custom-call | tf_op jit(solution)/shard_map/pallas_call | solution.py:285
  95.9 19.4 %all_to_all.15 = bf16[8,256,256]{2,1,0:T(8,128)(2,1)S(1)} all-to-all(bf16[8,256,256]{2,1,0:T(8,128)(2,1)} %shard_map.67), channel_id=1, replica_groups=mesh['seq'=64,'tensor'=8] {'tensor'}, dimensions={0} | all-to-all | bytes 2097152 | tf_op jit(solution)/shard_map/all_to_all | solution.py:320
  115.3 0.8 reduce_sum.12
Async XLA Ops:
  0.0 67.9 %copy-start = (f32[4,16]{1,0:T(4,128)S(1)}, f32[4,16]{1,0:T(4,128)}, u32[]{:S(2)}) copy-start(f32[4,16]{1,0:T(4,128)} %param.11) | copy-start | bytes 772
  0.8 8.8 %collective-permute-start = (bf16[3,6,512]{2,1,0:T(8,128)(2,1)S(1)}, bf16[3,6,512]{2,1,0:T(8,128)(2,1)S(1)}, u32[]{:S(2)}, u32[]{:S(2)}) collective-permute-start(bf16[3,6,512]{2,1,0:T(8,128)(2,1)S(1)} %slice.3), channel_id=1, source_target_pairs={{0,8},{8,16},{16,24},{24,32},{32,40},{40,48},{48,56},{56,64},{64,7... | collective-permute-start | bytes 55304 | tf_op jit(solution)/shard_map/ppermute | solution.py:20
  9.6 0.6 copy-start.3
  13.8 40.9 %all-to-all-start = ((bf16[64,8,256]{2,1,0:T(8,128)(2,1)}), bf16[64,8,256]{2,1,0:T(8,128)(2,1)S(1)}, u32[]{:S(2)}, u32[]{:S(2)}) async-start(bf16[64,8,256]{2,1,0:T(8,128)(2,1)} %bitcast.18), calls=%async_computation | async-start | bytes 524288 | tf_op jit(solution)/shard_map/all_to_all | solution.py:314
  54.7 0.7 copy-start.2
  63.7 27.8 %all-to-all-start.1 = ((bf16[64,8,256]{2,1,0:T(8,128)(2,1)}), bf16[64,8,256]{2,1,0:T(8,128)(2,1)S(1)}, u32[]{:S(2)}, u32[]{:S(2)}) async-start(bf16[64,8,256]{2,1,0:T(8,128)(2,1)} %shard_map.66), calls=%async_computation.1 | async-start | bytes 524288 | tf_op jit(solution)/shard_map/all_to_all | solution.py:316
  91.4 0.7 copy-start.1

commit v19 on v17

--- a/solution.py
+++ b/solution.py
@@ -278,7 +278,7 @@
         o_ref[p] = acc.astype(jnp.bfloat16)
 
 
-def project(filtered_home, q_cols, out_values, scale_cols, n_pieces, steps=2):
+def project(filtered_home, q_cols, out_values, scale_cols, n_pieces, steps=1):
     chans, rows = filtered_home.shape
     width = out_values.shape[1] // n_pieces
     per_step = n_pieces // steps

time: 117 us -> 117 us (level)
  no operation moved by 1% of the time
where the time goes in v19:
time: 117 us; the launch traced here: 116 us
  waiting for transfers between devices  34.6 us (30%)
  starting transfers between devices  26.3 us (22%)
  Pallas kernels  21.7 us (19%)
  blocking collectives  19.4 us (17%)
  other arithmetic  7.51 us (6%)
  local copies, waits for them, and re-layouts  6.83 us (6%)
    all_to_all x1, waiting for transfers between devices, local(): lax.all_to_all(filtered, 'seq', 0, 0, tiled=True)  22.9 us
    all_to_all x1, blocking collectives, local(): gathered = lax.all_to_all(pieces, 'tensor', 0, 0, tiled=True)  19.4 us
    all_to_all x1, starting transfers between devices, local(): lax.all_to_all(gated_kv.reshape(groups, -1, tok_rows), 'seq', 0, 0, tiled...  17.2 us
    all_to_all x1, waiting for transfers between devices, local(): lax.all_to_all(gated_kv.reshape(groups, -1, tok_rows), 'seq', 0, 0, tiled...  11.5 us
    pallas_call x1, Pallas kernels, long_conv(): pl.pallas_call(_conv_body, out_shape=jax.ShapeDtypeStruct((blocks, ch, si...  8.32 us
    unnamed x13, local copies, waits for them, and re-layouts  6.07 us
    pallas_call x1, Pallas kernels, filter_spectrum(): pl.pallas_call(_filter_body, grid=(ch // ch_block,), in_specs=[pl.BlockSp...  5.82 us
    ppermute x1, starting transfers between devices, passed_along(): return lax.ppermute(x, axis, pairs)  4.92 us
  transfers between devices with their start and end apart: 3, of which 3 were waited for; matrix products, arithmetic and copies ran while one was open for 9% of the time, Pallas kernels for 5%

profile of v19, /device:TPU:1, one launch (start us, length us, event | category | flops | bytes accessed | tf_op | source)
XLA Modules:
  0.0 116.4 jit_solution(15997886895238082622)
XLA Ops:
  0.0 0.0 copy-start
  0.0 0.8 slice.3
  0.8 4.9 %collective-permute-start = (bf16[3,6,512]{2,1,0:T(8,128)(2,1)S(1)}, bf16[3,6,512]{2,1,0:T(8,128)(2,1)S(1)}, u32[]{:S(2)}, u32[]{:S(2)}) collective-permute-start(bf16[3,6,512]{2,1,0:T(8,128)(2,1)S(1)} %slice.3), channel_id=1, source_target_pairs={{0,8},{8,16},{16,24},{24,32},{32,40},{40,48},{48,56},{56,64},{64,7... | collective-permute-start | bytes 55304 | tf_op jit(solution)/shard_map/ppermute | solution.py:20
  5.7 0.7 broadcast_bitcast_fusion.1
  6.4 0.3 fusion.30
  6.7 2.0 %copy.12 = f32[1,8,64,256]{3,2,1,0:T(8,128)} copy(f32[1,8,64,256]{3,1,2,0:T(8,128)} %bitcast.17) | data formatting | bytes 1048576
  8.7 0.6 copy.8
  9.3 0.2 collective-permute-done.prior_ref
  9.6 0.0 copy-start.3
  9.6 0.6 copy-done.3
  10.2 3.5 %shard_map.64 = (bf16[512,256]{1,0:T(8,128)(2,1)}, bf16[512,256]{1,0:T(8,128)(2,1)}) custom-call(bf16[3,256,512]{2,1,0:T(8,128)(2,1)} %proj_ref.1, bf16[3,6,512]{2,1,0:T(8,128)(2,1)} %copy-done.3, f32[3,7,512]{2,1,0:T(8,128)} %w_ref.2), custom_call_target="tpu_custom_call" | custom-call | tf_op jit(solution)/shard_map/pallas_call | solution.py:118
  13.6 17.2 %all-to-all-start = ((bf16[64,8,256]{2,1,0:T(8,128)(2,1)}), bf16[64,8,256]{2,1,0:T(8,128)(2,1)S(1)}, u32[]{:S(2)}, u32[]{:S(2)}) async-start(bf16[64,8,256]{2,1,0:T(8,128)(2,1)} %bitcast.18), calls=%async_computation | async-start | bytes 524288 | tf_op jit(solution)/shard_map/all_to_all | solution.py:314
  30.8 0.6 fusion.15.casa_h
  31.4 0.7 subtract_convert_fusion.1.casa_l
  32.1 1.0 fusion.12
  33.1 0.8 fusion.cbsb_h
  33.9 0.7 subtract_convert_fusion.cbsb_l
  34.6 1.2 %fusion.19 = (f32[128,256]{1,0:T(8,128)}, f32[128,256]{1,0:T(8,128)}) fusion(), kind=kLoop, calls=%fused_computation.35 | loop fusion | flops 458752 | bytes 262144 | tf_op jit(solution)/shard_map/sin | solution.py:226
  35.8 5.8 %shard_map.65 = (f32[8,128,256]{2,1,0:T(8,128)}, f32[8,128,256]{2,1,0:T(8,128)}) custom-call(f32[8,64,256]{2,1,0:T(8,128)} %bitcast.15, bf16[256,64]{1,0:T(8,128)(2,1)} %fusion.15.casa_h, bf16[256,64]{1,0:T(8,128)(2,1)} %subtract_convert_fusion.1.casa_l, bf16[256,512]{1,0:T(8,128)(2,1)} %fusion.cbsb_h, bf16[256,512]{1,0:T(8,128)(2,1)} %subtract_convert_fusion.cbsb_l, ...), custom_call_target="tpu_custom_call" | custom-call | tf_op jit(solution)/shard_map/pallas_call | solution.py:244
  41.7 0.1 sine_negate_fusion
  41.8 0.6 fusion.24.inv_h
  42.4 0.6 subtract_convert_fusion.2.inv_l
  43.0 11.5 %all-to-all-done.x_ref = bf16[64,8,256]{2,1,0:T(8,128)(2,1)S(1)} async-done(((bf16[64,8,256]{2,1,0:T(8,128)(2,1)}), bf16[64,8,256]{2,1,0:T(8,128)(2,1)S(1)}, u32[]{:S(2)}, u32[]{:S(2)}) %all-to-all-start) | async-done | bytes 262176 | tf_op jit(solution)/shard_map/all_to_all | solution.py:314
  54.5 0.0 copy-start.2
  54.5 0.7 copy-done.2
  55.2 8.3 %shard_map.66 = bf16[64,8,256]{2,1,0:T(8,128)(2,1)} custom-call(bf16[64,8,256]{2,1,0:T(8,128)(2,1)} %copy-done.2, f32[8,128,256]{2,1,0:T(8,128)} %get-tuple-element.10.fh_re_ref, f32[8,128,256]{2,1,0:T(8,128)} %get-tuple-element.11.fh_im_ref, f32[1,2048]{1,0:T(1,128)} %bitcast.20, bf16[256,64]{1,0:T(8,128)(2,1)} %fusion.15.casa_h, ...), custom_call_target="tpu_custom_call" | custom-call | tf_op jit(solution)/shard_map/pallas_call | solution.py:258
  63.5 4.2 %all-to-all-start.1 = ((bf16[64,8,256]{2,1,0:T(8,128)(2,1)}), bf16[64,8,256]{2,1,0:T(8,128)(2,1)S(1)}, u32[]{:S(2)}, u32[]{:S(2)}) async-start(bf16[64,8,256]{2,1,0:T(8,128)(2,1)} %shard_map.66), calls=%async_computation.1 | async-start | bytes 524288 | tf_op jit(solution)/shard_map/all_to_all | solution.py:316
  67.7 0.0 copy-done
  67.7 0.1 broadcast_bitcast_fusion
  67.8 0.6 copy.13
  68.4 22.9 %all-to-all-done.1 = bf16[64,8,256]{2,1,0:T(8,128)(2,1)S(1)} async-done(((bf16[64,8,256]{2,1,0:T(8,128)(2,1)}), bf16[64,8,256]{2,1,0:T(8,128)(2,1)S(1)}, u32[]{:S(2)}, u32[]{:S(2)}) %all-to-all-start.1) | async-done | bytes 262176 | tf_op jit(solution)/shard_map/all_to_all | solution.py:316
  91.3 0.0 copy-start.1
  91.3 0.7 copy-done.1
  92.0 4.1 %shard_map.67 = bf16[8,256,256]{2,1,0:T(8,128)(2,1)} custom-call(bf16[512,256]{1,0:T(8,128)(2,1)} %bitcast.16, bf16[512,256]{1,0:T(8,128)(2,1)} %get-tuple-element.12.q_ref, bf16[512,2048]{1,0:T(8,128)(2,1)} %w_ref.3, f32[4,2048]{1,0:T(4,128)} %bitcast.19), custom_call_target="tpu_custom_call" | custom-call | tf_op jit(solution)/shard_map/pallas_call | solution.py:285
  96.1 19.4 %all_to_all.15 = bf16[8,256,256]{2,1,0:T(8,128)(2,1)S(1)} all-to-all(bf16[8,256,256]{2,1,0:T(8,128)(2,1)} %shard_map.67), channel_id=1, replica_groups=mesh['seq'=64,'tensor'=8] {'tensor'}, dimensions={0} | all-to-all | bytes 2097152 | tf_op jit(solution)/shard_map/all_to_all | solution.py:320
  115.5 0.8 reduce_sum.12
Async XLA Ops:
  0.0 67.7 %copy-start = (f32[4,16]{1,0:T(4,128)S(1)}, f32[4,16]{1,0:T(4,128)}, u32[]{:S(2)}) copy-start(f32[4,16]{1,0:T(4,128)} %param.11) | copy-start | bytes 772
  0.8 8.8 %collective-permute-start = (bf16[3,6,512]{2,1,0:T(8,128)(2,1)S(1)}, bf16[3,6,512]{2,1,0:T(8,128)(2,1)S(1)}, u32[]{:S(2)}, u32[]{:S(2)}) collective-permute-start(bf16[3,6,512]{2,1,0:T(8,128)(2,1)S(1)} %slice.3), channel_id=1, source_target_pairs={{0,8},{8,16},{16,24},{24,32},{32,40},{40,48},{48,56},{56,64},{64,7... | collective-permute-start | bytes 55304 | tf_op jit(solution)/shard_map/ppermute | solution.py:20
  9.6 0.6 copy-start.3
  13.6 40.9 %all-to-all-start = ((bf16[64,8,256]{2,1,0:T(8,128)(2,1)}), bf16[64,8,256]{2,1,0:T(8,128)(2,1)S(1)}, u32[]{:S(2)}, u32[]{:S(2)}) async-start(bf16[64,8,256]{2,1,0:T(8,128)(2,1)} %bitcast.18), calls=%async_computation | async-start | bytes 524288 | tf_op jit(solution)/shard_map/all_to_all | solution.py:314
  54.5 0.7 copy-start.2
  63.5 27.8 %all-to-all-start.1 = ((bf16[64,8,256]{2,1,0:T(8,128)(2,1)}), bf16[64,8,256]{2,1,0:T(8,128)(2,1)S(1)}, u32[]{:S(2)}, u32[]{:S(2)}) async-start(bf16[64,8,256]{2,1,0:T(8,128)(2,1)} %shard_map.66), calls=%async_computation.1 | async-start | bytes 524288 | tf_op jit(solution)/shard_map/all_to_all | solution.py:316
  91.3 0.7 copy-start.1
